TPU v7x, 128 devices: a whole 4x4x4 slice. The times are simulated.
128 devices in a mesh: ctx: 32 (over y, x, core), head: 4 (over z).
Axes of the slice: x: 4, y: 4, z: 4, core: 2. Of those that a mesh axis runs over, the one named last changes fastest.
Arguments:
- queries: bfloat16 [4096, 4096], P('ctx', 'head'), may hold values from -6 to 6
- key_input: bfloat16 [2, 4096, 4096], P(None, 'ctx', 'head'), may hold values from -6 to 6
- value_input: bfloat16 [2, 4096, 4096], P(None, 'ctx', 'head'), may hold values from -6 to 6
- beta_rates: float32 [32, 2, 4096], P('head', None, 'ctx'), may hold values from 0 to 1.9, as said below
- out_grad: bfloat16 [4096, 4096], P(('ctx', 'head')), may hold values from -0.75 to 0.75
- out_weight: bfloat16 [4096, 4096], P('head'), may hold values from -0.09375 to 0.09375
Outputs:
- grad_queries: bfloat16 [4096, 4096], P('ctx', 'head')
- grad_keys: bfloat16 [2, 4096, 4096], P(None, 'ctx', 'head')
- grad_values: bfloat16 [2, 4096, 4096], P(None, 'ctx', 'head')
- grad_rates: float32 [32, 2, 4096], P('head', None, 'ctx')
Inputs may be any that keep to these rules, and one draw needn't show every extreme that they name: `beta_rates`: positive strengths.
All inputs are finite; a program needn't handle non-finite values.
Results may differ from a plain program's by a relative error of at most 0.011.
Values may be sent and summed in bfloat16 or wider, within the bound.
No kernel may reach another device: no remote copies, remote signals or barrier semaphores. Data moves between devices by JAX's collectives and lax.ppermute only.
A program may use at most 192 MiB of HBM per device.

v0:
```python
import jax
import jax.numpy as jnp
from jax import lax
from jax.sharding import PartitionSpec as P

HEAD_DIM = 128
BLOCK = 64


highest = lax.Precision.HIGHEST


def shifted(value, axis, by):
    count = lax.axis_size(axis)
    pairs = [(i, i + by) for i in range(count) if 0 <= i + by < count]
    return lax.ppermute(value, axis, pairs)


def block_solve(key_rows, value_rows, rate_rows):
    length = key_rows.shape[1]
    gram = jnp.einsum("bik,bjk->bij", key_rows, key_rows, precision=highest)
    strict = jnp.tril(jnp.ones((length, length), key_rows.dtype), -1)
    system = jnp.eye(length, dtype=key_rows.dtype) + gram * rate_rows[:, None, :] * strict
    joined = jnp.concatenate([key_rows, value_rows], axis=2)
    solved = jax.scipy.linalg.solve_triangular(system, joined, lower=True, unit_diagonal=True)
    return (solved[..., : key_rows.shape[2]], solved[..., key_rows.shape[2] :])


def read_mask(query_rows, length, dtype):
    house_count = length // query_rows
    upper = house_count * (jnp.arange(query_rows) + 1)
    return (jnp.arange(length)[None, :] < upper[:, None]).astype(dtype)


def solved_step(state_in, pieces):
    query_rows, key_rows, rate_rows, solved_k, solved_v = pieces
    errors = jnp.einsum("bik,bkv->biv", solved_k, state_in, precision=highest) - solved_v
    weighted = errors * rate_rows[:, :, None]
    scores = jnp.einsum("btk,bik->bti", query_rows, key_rows, precision=highest)
    scores = scores * read_mask(query_rows.shape[1], key_rows.shape[1], scores.dtype)[None]
    outputs = jnp.einsum("btk,bkv->btv", query_rows, state_in, precision=highest)
    outputs = outputs - jnp.einsum("bti,biv->btv", scores, weighted, precision=highest)
    state_out = state_in - jnp.einsum("bik,biv->bkv", key_rows, weighted, precision=highest)
    return (state_out, outputs)


def arrange(query_all, raw_keys, value_all, rate_all, block_len):
    tokens, head_count, head_width = query_all.shape
    house_count = raw_keys.shape[0]
    scaling = lax.rsqrt(jnp.sum(raw_keys * raw_keys, axis=-1, keepdims=True) + 1e-06)
    normed = raw_keys * scaling
    blocks = tokens // block_len
    query_blocks = query_all.reshape(blocks, block_len, head_count, head_width).transpose(
        0, 2, 1, 3
    )

    def reorder(tensor):
        last_width = tensor.shape[-1]
        shaped = tensor.reshape(house_count, blocks, block_len, head_count, last_width)
        return shaped.transpose(1, 3, 2, 0, 4).reshape(
            blocks, head_count, block_len * house_count, last_width
        )

    rate_blocks = rate_all.reshape(head_count, house_count, blocks, block_len)
    rate_blocks = rate_blocks.transpose(2, 0, 3, 1).reshape(
        blocks, head_count, block_len * house_count
    )
    return (query_blocks, reorder(normed), reorder(value_all), rate_blocks)


def matmul_heads(left, right):
    return jnp.einsum("hij,hjk->hik", left, right, precision=highest)


def compose(earlier, later):
    return (matmul_heads(later[0], earlier[0]), matmul_heads(later[0], earlier[1]) + later[1])


def shards(queries, key_input, value_input, beta_rates, out_grad, out_weight):
    d_attn = lax.dot_general(
        lax.all_gather(out_grad, "head", axis=0, tiled=True),
        out_weight,
        (((1,), (1,)), ((), ())),
        preferred_element_type=jnp.float32,
    ).astype(jnp.bfloat16)
    tokens = queries.shape[0]
    head_count = queries.shape[1] // HEAD_DIM
    house_count = key_input.shape[0]
    query_all = queries.astype(jnp.float32).reshape(tokens, head_count, HEAD_DIM)
    raw_keys = key_input.astype(jnp.float32).reshape(house_count, tokens, head_count, HEAD_DIM)
    value_all = value_input.astype(jnp.float32).reshape(house_count, tokens, head_count, HEAD_DIM)
    grad_out = d_attn.astype(jnp.float32).reshape(tokens, head_count, HEAD_DIM)
    blocks = tokens // BLOCK
    rows_block = BLOCK * house_count

    def arrange_scaled(query_arg, key_arg, value_arg, rate_arg):
        return arrange(query_arg * HEAD_DIM ** (-0.5), key_arg, value_arg, rate_arg, BLOCK)

    arranged, arrange_pull = jax.vjp(arrange_scaled, query_all, raw_keys, value_all, beta_rates)
    query_blocks, key_blocks, value_blocks, rate_blocks = arranged
    flat_shape = (blocks * head_count, rows_block, HEAD_DIM)
    block_shape = (blocks, head_count, rows_block, HEAD_DIM)
    solved_flat, solve_pull = jax.vjp(
        block_solve,
        key_blocks.reshape(flat_shape),
        value_blocks.reshape(flat_shape),
        rate_blocks.reshape(blocks * head_count, rows_block),
    )
    solved_k = solved_flat[0].reshape(block_shape)
    solved_v = solved_flat[1].reshape(block_shape)
    grad_blocks = grad_out.reshape(blocks, BLOCK, head_count, HEAD_DIM).transpose(0, 2, 1, 3)
    identity_b = jnp.broadcast_to(
        jnp.eye(HEAD_DIM, dtype=jnp.float32), (head_count, HEAD_DIM, HEAD_DIM)
    )
    zero_b = jnp.zeros((head_count, HEAD_DIM, HEAD_DIM), jnp.float32)

    def block_maps(pieces):
        query_rows, key_rows, rate_rows, solved_kr, solved_vr, grad_rows = pieces
        scaled_keys = key_rows * rate_rows[:, :, None]
        transfer = identity_b - jnp.einsum(
            "bik,bil->bkl", scaled_keys, solved_kr, precision=highest
        )
        offset = jnp.einsum("bik,biv->bkv", scaled_keys, solved_vr, precision=highest)
        scores = jnp.einsum("btk,bik->bti", query_rows, key_rows, precision=highest)
        scores = (
            scores
            * read_mask(query_rows.shape[1], key_rows.shape[1], scores.dtype)[None]
            * rate_rows[:, None, :]
        )
        reading = query_rows - jnp.einsum("bti,bik->btk", scores, solved_kr, precision=highest)
        local_grad = jnp.einsum("btk,btv->bkv", reading, grad_rows, precision=highest)
        return (transfer, offset, local_grad)

    transfers, offsets, local_grads = lax.map(
        block_maps, (query_blocks, key_blocks, rate_blocks, solved_k, solved_v, grad_blocks)
    )

    def forward_fold(carried, pieces):
        return (compose(carried, pieces), None)

    (device_p, device_r), unused = lax.scan(
        forward_fold, (identity_b, zero_b), (transfers, offsets)
    )

    def adjoint_fold(carried, pieces):
        transfer, local_grad = pieces
        return (matmul_heads(jnp.swapaxes(transfer, 1, 2), carried) + local_grad, None)

    device_g, unused_two = lax.scan(adjoint_fold, zero_b, (transfers, local_grads), reverse=True)

    def forward_turn(counter, carried):
        return shifted(matmul_heads(device_p, carried) + device_r, "ctx", 1)

    start_state = lax.fori_loop(0, lax.axis_size("ctx") - 1, forward_turn, zero_b)
    transposed_p = jnp.swapaxes(device_p, 1, 2)

    def backward_turn(counter, carried):
        return shifted(matmul_heads(transposed_p, carried) + device_g, "ctx", -1)

    end_grad = lax.fori_loop(0, lax.axis_size("ctx") - 1, backward_turn, zero_b)

    def local_forward(query_arg, key_arg, rate_arg, solved_k_arg, solved_v_arg):
        final, outputs_all = lax.scan(
            solved_step, start_state, (query_arg, key_arg, rate_arg, solved_k_arg, solved_v_arg)
        )
        return (outputs_all, final)

    outputs_pair, pullback = jax.vjp(
        local_forward, query_blocks, key_blocks, rate_blocks, solved_k, solved_v
    )
    grad_qb, grad_kb, grad_rb, grad_sk, grad_sv = pullback((grad_blocks, end_grad))
    solve_k, solve_v, solve_r = solve_pull(
        (grad_sk.reshape(flat_shape), grad_sv.reshape(flat_shape))
    )
    grad_kb = grad_kb + solve_k.reshape(block_shape)
    grad_vb = solve_v.reshape(block_shape)
    grad_rb = grad_rb + solve_r.reshape(blocks, head_count, rows_block)
    grad_q, grad_k, grad_v, grad_b = arrange_pull((grad_qb, grad_kb, grad_vb, grad_rb))
    return (
        grad_q.reshape(tokens, head_count * HEAD_DIM).astype(jnp.bfloat16),
        grad_k.reshape(house_count, tokens, head_count * HEAD_DIM).astype(jnp.bfloat16),
        grad_v.reshape(house_count, tokens, head_count * HEAD_DIM).astype(jnp.bfloat16),
        grad_b,
    )


def solution(mesh):
    placed = (
        P("ctx", "head"),
        P(None, "ctx", "head"),
        P(None, "ctx", "head"),
        P("head", None, "ctx"),
        P(("ctx", "head"), None),
        P("head", None),
    )
    return jax.shard_map(
        shards,
        mesh=mesh,
        in_specs=placed,
        out_specs=(
            P("ctx", "head"),
            P(None, "ctx", "head"),
            P(None, "ctx", "head"),
            P("head", None, "ctx"),
        ),
        check_vma=False,
    )
```

profile of v0, /device:TPU:47, one launch (start us, length us, event | category | flops | bytes accessed | tf_op | source)
XLA Modules:
  0.0 1288.6 jit_solution(9259809610973605704)
XLA Ops:
  15.1 157.2 %custom-call.10 = f32[16,1,128,128]{2,3,1,0:T(8,128)S(1)} custom-call(f32[16,1,128,128]{3,2,1,0:T(8,128)S(1)} %add_bitcast_fusion), custom_call_target="InvertDiagBlocksLowerTriangular" | custom-call | tf_op jit(solution)/shard_map/jvp(jit(_solve_triangular))/vmap()/triangular_solve | solution.py:25
  185.6 6.6 fusion.126
  195.8 15.8 %while.111 = (s32[]{:T(128)}, f32[2,8,128,128]{3,2,1,0:T(8,128)}, f32[2,8,128,128]{3,2,1,0:T(8,128)}, f32[2,8,128,128]{3,2,1,0:T(8,128)}, f32[2,8,128,128]{3,2,1...) while((s32[]{:T(128)}, f32[2,8,128,128]{3,2,1,0:T(8,128)}, ...), condition=%wide.region_2.3_spmd.clone, body=%wide.region_1.2_spmd.clone.sunk | while | flops 705249408 | bytes 19294924 | solution.py:134
  212.6 12.6 while.114
  225.2 477.6 %while.110 = (s32[]{:T(128)}, f32[8,128,128]{2,1,0:T(8,128)S(1)}, f32[8,128,128]{2,1,0:T(8,128)}, f32[8,128,128]{2,1,0:T(8,128)}, s32[]{:T(128)}) while((s32[]{:T(128)}, f32[8,128,128]{2,1,0:T(8,128)S(1)}, f32[8,128,128]{2,1,0:T(8,128)}, f32[8,128,128]{2,1,0:T(8,128)}, s32[]{:T(128)}) %tuple.200), condition=%wide.region_10.11_spmd, body=%wide.region_9.10_spmd.sunk | while | flops 201457664 | bytes 4194405 | solution.py:154
  231.6 6.4 collective-permute-done.1
  247.1 6.4 collective-permute-done.1
  309.0 6.4 collective-permute-done.1
  324.5 6.4 collective-permute-done.1
  340.0 6.4 collective-permute-done.1
  402.0 6.4 collective-permute-done.1
  417.5 6.4 collective-permute-done.1
  433.0 6.4 collective-permute-done.1
  707.1 12.6 while.112
  719.7 8.1 while.115
  728.8 479.7 %while.109 = (s32[]{:T(128)}, f32[8,128,128]{2,1,0:T(8,128)S(1)}, f32[8,128,128]{2,1,0:T(8,128)}, f32[8,128,128]{2,1,0:T(8,128)}, s32[]{:T(128)}) while((s32[]{:T(128)}, f32[8,128,128]{2,1,0:T(8,128)S(1)}, f32[8,128,128]{2,1,0:T(8,128)}, f32[8,128,128]{2,1,0:T(8,128)}, s32[]{:T(128)}) %tuple.197), condition=%wide.region_8.9_spmd, body=%wide.region_7.8_spmd.sunk | while | flops 201457664 | bytes 4194405 | solution.py:160
  733.4 11.5 collective-permute-done
  749.5 10.9 collective-permute-done
  764.9 10.9 collective-permute-done
  780.4 10.9 collective-permute-done
  795.8 10.9 collective-permute-done
  811.3 10.9 collective-permute-done
  826.7 10.9 collective-permute-done
  842.2 10.9 collective-permute-done
  857.6 10.9 collective-permute-done
  873.1 10.9 collective-permute-done
  888.5 10.9 collective-permute-done
  904.0 10.9 collective-permute-done
  919.4 10.9 collective-permute-done
  934.9 10.9 collective-permute-done
  950.3 10.9 collective-permute-done
  965.8 10.9 collective-permute-done
  981.2 10.9 collective-permute-done
  996.7 10.9 collective-permute-done
  1012.1 10.9 collective-permute-done
  1027.6 10.9 collective-permute-done
  1043.0 10.9 collective-permute-done
  1058.5 10.9 collective-permute-done
  1073.9 10.9 collective-permute-done
  1089.4 10.9 collective-permute-done
  1104.8 10.9 collective-permute-done
  1120.3 10.9 collective-permute-done
  1135.7 10.9 collective-permute-done
  1151.2 10.9 collective-permute-done
  1166.6 10.9 collective-permute-done
  1182.1 10.9 collective-permute-done
  1197.5 10.9 collective-permute-done
  1212.7 38.1 %while.113 = (s32[]{:T(128)}, f32[8,128,128]{2,1,0:T(8,128)S(1)}, f32[2,8,64,128]{3,2,1,0:T(8,128)}, f32[2,8,128,128]{3,2,1,0:T(8,128)}, f32[2,8,128]{2,1,0:T(8,...) while((s32[]{:T(128)}, f32[8,128,128]{2,1,0:T(8,128)S(1)}, ...), condition=%wide.region_15.16_spmd.clone, body=%wide.region_13.15_spmd.clone.sunk | while | flops 1411136512 | bytes 45981328 | solution.py:163
  (399 shorter events, 718.5 us)
Async XLA Ops:
  7.2 178.4 %all-gather.2.cloned.1.call-start = ((), (), s32[]{:S(2)}) async-start(), calls=%async_computation | async-start | bytes 1310720 | tf_op jit(solution)/shard_map/all_gather | solution.py:81
  240.7 12.8 collective-permute-start.1
  256.2 12.8 collective-permute-start.1
  271.7 12.8 collective-permute-start.1
  287.2 12.8 collective-permute-start.1
  302.7 12.8 collective-permute-start.1
  318.1 12.8 collective-permute-start.1
  333.6 12.8 collective-permute-start.1
  349.1 12.8 collective-permute-start.1
  364.6 12.8 collective-permute-start.1
  380.1 12.8 collective-permute-start.1
  395.6 12.8 collective-permute-start.1
  411.1 12.8 collective-permute-start.1
  426.6 12.8 collective-permute-start.1
  442.1 12.8 collective-permute-start.1
  457.6 12.8 collective-permute-start.1
  473.1 12.8 collective-permute-start.1
  488.6 12.8 collective-permute-start.1
  504.1 12.8 collective-permute-start.1
  519.6 12.8 collective-permute-start.1
  535.1 12.8 collective-permute-start.1
  550.6 12.8 collective-permute-start.1
  566.1 12.8 collective-permute-start.1
  581.6 12.8 collective-permute-start.1
  597.1 12.8 collective-permute-start.1
  612.5 12.8 collective-permute-start.1
  628.0 12.8 collective-permute-start.1
  643.5 12.8 collective-permute-start.1
  659.0 12.8 collective-permute-start.1
  674.5 12.8 collective-permute-start.1
  690.0 12.8 collective-permute-start.1
  731.5 13.4 %collective-permute-start = (f32[8,128,128]{2,1,0:T(8,128)}, f32[8,128,128]{2,1,0:T(8,128)S(1)}, u32[]{:S(2)}, u32[]{:S(2)}) collective-permute-start(f32[8,128,128]{2,1,0:T(8,128)} %convolution_add_fusion.17), channel_id=1, source_target_pairs={{4,0},{8,4},{12,8},{16,12},{20,16},{24,20},{28,24},{32,28},{36,32}... | collective-permute-start | bytes 1572872 | tf_op jit(solution)/shard_map/while/body/eval_jaxpr/ppermute | solution.py:16
  747.6 12.8 collective-permute-start
  763.0 12.8 collective-permute-start
  778.5 12.8 collective-permute-start
  793.9 12.8 collective-permute-start
  809.4 12.8 collective-permute-start
  824.8 12.8 collective-permute-start
  840.3 12.8 collective-permute-start
  902.1 12.8 collective-permute-start
  917.5 12.8 collective-permute-start
  933.0 12.8 collective-permute-start
  948.4 12.8 collective-permute-start
  963.9 12.8 collective-permute-start
  979.3 12.8 collective-permute-start
  994.8 12.8 collective-permute-start
  1010.2 12.8 collective-permute-start
  1195.6 12.8 collective-permute-start
  (64 other events, 323.1 us)
Sparse Core Ops, SparseCore 0:
  9.7 23.9 all-gather.1
where the time goes:
time: 1300 us; the launch traced here: 1290 us
  waiting for transfers between devices  538 us (41%)
  matrix products  259 us (20%)
  starting transfers between devices  254 us (20%)
  other arithmetic  164 us (13%)
  local copies, waits for them, and re-layouts  56.6 us (4%)
  between operations  14.9 us (1%)
    ppermute x62, waiting for transfers between devices, shifted(): return lax.ppermute(value, axis, pairs)  537 us
    ppermute x62, starting transfers between devices, shifted(): return lax.ppermute(value, axis, pairs)  254 us
    dot_general x68, matrix products, matmul_heads(): return jnp.einsum('hij,hjk->hik', left, right, precision=highest)  181 us
    another operation x5, other arithmetic, block_solve(): jax.scipy.linalg.solve_triangular(system, joined, lower=True, unit_diagon...  157 us
  transfers between devices with their start and end apart: 63, of which 62 were waited for; matrix products, arithmetic and copies ran while one was open for 14% of the time, Pallas kernels for 0%

commit v1 on v0

v1 whole, which is shorter than its diff:
```python
import functools

import jax
import jax.numpy as jnp
from jax import lax
from jax.experimental import pallas as pl
from jax.experimental.pallas import tpu as pltpu
from jax.sharding import PartitionSpec as P

WIDTH = 128
HALF = 4
PER_STEP = 2
SCALE = WIDTH ** (-0.5)
bf16 = jnp.bfloat16
f32 = jnp.float32


def dims(left, right):
    return (((left,), (right,)), ((), ()))


def nn(a, b):
    return lax.dot_general(a, b, dims(1, 0), preferred_element_type=f32)


def nt(a, b):
    return lax.dot_general(a, b, dims(1, 1), preferred_element_type=f32)


def tn(a, b):
    return lax.dot_general(a, b, dims(0, 0), preferred_element_type=f32)


def split(x):
    high = x.astype(bf16)
    return high, (x - high.astype(f32)).astype(bf16)


def iota(shape, dim):
    return lax.broadcasted_iota(jnp.int32, shape, dim)


def order(shape, dim):
    index = iota(shape, dim)
    tokens = shape[dim] // 2
    return jnp.where(index < tokens, 2 * index, 2 * (index - tokens) + 1)


def level_table(rows):
    left = order((rows, rows), 0)
    right = order((rows, rows), 1)
    differ = left ^ right
    level = jnp.zeros((rows, rows), jnp.int32)
    for bit in range(1, (rows - 1).bit_length()):
        level = level + (differ >= (1 << bit)).astype(jnp.int32)
    return jnp.where(left > right, level, -1)


def eye_mask(rows):
    return iota((rows, rows), 0) == iota((rows, rows), 1)


def column(row, diagonal):
    return jnp.sum(jnp.where(diagonal, row, 0.0), axis=1, keepdims=True)


def inverse_norms(keys):
    wide = keys.astype(f32)
    return lax.rsqrt(jnp.sum(wide * wide, axis=1, keepdims=True) + 1e-06)


def pick(ref, head):
    lanes = slice(head * WIDTH, (head + 1) * WIDTH)
    return jnp.concatenate([ref[0, :, lanes], ref[1, :, lanes]], axis=0)


def rate_row(ref, head):
    return jnp.concatenate([ref[head, 0:1, :], ref[head, 1:2, :]], axis=1)


def maps_kernel(place, k_ref, v_ref, b_ref, send_ref, keep_ref, nh_ref, nl_ref, y_ref, z_ref, level_ref):
    step = pl.program_id(0)
    rows = level_ref.shape[0]

    @pl.when(step == 0)
    def _():
        level_ref[...] = level_table(rows)

    diagonal = eye_mask(rows)
    heads = range(PER_STEP)
    keys = [pick(k_ref, h) for h in heads]
    values = [pick(v_ref, h) for h in heads]
    rates = [rate_row(b_ref, h) for h in heads]
    rate_cols = [column(r, diagonal) for r in rates]
    norms = [inverse_norms(k) for k in keys]
    grams = []
    for h in heads:
        raw = nt(keys[h], keys[h])
        norm_row = lax.rsqrt(jnp.sum(jnp.where(diagonal, raw, 0.0), axis=0, keepdims=True) + 1e-06)
        grams.append(jnp.where(level_ref[...] >= 0, raw * norms[h] * norm_row, 0.0))
    systems = [grams[h] * rates[h] for h in heads]
    ident = jnp.where(diagonal, 1.0, 0.0).astype(f32)
    inverse = [ident - jnp.where(level_ref[...] == 0, systems[h], 0.0) for h in heads]
    for level in range(1, (rows - 1).bit_length()):
        rounded = [t.astype(bf16) for t in inverse]
        inner = [
            nn(jnp.where(level_ref[...] == level, systems[h], 0.0).astype(bf16), rounded[h]).astype(bf16)
            for h in heads
        ]
        inverse = [inverse[h] - nn(rounded[h], inner[h]) for h in heads]
    rounded = [t.astype(bf16) for t in inverse]
    core_high = [nn(rounded[h], grams[h].astype(bf16)).astype(bf16) for h in heads]
    residual = []
    for h in heads:
        high, low = split(systems[h])
        residual.append(grams[h] - core_high[h].astype(f32) - nn(high, core_high[h]) - nn(low, core_high[h]))
    core_low = [nn(rounded[h], residual[h].astype(bf16)).astype(bf16) for h in heads]
    for h in heads:
        nh_ref[h] = core_high[h]
        nl_ref[h] = core_low[h]
    for h in heads:
        both = jnp.concatenate([keys[h].astype(f32) * norms[h], values[h].astype(f32)], axis=1)
        high, low = split(both * rate_cols[h])
        solved = both - nn(core_high[h], high) - nn(core_low[h], high) - nn(core_high[h], low)
        y_ref[h] = solved[:, :WIDTH]
        z_ref[h] = solved[:, WIDTH:]
        high, low = split(solved * (rate_cols[h] * norms[h]))
        mapped = (tn(keys[h], high) + tn(keys[h], low)).astype(bf16)
        steps_half = HALF // PER_STEP

        @pl.when(step < steps_half)
        def _():
            send_ref[step * PER_STEP + h] = mapped

        @pl.when(step >= steps_half)
        def _():
            keep_ref[(step - steps_half) * PER_STEP + h] = mapped


def local_grad_kernel(place, og_ref, w_ref, k_ref, q_ref, b_ref, y_ref, send_ref, keep_ref, do_ref, u_ref):
    step = pl.program_id(0)
    steps_half = HALF // PER_STEP
    tokens = q_ref.shape[0]
    rows = 2 * tokens
    diagonal = eye_mask(rows)
    seen = order((rows, tokens), 0) < 2 * (iota((rows, tokens), 1) + 1)
    for h in range(PER_STEP):
        lanes = slice(h * WIDTH, (h + 1) * WIDTH)
        grad = nt(og_ref[...], w_ref[lanes, :]).astype(bf16)
        do_ref[h] = grad
        keys = pick(k_ref, h)
        query = q_ref[:, lanes]
        rate_col = column(rate_row(b_ref, h), diagonal)
        scores = jnp.where(seen, nt(keys, query) * (inverse_norms(keys) * SCALE), 0.0)
        high, low = split(scores)
        reached = nn(high, grad) + nn(low, grad)
        u_ref[h] = reached
        uh, ul = split(reached * rate_col)
        yh, yl = split(y_ref[h])
        local = (tn(query, grad) * SCALE - tn(yh, uh) - tn(yl, uh) - tn(yh, ul)).astype(bf16)

        @pl.when(step < steps_half)
        def _():
            send_ref[step * PER_STEP + h] = local

        @pl.when(step >= steps_half)
        def _():
            keep_ref[(step - steps_half) * PER_STEP + h] = local


def pair_kernel(place, keep_ref, got_ref, gkeep_ref, ggot_ref, *outs):
    core = place[0]
    spot = place[1]
    for shift in range(HALF):
        slot = lax.rem(spot + shift, HALF)
        mine, other = keep_ref[slot].astype(f32), got_ref[slot].astype(f32)
        first = jnp.where(core == 0, mine, other)
        second = jnp.where(core == 0, other, mine)
        mine, other = gkeep_ref[slot].astype(f32), ggot_ref[slot].astype(f32)
        gfirst = jnp.where(core == 0, mine, other)
        gsecond = jnp.where(core == 0, other, mine)
        joined = first + second - nn(second[:, :WIDTH].astype(bf16), first.astype(bf16))
        gjoined = gfirst + gsecond - tn(first[:, :WIDTH].astype(bf16), gsecond.astype(bf16))
        outs[shift][:, : 2 * WIDTH] = joined.astype(bf16)
        outs[shift][:, 2 * WIDTH :] = gjoined.astype(bf16)


def join(first, second):
    forward = first[:, : 2 * WIDTH] + second[:, : 2 * WIDTH]
    forward = forward - nn(second[:, :WIDTH].astype(bf16), first[:, : 2 * WIDTH].astype(bf16))
    backward = first[:, 2 * WIDTH :] + second[:, 2 * WIDTH :]
    backward = backward - tn(first[:, :WIDTH].astype(bf16), second[:, 2 * WIDTH :].astype(bf16))
    return jnp.concatenate([forward, backward], axis=1)


def gather_slots(slots, refs, spot):
    for shift in range(HALF):
        slots[lax.rem(spot + HALF - shift, HALF)] = refs[shift][...]


def row_kernel(place, a_ref, b_ref, c_ref, d_ref, out_ref, slots):
    gather_slots(slots, (a_ref, b_ref, c_ref, d_ref), place[1])
    maps = [slots[i].astype(f32) for i in range(HALF)]
    out_ref[...] = join(join(maps[0], maps[1]), join(maps[2], maps[3])).astype(bf16)


def advance(block, state):
    high, low = split(state)
    moved = nn(block[:, :WIDTH], jnp.concatenate([high, low], axis=1))
    return state - moved[:, :WIDTH] - moved[:, WIDTH:] + block[:, WIDTH : 2 * WIDTH].astype(f32)


def retreat(block, grad):
    high, low = split(grad)
    moved = tn(block[:, :WIDTH], jnp.concatenate([high, low], axis=1))
    return grad - moved[:, :WIDTH] - moved[:, WIDTH:] + block[:, 2 * WIDTH :].astype(f32)


def expand_kernel(place, a_ref, b_ref, c_ref, d_ref, e_ref, f_ref, g_ref, h_ref, o0, o1, o2, o3, chips, lines, found):
    spot, line = place[1], place[2]
    gather_slots(chips, (a_ref, b_ref, c_ref, d_ref), spot)
    gather_slots(lines, (e_ref, f_ref, g_ref, h_ref), line)
    state = jnp.zeros((WIDTH, WIDTH), f32)
    grad = jnp.zeros((WIDTH, WIDTH), f32)
    for i in range(HALF - 1):
        state = jnp.where(i < line, advance(lines[i], state), state)
        back = HALF - 1 - i
        grad = jnp.where(back > line, retreat(lines[back], grad), grad)
    for i in range(HALF):
        found[i, :, :WIDTH] = state.astype(bf16)
        back = HALF - 1 - i
        found[back, :, WIDTH:] = grad.astype(bf16)
        if i < HALF - 1:
            state = advance(chips[i], state)
            grad = retreat(chips[back], grad)
    for shift, out in enumerate((o0, o1, o2, o3)):
        out[...] = found[lax.rem(spot + shift, HALF)]


def down_kernel(place, a_ref, b_ref, c_ref, d_ref, keep_ref, got_ref, gkeep_ref, ggot_ref, own_ref, send_ref, slots):
    core = place[0]
    gather_slots(slots, (a_ref, b_ref, c_ref, d_ref), place[1])
    for slot in range(HALF):
        state = slots[slot, :, :WIDTH]
        grad = slots[slot, :, WIDTH:]
        first = jnp.where(core == 0, keep_ref[slot].astype(f32), got_ref[slot].astype(f32))
        second = jnp.where(core == 0, got_ref[slot, :, :WIDTH].astype(f32), keep_ref[slot, :, :WIDTH].astype(f32))
        gsecond = jnp.where(core == 0, ggot_ref[slot].astype(f32), gkeep_ref[slot].astype(f32))
        middle = state.astype(f32) - nn(first[:, :WIDTH].astype(bf16), state) + first[:, WIDTH:]
        gmiddle = grad.astype(f32) - tn(second.astype(bf16), grad) + gsecond
        early = jnp.concatenate([state.astype(f32), gmiddle], axis=1)
        late = jnp.concatenate([middle, grad.astype(f32)], axis=1)
        own_ref[slot] = jnp.where(core == 0, early, late).astype(bf16)
        send_ref[slot] = jnp.where(core == 0, late, early).astype(bf16)


def grads_kernel(
    place, k_ref, q_ref, b_ref, do_ref, nh_ref, nl_ref, y_ref, z_ref, u_ref, own_ref, got_ref,
    dq_ref, dk_ref, dv_ref, db_ref,
):
    step = pl.program_id(0)
    steps_half = HALF // PER_STEP
    tokens = q_ref.shape[0]
    rows = 2 * tokens
    diagonal = eye_mask(rows)
    before = order((rows, rows), 1) < order((rows, rows), 0)
    seen = order((tokens, rows), 1) < 2 * (iota((tokens, rows), 0) + 1)
    seen_t = order((rows, tokens), 0) < 2 * (iota((rows, tokens), 1) + 1)
    for h in range(PER_STEP):
        lanes = slice(h * WIDTH, (h + 1) * WIDTH)
        slot = lax.rem(step, steps_half) * PER_STEP + h
        ends = jnp.where(step < steps_half, got_ref[slot].astype(f32), own_ref[slot].astype(f32)).astype(bf16)
        state, after = ends[:, :WIDTH], ends[:, WIDTH:]
        keys = pick(k_ref, h)
        query = q_ref[:, lanes]
        grad = do_ref[h]
        rate = column(rate_row(b_ref, h), diagonal)
        norm = inverse_norms(keys)
        yh, yl = split(y_ref[h])
        errors = nn(yh, state) + nn(yl, state) - z_ref[h]
        weighted = errors * rate
        d_weighted = -u_ref[h] - norm * nn(keys, after)
        high, low = split(d_weighted * rate)
        back = d_weighted - tn(nh_ref[h], high) - tn(nl_ref[h], high) - tn(nh_ref[h], low)
        scaled = back * rate
        d_rate = jnp.sum(errors * back, axis=1, keepdims=True)
        d_rate = jnp.sum(jnp.where(diagonal, d_rate, 0.0), axis=0, keepdims=True)
        db_ref[h, 0:1, :] = d_rate[:, :tokens]
        db_ref[h, 1:2, :] = d_rate[:, tokens:]
        dv_ref[0, :, lanes] = (-scaled[:tokens]).astype(bf16)
        dv_ref[1, :, lanes] = (-scaled[tokens:]).astype(bf16)
        wh, wl = split(weighted)
        fh, fl = split(scaled)
        wn = (weighted * norm).astype(bf16)
        fn = (scaled * norm).astype(bf16)
        d_scores = jnp.where(seen, -nt(grad, wn), 0.0).astype(bf16)
        dq = nt(grad, state) + nn(d_scores, keys)
        dq_ref[:, lanes] = (dq * SCALE).astype(bf16)
        d_scores_t = jnp.where(seen_t, -nt(wh, grad), 0.0).astype(bf16)
        lower = nt(jnp.concatenate([fh, fl], axis=1), jnp.concatenate([wn, wn], axis=1))
        upper = nt(jnp.concatenate([wh, wl], axis=1), jnp.concatenate([fn, fn], axis=1))
        pairs = jnp.where(before, lower, jnp.where(diagonal, 0.0, upper)).astype(bf16)
        dk = nn(d_scores_t, query) * SCALE - nt(wh, after) + nt(fh, state) - nn(pairs, keys)
        unit = keys.astype(f32) * norm
        dk = norm * (dk - unit * jnp.sum(unit * dk, axis=1, keepdims=True))
        dk_ref[0, :, lanes] = dk[:tokens].astype(bf16)
        dk_ref[1, :, lanes] = dk[tokens:].astype(bf16)


def whole(shape):
    return pl.BlockSpec(shape, lambda *unused: (0,) * len(shape))


def run(kernel, name, place, args, in_specs, outs, out_specs, grid=(1,), scratch=(), cost=None):
    return pl.pallas_call(
        kernel,
        name=name,
        grid_spec=pltpu.PrefetchScalarGridSpec(
            num_scalar_prefetch=1,
            grid=grid,
            in_specs=in_specs,
            out_specs=out_specs,
            scratch_shapes=list(scratch),
        ),
        out_shape=[jax.ShapeDtypeStruct(shape, dtype) for shape, dtype in outs],
        compiler_params=pltpu.CompilerParams(vmem_limit_bytes=40 * 2**20),
        cost_estimate=cost,
    )(place, *args)


def small(kernel, name, place, args, outs, scratch=()):
    return run(
        kernel, name, place, args,
        [whole(a.shape) for a in args],
        outs,
        [whole(shape) for shape, unused in outs],
        scratch=scratch,
    )


def shards(queries, key_input, value_input, beta_rates, out_grad, out_weight):
    tokens = queries.shape[0]
    heads = queries.shape[1] // WIDTH
    rows = 2 * tokens
    model = out_weight.shape[1]
    me = lax.axis_index("ctx")
    place = jnp.stack([me % 2, (me // 2) % HALF, me // (2 * HALF)]).astype(jnp.int32)

    def move(value, target):
        return lax.ppermute(value, "ctx", [(i, target(i)) for i in range(32)])

    def other_core(i):
        return i ^ 1

    def along_x(by):
        return lambda i: (i // 8) * 8 + ((i // 2 + by) % HALF) * 2 + i % 2

    def along_y(by):
        return lambda i: (i + 8 * by) % 32

    steps = heads // PER_STEP
    half_steps = steps // 2

    def block(step, place_ref):
        return lax.rem(step + half_steps * (1 - place_ref[0]), steps)

    kv_spec = pl.BlockSpec((2, tokens, PER_STEP * WIDTH), lambda s, p: (0, 0, block(s, p)))
    q_spec = pl.BlockSpec((tokens, PER_STEP * WIDTH), lambda s, p: (0, block(s, p)))
    b_spec = pl.BlockSpec((PER_STEP, 2, tokens), lambda s, p: (block(s, p), 0, 0))

    def by_step(*shape):
        return pl.BlockSpec((PER_STEP,) + shape, lambda s, p: (s, 0, 0))

    gathered = lax.all_gather(out_grad, "head", axis=0, tiled=True)
    send, keep, core_high, core_low, solved_k, solved_v = run(
        maps_kernel, "maps", place, (key_input, value_input, beta_rates),
        [kv_spec, kv_spec, b_spec],
        [((HALF, WIDTH, 2 * WIDTH), bf16)] * 2 + [((heads, rows, rows), bf16)] * 2
        + [((heads, rows, WIDTH), f32)] * 2,
        [whole((HALF, WIDTH, 2 * WIDTH))] * 2 + [by_step(rows, rows)] * 2 + [by_step(rows, WIDTH)] * 2,
        grid=(steps,),
        scratch=[pltpu.VMEM((rows, rows), jnp.int32)],
        cost=pl.CostEstimate(flops=14_000_000_000, transcendentals=0, bytes_accessed=8_000_000),
    )
    got = move(send, other_core)
    gsend, gkeep, grad, reached = run(
        local_grad_kernel, "local_grad", place,
        (gathered, out_weight, key_input, queries, beta_rates, solved_k),
        [
            whole((tokens, model)),
            pl.BlockSpec((PER_STEP * WIDTH, model), lambda s, p: (block(s, p), 0)),
            kv_spec, q_spec, b_spec, by_step(rows, WIDTH),
        ],
        [((HALF, WIDTH, WIDTH), bf16)] * 2 + [((heads, tokens, WIDTH), bf16), ((heads, rows, WIDTH), f32)],
        [whole((HALF, WIDTH, WIDTH))] * 2 + [by_step(tokens, WIDTH), by_step(rows, WIDTH)],
        grid=(steps,),
        cost=pl.CostEstimate(flops=4_000_000_000, transcendentals=0, bytes_accessed=14_000_000),
    )
    ggot = move(gsend, other_core)
    map_shape = ((WIDTH, 3 * WIDTH), bf16)
    chip = small(pair_kernel, "pair", place, (keep, got, gkeep, ggot), [map_shape] * HALF)
    chip = [chip[0]] + [move(chip[by], along_x(by)) for by in range(1, HALF)]
    slots = pltpu.VMEM((HALF, WIDTH, 3 * WIDTH), bf16)
    (line,) = small(row_kernel, "line", place, chip, [map_shape], [slots])
    lines = [line] + [move(line, along_y(by)) for by in range(1, HALF)]
    ends_shape = ((WIDTH, 2 * WIDTH), bf16)
    ends_slots = pltpu.VMEM((HALF, WIDTH, 2 * WIDTH), bf16)
    ends = small(expand_kernel, "expand", place, chip + lines, [ends_shape] * HALF, [slots, slots, ends_slots])
    ends = [ends[0]] + [move(ends[by], along_x(by)) for by in range(1, HALF)]
    own, passed = small(
        down_kernel, "down", place, ends + [keep, got, gkeep, ggot],
        [((HALF, WIDTH, 2 * WIDTH), bf16)] * 2, [ends_slots],
    )
    taken = move(passed, other_core)
    return tuple(run(
        grads_kernel, "grads", place,
        (key_input, queries, beta_rates, grad, core_high, core_low, solved_k, solved_v, reached, own, taken),
        [
            kv_spec, q_spec, b_spec, by_step(tokens, WIDTH), by_step(rows, rows), by_step(rows, rows),
            by_step(rows, WIDTH), by_step(rows, WIDTH), by_step(rows, WIDTH),
            whole((HALF, WIDTH, 2 * WIDTH)), whole((HALF, WIDTH, 2 * WIDTH)),
        ],
        [
            (queries.shape, bf16), (key_input.shape, bf16), (value_input.shape, bf16), (beta_rates.shape, f32),
        ],
        [q_spec, kv_spec, kv_spec, b_spec],
        grid=(steps,),
        cost=pl.CostEstimate(flops=8_000_000_000, transcendentals=0, bytes_accessed=14_000_000),
    ))


def solution(mesh):
    placed = (
        P("ctx", "head"),
        P(None, "ctx", "head"),
        P(None, "ctx", "head"),
        P("head", None, "ctx"),
        P(("ctx", "head"), None),
        P("head", None),
    )
    return jax.shard_map(
        shards,
        mesh=mesh,
        in_specs=placed,
        out_specs=(
            P("ctx", "head"),
            P(None, "ctx", "head"),
            P(None, "ctx", "head"),
            P("head", None, "ctx"),
        ),
        check_vma=False,
    )
```

time: 1300 us -> 102 us (0.08)
  the two profiles are of different devices: /device:TPU:47 before, /device:TPU:1 now
where the time goes in v1:
time: 102 us; the launch traced here: 101 us
  Pallas kernels  41.4 us (41%)
  starting transfers between devices  20.1 us (20%)
  waiting for transfers between devices  15.3 us (15%)
  between operations  14.1 us (14%)
  local copies, waits for them, and re-layouts  10.3 us (10%)
    pallas_call x7, Pallas kernels, run(): pl.pallas_call(kernel, name=name, grid_spec=pltpu.PrefetchScalarGridSpec(...  41.4 us
    ppermute x12, starting transfers between devices, move(): return lax.ppermute(value, 'ctx', [(i, target(i)) for i in range(32)])  20 us
    ppermute x12, waiting for transfers between devices, move(): return lax.ppermute(value, 'ctx', [(i, target(i)) for i in range(32)])  13 us
    unnamed x28, local copies, waits for them, and re-layouts  10.3 us
  transfers between devices with their start and end apart: 13, of which 11 were waited for; matrix products, arithmetic and copies ran while one was open for 0% of the time, Pallas kernels for 29%

profile of v1, /device:TPU:1, one launch (start us, length us, event | category | flops | bytes accessed | tf_op | source)
XLA Modules:
  0.0 101.3 jit_solution(895716443966346842)
XLA Ops:
  7.2 0.0 all-gather.2.cloned.1.call-start
  7.2 0.7 all-gather.2.cloned.1.call-update
  7.9 0.1 pad_add_fusion.place
  8.0 1.0 %copy-done.2 = bf16[2,128,1024]{2,1,0:T(8,128)(2,1)S(1)} copy-done((bf16[2,128,1024]{2,1,0:T(8,128)(2,1)S(1)}, bf16[2,128,1024]{2,1,0:T(8,128)(2,1)}, u32[]{:S(2)}) %copy-start.2) | copy-done | bytes 524312
  9.1 1.0 %copy-done.3 = bf16[2,128,1024]{2,1,0:T(8,128)(2,1)S(1)} copy-done((bf16[2,128,1024]{2,1,0:T(8,128)(2,1)S(1)}, bf16[2,128,1024]{2,1,0:T(8,128)(2,1)}, u32[]{:S(2)}) %copy-start.3) | copy-done | bytes 524312
  10.1 0.7 copy-done.6
  10.8 19.4 %maps.1 = (bf16[4,128,256]{2,1,0:T(8,128)(2,1)S(1)}, bf16[4,128,256]{2,1,0:T(8,128)(2,1)S(1)}, bf16[8,256,256]{2,1,0:T(8,128)(2,1)S(1)}, bf16[8,256,256]{2,1,0:T...) custom-call(s32[3]{0:T(128)S(1)} %pad_add_fusion.place, bf16[2,128,1024]{2,1,0:T(8,128)(2,1)S(1)} %copy-done.3, ...), custom_call_target="tpu_custom_call" | custom-call | flops 14000000000 | bytes 8000000 | tf_op jit(solution)/shard_map/maps/pallas_call | solution.py:315
  30.2 0.0 copy-start.8
  30.2 1.0 copy-done.8
  31.2 1.0 copy-done.10
  32.2 1.0 copy-done.12
  33.1 1.4 %collective-permute-start = (bf16[4,128,256]{2,1,0:T(8,128)(2,1)S(1)}, bf16[4,128,256]{2,1,0:T(8,128)(2,1)S(1)}, u32[]{:S(2)}, u32[]{:S(2)}) collective-permute-start(bf16[4,128,256]{2,1,0:T(8,128)(2,1)S(1)} %get-tuple-element.31), channel_id=1, source_target_pairs={{0,4},{4,0},{8,12},{12,8},{16,20},{20,16},{24,28},{28,24},{32,36},... | collective-permute-start | bytes 786440 | tf_op jit(solution)/shard_map/ppermute | solution.py:350
  34.5 1.6 %all-gather.2.cloned.1.call-done.og_ref = bf16[128,4096]{1,0:T(8,128)(2,1)} async-done(((bf16[32,4096]{1,0:T(8,128)(2,1)}), bf16[128,4096]{1,0:T(8,128)(2,1)}) %all-gather.2.cloned.1.call-update) | async-done | bytes 1048592 | tf_op jit(solution)/shard_map/all_gather | solution.py:374
  36.2 0.0 copy-done.4
  36.2 0.0 copy-done.5
  36.2 0.0 copy-done.7
  36.2 3.4 %copy-done = bf16[1024,4096]{1,0:T(8,128)(2,1)S(1)} copy-done((bf16[1024,4096]{1,0:T(8,128)(2,1)S(1)}, bf16[1024,4096]{1,0:T(8,128)(2,1)}, u32[]{:S(2)}) %copy-start) | copy-done | bytes 8388632
  39.6 1.2 %copy-done.1 = bf16[128,4096]{1,0:T(8,128)(2,1)S(1)} copy-done((bf16[128,4096]{1,0:T(8,128)(2,1)S(1)}, bf16[128,4096]{1,0:T(8,128)(2,1)}, u32[]{:S(2)}) %copy-start.1) | copy-done | bytes 1048600
  40.8 9.7 %local_grad.1 = (bf16[4,128,128]{2,1,0:T(8,128)(2,1)S(1)}, bf16[4,128,128]{2,1,0:T(8,128)(2,1)S(1)}, bf16[8,128,128]{2,1,0:T(8,128)(2,1)S(1)}, f32[8,256,128]{2,1,0:T(8,128)S(1)}) custom-call(s32[3]{0:T(128)S(1)} %pad_add_fusion.place, bf16[128,4096]{1,0:T(8,128)(2,1)S(1)} %copy-done.1, bf16[1024,4096]{1,0:T(8,128)(2,1)S(1)} %copy-done, ...), custom_call_target="tpu_custom_call" | custom-call | flops 4000000000 | bytes 14000000 | tf_op jit(solution)/shard_map/local_grad/pallas_call | solution.py:315
  50.5 1.7 %collective-permute-start.1 = (bf16[4,128,128]{2,1,0:T(8,128)(2,1)S(1)}, bf16[4,128,128]{2,1,0:T(8,128)(2,1)S(1)}, u32[]{:S(2)}, u32[]{:S(2)}) collective-permute-start(bf16[4,128,128]{2,1,0:T(8,128)(2,1)S(1)} %get-tuple-element.33), channel_id=1, source_target_pairs={{0,4},{4,0},{8,12},{12,8},{16,20},{20,16},{24,28},{28,24},{32,36},... | collective-permute-start | bytes 393224 | tf_op jit(solution)/shard_map/ppermute | solution.py:350
  52.2 0.0 collective-permute-done.got_ref
  52.2 1.0 collective-permute-done.1.ggot_ref
  53.1 0.9 pair.1
  54.0 1.3 %collective-permute-start.2 = (bf16[128,384]{1,0:T(8,128)(2,1)S(1)}, bf16[128,384]{1,0:T(8,128)(2,1)S(1)}, u32[]{:S(2)}, u32[]{:S(2)}) collective-permute-start(bf16[128,384]{1,0:T(8,128)(2,1)S(1)} %get-tuple-element.35), channel_id=1, source_target_pairs={{0,8},{4,12},{8,16},{12,20},{16,24},{20,28},{24,0},{28,4},{32,40},... | collective-permute-start | bytes 294920 | tf_op jit(solution)/shard_map/ppermute | solution.py:350
  55.3 2.4 %collective-permute-start.3 = (bf16[128,384]{1,0:T(8,128)(2,1)S(1)}, bf16[128,384]{1,0:T(8,128)(2,1)S(1)}, u32[]{:S(2)}, u32[]{:S(2)}) collective-permute-start(bf16[128,384]{1,0:T(8,128)(2,1)S(1)} %get-tuple-element.36), channel_id=1, source_target_pairs={{0,16},{4,20},{8,24},{12,28},{16,0},{20,4},{24,8},{28,12},{32,48},... | collective-permute-start | bytes 294920 | tf_op jit(solution)/shard_map/ppermute | solution.py:350
  57.7 1.2 %collective-permute-start.4 = (bf16[128,384]{1,0:T(8,128)(2,1)S(1)}, bf16[128,384]{1,0:T(8,128)(2,1)S(1)}, u32[]{:S(2)}, u32[]{:S(2)}) collective-permute-start(bf16[128,384]{1,0:T(8,128)(2,1)S(1)} %get-tuple-element.37), channel_id=1, source_target_pairs={{0,24},{4,28},{8,0},{12,4},{16,8},{20,12},{24,16},{28,20},{32,56},... | collective-permute-start | bytes 294920 | tf_op jit(solution)/shard_map/ppermute | solution.py:350
  58.9 0.5 collective-permute-done.2.b_ref
  59.3 3.0 %collective-permute-done.3.c_ref = bf16[128,384]{1,0:T(8,128)(2,1)S(1)} collective-permute-done((bf16[128,384]{1,0:T(8,128)(2,1)S(1)}, bf16[128,384]{1,0:T(8,128)(2,1)S(1)}, u32[]{:S(2)}, u32[]{:S(2)}) %collective-permute-start.3) | collective-permute-done | bytes 98336 | tf_op jit(solution)/shard_map/ppermute | solution.py:350
  62.3 0.0 collective-permute-done.4.d_ref
  62.3 0.9 line.1.e_ref
  63.3 2.5 %collective-permute-start.7 = (bf16[128,384]{1,0:T(8,128)(2,1)S(1)}, bf16[128,384]{1,0:T(8,128)(2,1)S(1)}, u32[]{:S(2)}, u32[]{:S(2)}) collective-permute-start(bf16[128,384]{1,0:T(8,128)(2,1)S(1)} %line.1.e_ref), channel_id=1, source_target_pairs={{0,96},{4,100},{8,104},{12,108},{16,112},{20,116},{24,120},{28,124... | collective-permute-start | bytes 294920 | tf_op jit(solution)/shard_map/ppermute | solution.py:350
  65.8 0.6 collective-permute-start.6
  66.4 0.5 collective-permute-start.5
  67.0 0.5 collective-permute-done.7.h_ref
  67.4 3.4 %collective-permute-done.6.g_ref = bf16[128,384]{1,0:T(8,128)(2,1)S(1)} collective-permute-done((bf16[128,384]{1,0:T(8,128)(2,1)S(1)}, bf16[128,384]{1,0:T(8,128)(2,1)S(1)}, u32[]{:S(2)}, u32[]{:S(2)}) %collective-permute-start.6) | collective-permute-done | bytes 98336 | tf_op jit(solution)/shard_map/ppermute | solution.py:350
  70.8 1.4 %collective-permute-done.5.f_ref = bf16[128,384]{1,0:T(8,128)(2,1)S(1)} collective-permute-done((bf16[128,384]{1,0:T(8,128)(2,1)S(1)}, bf16[128,384]{1,0:T(8,128)(2,1)S(1)}, u32[]{:S(2)}, u32[]{:S(2)}) %collective-permute-start.5) | collective-permute-done | bytes 98336 | tf_op jit(solution)/shard_map/ppermute | solution.py:350
  72.2 1.6 %expand.1 = (bf16[128,256]{1,0:T(8,128)(2,1)S(1)}, bf16[128,256]{1,0:T(8,128)(2,1)S(1)}, bf16[128,256]{1,0:T(8,128)(2,1)S(1)}, bf16[128,256]{1,0:T(8,128)(2,1)S(1)}) custom-call(s32[3]{0:T(128)S(1)} %pad_add_fusion.place, bf16[128,384]{1,0:T(8,128)(2,1)S(1)} %get-tuple-element.34.a_ref, bf16[128,384]{1,0:T(8,128)(2,1)S(1)} %collective-permute-done.2.b_ref, ...), custom_call_target="tpu_custom_call" | custom-call | tf_op jit(solution)/shard_map/expand/pallas_call | solution.py:315
  73.8 0.4 collective-permute-start.8
  74.2 2.0 %collective-permute-start.9 = (bf16[128,256]{1,0:T(8,128)(2,1)S(1)}, bf16[128,256]{1,0:T(8,128)(2,1)S(1)}, u32[]{:S(2)}, u32[]{:S(2)}) collective-permute-start(bf16[128,256]{1,0:T(8,128)(2,1)S(1)} %get-tuple-element.40), channel_id=1, source_target_pairs={{0,16},{4,20},{8,24},{12,28},{16,0},{20,4},{24,8},{28,12},{32,48},... | collective-permute-start | bytes 196616 | tf_op jit(solution)/shard_map/ppermute | solution.py:350
  76.2 1.2 %collective-permute-start.10 = (bf16[128,256]{1,0:T(8,128)(2,1)S(1)}, bf16[128,256]{1,0:T(8,128)(2,1)S(1)}, u32[]{:S(2)}, u32[]{:S(2)}) collective-permute-start(bf16[128,256]{1,0:T(8,128)(2,1)S(1)} %get-tuple-element.41), channel_id=1, source_target_pairs={{0,24},{4,28},{8,0},{12,4},{16,8},{20,12},{24,16},{28,20},{32,56},... | collective-permute-start | bytes 196616 | tf_op jit(solution)/shard_map/ppermute | solution.py:350
  77.4 0.8 collective-permute-done.8.b_ref
  78.2 0.7 collective-permute-done.9.c_ref
  78.9 0.6 collective-permute-done.10.d_ref
  79.5 0.8 down.1
  80.3 4.8 %collective-permute-start.11 = (bf16[4,128,256]{2,1,0:T(8,128)(2,1)S(1)}, bf16[4,128,256]{2,1,0:T(8,128)(2,1)S(1)}, u32[]{:S(2)}, u32[]{:S(2)}) collective-permute-start(bf16[4,128,256]{2,1,0:T(8,128)(2,1)S(1)} %get-tuple-element.43), channel_id=1, source_target_pairs={{0,4},{4,0},{8,12},{12,8},{16,20},{20,16},{24,28},{28,24},{32,36},... | collective-permute-start | bytes 786440 | tf_op jit(solution)/shard_map/ppermute | solution.py:350
  85.1 1.2 %collective-permute-done.11.got_ref = bf16[4,128,256]{2,1,0:T(8,128)(2,1)S(1)} collective-permute-done((bf16[4,128,256]{2,1,0:T(8,128)(2,1)S(1)}, bf16[4,128,256]{2,1,0:T(8,128)(2,1)S(1)}, u32[]{:S(2)}, u32[]{:S(2)}) %collective-permute-start.11) | collective-permute-done | bytes 262176 | tf_op jit(solution)/shard_map/ppermute | solution.py:350
  86.3 0.0 copy-done.9
  86.3 8.2 %grads.1 = (bf16[128,1024]{1,0:T(8,128)(2,1)}, bf16[2,128,1024]{2,1,0:T(8,128)(2,1)}, bf16[2,128,1024]{2,1,0:T(8,128)(2,1)}, f32[8,2,128]{2,1,0:T(2,128)}) custom-call(s32[3]{0:T(128)S(1)} %pad_add_fusion.place, bf16[2,128,1024]{2,1,0:T(8,128)(2,1)S(1)} %copy-done.4, bf16[128,1024]{1,0:T(8,128)(2,1)S(1)} %copy-done.5, f32[8,2,128]{2,1,0:T(2,128)S(1)} %copy-done.7, ...), custom_call_target="tpu_custom_call" | custom-call | flops 8000000000 | bytes 14000000 | tf_op jit(solution)/shard_map/grads/pallas_call | solution.py:315
  (15 shorter events, 0.0 us)
Async XLA Ops:
  7.2 29.0 %all-gather.2.cloned.1.call-start = ((), (), s32[]{:S(2)}) async-start(), calls=%async_computation | async-start | bytes 1310720 | tf_op jit(solution)/shard_map/all_gather | solution.py:374
  8.0 1.0 %copy-start.2 = (bf16[2,128,1024]{2,1,0:T(8,128)(2,1)S(1)}, bf16[2,128,1024]{2,1,0:T(8,128)(2,1)}, u32[]{:S(2)}) copy-start(bf16[2,128,1024]{2,1,0:T(8,128)(2,1)} %v_ref.1) | copy-start | bytes 1572868
  9.1 1.0 %copy-start.3 = (bf16[2,128,1024]{2,1,0:T(8,128)(2,1)S(1)}, bf16[2,128,1024]{2,1,0:T(8,128)(2,1)}, u32[]{:S(2)}) copy-start(bf16[2,128,1024]{2,1,0:T(8,128)(2,1)} %k_ref.5) | copy-start | bytes 1572868
  10.1 0.7 copy-start.6
  10.8 25.4 %copy-start.4 = (bf16[2,128,1024]{2,1,0:T(8,128)(2,1)S(1)}, bf16[2,128,1024]{2,1,0:T(8,128)(2,1)}, u32[]{:S(2)}) copy-start(bf16[2,128,1024]{2,1,0:T(8,128)(2,1)} %k_ref.5) | copy-start | bytes 1572868
  10.8 25.4 %copy-start.5 = (bf16[128,1024]{1,0:T(8,128)(2,1)S(1)}, bf16[128,1024]{1,0:T(8,128)(2,1)}, u32[]{:S(2)}) copy-start(bf16[128,1024]{1,0:T(8,128)(2,1)} %q_ref.3) | copy-start | bytes 786436
  10.8 25.4 %copy-start.7 = (f32[8,2,128]{2,1,0:T(2,128)S(1)}, f32[8,2,128]{2,1,0:T(2,128)}, u32[]{:S(2)}) copy-start(f32[8,2,128]{2,1,0:T(2,128)} %b_ref.5) | copy-start | bytes 24580
  30.2 1.0 copy-start.8
  31.2 1.0 copy-start.10
  32.2 1.0 copy-start.12
  33.1 19.0 %collective-permute-start = (bf16[4,128,256]{2,1,0:T(8,128)(2,1)S(1)}, bf16[4,128,256]{2,1,0:T(8,128)(2,1)S(1)}, u32[]{:S(2)}, u32[]{:S(2)}) collective-permute-start(bf16[4,128,256]{2,1,0:T(8,128)(2,1)S(1)} %get-tuple-element.31), channel_id=1, source_target_pairs={{0,4},{4,0},{8,12},{12,8},{16,20},{20,16},{24,28},{28,24},{32,36},... | collective-permute-start | bytes 786440 | tf_op jit(solution)/shard_map/ppermute | solution.py:350
  36.2 3.4 %copy-start = (bf16[1024,4096]{1,0:T(8,128)(2,1)S(1)}, bf16[1024,4096]{1,0:T(8,128)(2,1)}, u32[]{:S(2)}) copy-start(bf16[1024,4096]{1,0:T(8,128)(2,1)} %w_ref.1) | copy-start | bytes 25165828
  39.6 1.2 %copy-start.1 = (bf16[128,4096]{1,0:T(8,128)(2,1)S(1)}, bf16[128,4096]{1,0:T(8,128)(2,1)}, u32[]{:S(2)}) copy-start(bf16[128,4096]{1,0:T(8,128)(2,1)} %all-gather.2.cloned.1.call-done.og_ref) | copy-start | bytes 3145732
  40.8 45.5 %copy-start.9 = (bf16[8,256,256]{2,1,0:T(8,128)(2,1)S(1)}, bf16[8,256,256]{2,1,0:T(8,128)(2,1)}, u32[]{:S(2)}) copy-start(bf16[8,256,256]{2,1,0:T(8,128)(2,1)} %copy-done.8) | copy-start | bytes 3145732
  40.8 45.5 %copy-start.11 = (bf16[8,256,256]{2,1,0:T(8,128)(2,1)S(1)}, bf16[8,256,256]{2,1,0:T(8,128)(2,1)}, u32[]{:S(2)}) copy-start(bf16[8,256,256]{2,1,0:T(8,128)(2,1)} %copy-done.10) | copy-start | bytes 3145732
  40.8 45.5 %copy-start.13 = (f32[8,256,128]{2,1,0:T(8,128)S(1)}, f32[8,256,128]{2,1,0:T(8,128)}, u32[]{:S(2)}) copy-start(f32[8,256,128]{2,1,0:T(8,128)} %copy-done.12) | copy-start | bytes 3145732
  50.5 2.6 %collective-permute-start.1 = (bf16[4,128,128]{2,1,0:T(8,128)(2,1)S(1)}, bf16[4,128,128]{2,1,0:T(8,128)(2,1)S(1)}, u32[]{:S(2)}, u32[]{:S(2)}) collective-permute-start(bf16[4,128,128]{2,1,0:T(8,128)(2,1)S(1)} %get-tuple-element.33), channel_id=1, source_target_pairs={{0,4},{4,0},{8,12},{12,8},{16,20},{20,16},{24,28},{28,24},{32,36},... | collective-permute-start | bytes 393224 | tf_op jit(solution)/shard_map/ppermute | solution.py:350
  54.0 5.3 %collective-permute-start.2 = (bf16[128,384]{1,0:T(8,128)(2,1)S(1)}, bf16[128,384]{1,0:T(8,128)(2,1)S(1)}, u32[]{:S(2)}, u32[]{:S(2)}) collective-permute-start(bf16[128,384]{1,0:T(8,128)(2,1)S(1)} %get-tuple-element.35), channel_id=1, source_target_pairs={{0,8},{4,12},{8,16},{12,20},{16,24},{20,28},{24,0},{28,4},{32,40},... | collective-permute-start | bytes 294920 | tf_op jit(solution)/shard_map/ppermute | solution.py:350
  55.3 7.0 %collective-permute-start.3 = (bf16[128,384]{1,0:T(8,128)(2,1)S(1)}, bf16[128,384]{1,0:T(8,128)(2,1)S(1)}, u32[]{:S(2)}, u32[]{:S(2)}) collective-permute-start(bf16[128,384]{1,0:T(8,128)(2,1)S(1)} %get-tuple-element.36), channel_id=1, source_target_pairs={{0,16},{4,20},{8,24},{12,28},{16,0},{20,4},{24,8},{28,12},{32,48},... | collective-permute-start | bytes 294920 | tf_op jit(solution)/shard_map/ppermute | solution.py:350
  57.7 4.7 %collective-permute-start.4 = (bf16[128,384]{1,0:T(8,128)(2,1)S(1)}, bf16[128,384]{1,0:T(8,128)(2,1)S(1)}, u32[]{:S(2)}, u32[]{:S(2)}) collective-permute-start(bf16[128,384]{1,0:T(8,128)(2,1)S(1)} %get-tuple-element.37), channel_id=1, source_target_pairs={{0,24},{4,28},{8,0},{12,4},{16,8},{20,12},{24,16},{28,20},{32,56},... | collective-permute-start | bytes 294920 | tf_op jit(solution)/shard_map/ppermute | solution.py:350
  63.3 4.2 %collective-permute-start.7 = (bf16[128,384]{1,0:T(8,128)(2,1)S(1)}, bf16[128,384]{1,0:T(8,128)(2,1)S(1)}, u32[]{:S(2)}, u32[]{:S(2)}) collective-permute-start(bf16[128,384]{1,0:T(8,128)(2,1)S(1)} %line.1.e_ref), channel_id=1, source_target_pairs={{0,96},{4,100},{8,104},{12,108},{16,112},{20,116},{24,120},{28,124... | collective-permute-start | bytes 294920 | tf_op jit(solution)/shard_map/ppermute | solution.py:350
  65.8 5.0 %collective-permute-start.6 = (bf16[128,384]{1,0:T(8,128)(2,1)S(1)}, bf16[128,384]{1,0:T(8,128)(2,1)S(1)}, u32[]{:S(2)}, u32[]{:S(2)}) collective-permute-start(bf16[128,384]{1,0:T(8,128)(2,1)S(1)} %line.1.e_ref), channel_id=1, source_target_pairs={{0,64},{4,68},{8,72},{12,76},{16,80},{20,84},{24,88},{28,92},{32,9... | collective-permute-start | bytes 294920 | tf_op jit(solution)/shard_map/ppermute | solution.py:350
  66.4 5.8 %collective-permute-start.5 = (bf16[128,384]{1,0:T(8,128)(2,1)S(1)}, bf16[128,384]{1,0:T(8,128)(2,1)S(1)}, u32[]{:S(2)}, u32[]{:S(2)}) collective-permute-start(bf16[128,384]{1,0:T(8,128)(2,1)S(1)} %line.1.e_ref), channel_id=1, source_target_pairs={{0,32},{4,36},{8,40},{12,44},{16,48},{20,52},{24,56},{28,60},{32,6... | collective-permute-start | bytes 294920 | tf_op jit(solution)/shard_map/ppermute | solution.py:350
  73.8 4.4 %collective-permute-start.8 = (bf16[128,256]{1,0:T(8,128)(2,1)S(1)}, bf16[128,256]{1,0:T(8,128)(2,1)S(1)}, u32[]{:S(2)}, u32[]{:S(2)}) collective-permute-start(bf16[128,256]{1,0:T(8,128)(2,1)S(1)} %get-tuple-element.39), channel_id=1, source_target_pairs={{0,8},{4,12},{8,16},{12,20},{16,24},{20,28},{24,0},{28,4},{32,40},... | collective-permute-start | bytes 196616 | tf_op jit(solution)/shard_map/ppermute | solution.py:350
  74.2 4.7 %collective-permute-start.9 = (bf16[128,256]{1,0:T(8,128)(2,1)S(1)}, bf16[128,256]{1,0:T(8,128)(2,1)S(1)}, u32[]{:S(2)}, u32[]{:S(2)}) collective-permute-start(bf16[128,256]{1,0:T(8,128)(2,1)S(1)} %get-tuple-element.40), channel_id=1, source_target_pairs={{0,16},{4,20},{8,24},{12,28},{16,0},{20,4},{24,8},{28,12},{32,48},... | collective-permute-start | bytes 196616 | tf_op jit(solution)/shard_map/ppermute | solution.py:350
  76.2 3.3 %collective-permute-start.10 = (bf16[128,256]{1,0:T(8,128)(2,1)S(1)}, bf16[128,256]{1,0:T(8,128)(2,1)S(1)}, u32[]{:S(2)}, u32[]{:S(2)}) collective-permute-start(bf16[128,256]{1,0:T(8,128)(2,1)S(1)} %get-tuple-element.41), channel_id=1, source_target_pairs={{0,24},{4,28},{8,0},{12,4},{16,8},{20,12},{24,16},{28,20},{32,56},... | collective-permute-start | bytes 196616 | tf_op jit(solution)/shard_map/ppermute | solution.py:350
  80.3 6.0 %collective-permute-start.11 = (bf16[4,128,256]{2,1,0:T(8,128)(2,1)S(1)}, bf16[4,128,256]{2,1,0:T(8,128)(2,1)S(1)}, u32[]{:S(2)}, u32[]{:S(2)}) collective-permute-start(bf16[4,128,256]{2,1,0:T(8,128)(2,1)S(1)} %get-tuple-element.43), channel_id=1, source_target_pairs={{0,4},{4,0},{8,12},{12,8},{16,20},{20,16},{24,28},{28,24},{32,36},... | collective-permute-start | bytes 786440 | tf_op jit(solution)/shard_map/ppermute | solution.py:350
Sparse Core Ops, SparseCore 0:
  9.7 26.4 all-gather.1

commit v2 on v1

--- a/solution.py
+++ b/solution.py
@@ -9,7 +9,7 @@
 
 WIDTH = 128
 HALF = 4
-PER_STEP = 2
+PER_STEP = 4
 SCALE = WIDTH ** (-0.5)
 bf16 = jnp.bfloat16
 f32 = jnp.float32
@@ -69,13 +69,25 @@
     return lax.rsqrt(jnp.sum(wide * wide, axis=1, keepdims=True) + 1e-06)
 
 
-def pick(ref, head):
+def pick(ref, head, part):
     lanes = slice(head * WIDTH, (head + 1) * WIDTH)
-    return jnp.concatenate([ref[0, :, lanes], ref[1, :, lanes]], axis=0)
-
-
-def rate_row(ref, head):
-    return jnp.concatenate([ref[head, 0:1, :], ref[head, 1:2, :]], axis=1)
+    half = ref.shape[1] // 2
+    span = slice(part * half, (part + 1) * half)
+    return jnp.concatenate([ref[0, span, lanes], ref[1, span, lanes]], axis=0)
+
+
+def put(ref, head, part, value):
+    lanes = slice(head * WIDTH, (head + 1) * WIDTH)
+    half = ref.shape[1] // 2
+    span = slice(part * half, (part + 1) * half)
+    ref[0, span, lanes] = value[:half]
+    ref[1, span, lanes] = value[half:]
+
+
+def rate_row(ref, head, part):
+    half = ref.shape[2] // 2
+    span = slice(part * half, (part + 1) * half)
+    return jnp.concatenate([ref[head, 0:1, span], ref[head, 1:2, span]], axis=1)
 
 
 def maps_kernel(place, k_ref, v_ref, b_ref, send_ref, keep_ref, nh_ref, nl_ref, y_ref, z_ref, level_ref):
@@ -88,84 +100,118 @@
 
     diagonal = eye_mask(rows)
     heads = range(PER_STEP)
-    keys = [pick(k_ref, h) for h in heads]
-    values = [pick(v_ref, h) for h in heads]
-    rates = [rate_row(b_ref, h) for h in heads]
+    chains = [(h, part) for h in heads for part in range(2)]
+    every = range(len(chains))
+    keys = [pick(k_ref, h, part) for h, part in chains]
+    rates = [rate_row(b_ref, h, part) for h, part in chains]
     rate_cols = [column(r, diagonal) for r in rates]
     norms = [inverse_norms(k) for k in keys]
     grams = []
-    for h in heads:
-        raw = nt(keys[h], keys[h])
+    for i in every:
+        raw = nt(keys[i], keys[i])
         norm_row = lax.rsqrt(jnp.sum(jnp.where(diagonal, raw, 0.0), axis=0, keepdims=True) + 1e-06)
-        grams.append(jnp.where(level_ref[...] >= 0, raw * norms[h] * norm_row, 0.0))
-    systems = [grams[h] * rates[h] for h in heads]
+        grams.append(jnp.where(level_ref[...] >= 0, raw * norms[i] * norm_row, 0.0))
+    systems = [grams[i] * rates[i] for i in every]
     ident = jnp.where(diagonal, 1.0, 0.0).astype(f32)
-    inverse = [ident - jnp.where(level_ref[...] == 0, systems[h], 0.0) for h in heads]
+    inverse = [ident - jnp.where(level_ref[...] == 0, systems[i], 0.0) for i in every]
     for level in range(1, (rows - 1).bit_length()):
         rounded = [t.astype(bf16) for t in inverse]
         inner = [
-            nn(jnp.where(level_ref[...] == level, systems[h], 0.0).astype(bf16), rounded[h]).astype(bf16)
-            for h in heads
+            nn(jnp.where(level_ref[...] == level, systems[i], 0.0).astype(bf16), rounded[i]).astype(bf16)
+            for i in every
         ]
-        inverse = [inverse[h] - nn(rounded[h], inner[h]) for h in heads]
+        inverse = [inverse[i] - nn(rounded[i], inner[i]) for i in every]
     rounded = [t.astype(bf16) for t in inverse]
-    core_high = [nn(rounded[h], grams[h].astype(bf16)).astype(bf16) for h in heads]
+    core_high = [nn(rounded[i], grams[i].astype(bf16)).astype(bf16) for i in every]
     residual = []
+    for i in every:
+        high, low = split(systems[i])
+        residual.append(grams[i] - core_high[i].astype(f32) - nn(high, core_high[i]) - nn(low, core_high[i]))
+    core_low = [nn(rounded[i], residual[i].astype(bf16)).astype(bf16) for i in every]
+    for i, (h, part) in enumerate(chains):
+        nh_ref[h, part] = core_high[i]
+        nl_ref[h, part] = core_low[i]
+
+    mapped = [None for h in heads]
+    for part in range(2):
+        solved = []
+        for h in heads:
+            i = 2 * h + part
+            values = pick(v_ref, h, part)
+            both = jnp.concatenate([keys[i].astype(f32) * norms[i], values.astype(f32)], axis=1)
+            if part:
+                high, low = split(mapped[h])
+                both = both - norms[i] * (nn(keys[i], high) + nn(keys[i], low))
+            high, low = split(both * rate_cols[i])
+            solved.append(both - nn(core_high[i], high) - nn(core_low[i], high) - nn(core_high[i], low))
+        for h in heads:
+            i = 2 * h + part
+            span = slice(part * rows, (part + 1) * rows)
+            y_ref[h, span] = solved[h][:, :WIDTH]
+            z_ref[h, span] = solved[h][:, WIDTH:]
+            high, low = split(solved[h] * (rate_cols[i] * norms[i]))
+            found = tn(keys[i], high) + tn(keys[i], low)
+            mapped[h] = found if part == 0 else mapped[h] + found
+    place_halves(step, send_ref, keep_ref, [m.astype(bf16) for m in mapped])
+
+
+def place_halves(step, send_ref, keep_ref, values):
+    steps_half = HALF // PER_STEP
+
+    @pl.when(step < steps_half)
+    def _():
+        for h, value in enumerate(values):
+            send_ref[step * PER_STEP + h] = value
+
+    @pl.when(step >= steps_half)
+    def _():
+        for h, value in enumerate(values):
+            keep_ref[(step - steps_half) * PER_STEP + h] = value
+
+
+def local_grad_kernel(
+    place, o0, o1, o2, o3, w_ref, k_ref, q_ref, b_ref, y_ref, send_ref, keep_ref, do_ref, u_ref, og_ref
+):
+    step = pl.program_id(0)
+
+    @pl.when(step == 0)
+    def _():
+        part = o0.shape[0]
+        for shift, ref in enumerate((o0, o1, o2, o3)):
+            where = pl.multiple_of(lax.rem(place[3] + HALF - shift, HALF) * part, part)
+            og_ref[pl.ds(where, part), :] = ref[...]
+
+    heads = range(PER_STEP)
+    tokens = q_ref.shape[0]
+    half = tokens // 2
+    rows = 2 * half
+    diagonal = eye_mask(rows)
+    seen = order((rows, half), 0) < 2 * (iota((rows, half), 1) + 1)
+    all_grads = nt(og_ref[...], w_ref[...]).astype(bf16)
+    grads = [all_grads[:, h * WIDTH : (h + 1) * WIDTH] for h in heads]
+    queries = [q_ref[:, h * WIDTH : (h + 1) * WIDTH] for h in heads]
+    scaled = [[] for h in heads]
+    for part in range(2):
+        for h in heads:
+            keys = pick(k_ref, h, part)
+            score = nt(keys, queries[h]) * (inverse_norms(keys) * SCALE)
+            if part == 0:
+                score = jnp.concatenate([jnp.where(seen, score[:, :half], 0.0), score[:, half:]], axis=1)
+                high, low = split(score)
+                reached = nn(high, grads[h]) + nn(low, grads[h])
+            else:
+                high, low = split(jnp.where(seen, score[:, half:], 0.0))
+                reached = nn(high, grads[h][half:]) + nn(low, grads[h][half:])
+            u_ref[h, part * rows : (part + 1) * rows] = reached
+            scaled[h].append(reached * column(rate_row(b_ref, h, part), diagonal))
+    found = []
     for h in heads:
-        high, low = split(systems[h])
-        residual.append(grams[h] - core_high[h].astype(f32) - nn(high, core_high[h]) - nn(low, core_high[h]))
-    core_low = [nn(rounded[h], residual[h].astype(bf16)).astype(bf16) for h in heads]
-    for h in heads:
-        nh_ref[h] = core_high[h]
-        nl_ref[h] = core_low[h]
-    for h in heads:
-        both = jnp.concatenate([keys[h].astype(f32) * norms[h], values[h].astype(f32)], axis=1)
-        high, low = split(both * rate_cols[h])
-        solved = both - nn(core_high[h], high) - nn(core_low[h], high) - nn(core_high[h], low)
-        y_ref[h] = solved[:, :WIDTH]
-        z_ref[h] = solved[:, WIDTH:]
-        high, low = split(solved * (rate_cols[h] * norms[h]))
-        mapped = (tn(keys[h], high) + tn(keys[h], low)).astype(bf16)
-        steps_half = HALF // PER_STEP
-
-        @pl.when(step < steps_half)
-        def _():
-            send_ref[step * PER_STEP + h] = mapped
-
-        @pl.when(step >= steps_half)
-        def _():
-            keep_ref[(step - steps_half) * PER_STEP + h] = mapped
-
-
-def local_grad_kernel(place, og_ref, w_ref, k_ref, q_ref, b_ref, y_ref, send_ref, keep_ref, do_ref, u_ref):
-    step = pl.program_id(0)
-    steps_half = HALF // PER_STEP
-    tokens = q_ref.shape[0]
-    rows = 2 * tokens
-    diagonal = eye_mask(rows)
-    seen = order((rows, tokens), 0) < 2 * (iota((rows, tokens), 1) + 1)
-    for h in range(PER_STEP):
-        lanes = slice(h * WIDTH, (h + 1) * WIDTH)
-        grad = nt(og_ref[...], w_ref[lanes, :]).astype(bf16)
-        do_ref[h] = grad
-        keys = pick(k_ref, h)
-        query = q_ref[:, lanes]
-        rate_col = column(rate_row(b_ref, h), diagonal)
-        scores = jnp.where(seen, nt(keys, query) * (inverse_norms(keys) * SCALE), 0.0)
-        high, low = split(scores)
-        reached = nn(high, grad) + nn(low, grad)
-        u_ref[h] = reached
-        uh, ul = split(reached * rate_col)
+        do_ref[h] = grads[h]
+        uh, ul = split(jnp.concatenate(scaled[h], axis=0))
         yh, yl = split(y_ref[h])
-        local = (tn(query, grad) * SCALE - tn(yh, uh) - tn(yl, uh) - tn(yh, ul)).astype(bf16)
-
-        @pl.when(step < steps_half)
-        def _():
-            send_ref[step * PER_STEP + h] = local
-
-        @pl.when(step >= steps_half)
-        def _():
-            keep_ref[(step - steps_half) * PER_STEP + h] = local
+        local = tn(queries[h], grads[h]) * SCALE - tn(yh, uh) - tn(yl, uh) - tn(yh, ul)
+        found.append(local.astype(bf16))
+    place_halves(step, send_ref, keep_ref, found)
 
 
 def pair_kernel(place, keep_ref, got_ref, gkeep_ref, ggot_ref, *outs):
@@ -260,58 +306,101 @@
 ):
     step = pl.program_id(0)
     steps_half = HALF // PER_STEP
+    heads = range(PER_STEP)
+    parts = range(2)
+    both = [(h, p) for h in heads for p in parts]
     tokens = q_ref.shape[0]
-    rows = 2 * tokens
+    half = tokens // 2
+    rows = 2 * half
     diagonal = eye_mask(rows)
     before = order((rows, rows), 1) < order((rows, rows), 0)
-    seen = order((tokens, rows), 1) < 2 * (iota((tokens, rows), 0) + 1)
-    seen_t = order((rows, tokens), 0) < 2 * (iota((rows, tokens), 1) + 1)
-    for h in range(PER_STEP):
-        lanes = slice(h * WIDTH, (h + 1) * WIDTH)
+    seen = order((half, rows), 1) < 2 * (iota((half, rows), 0) + 1)
+    seen_t = order((rows, half), 0) < 2 * (iota((rows, half), 1) + 1)
+    spans = [slice(p * rows, (p + 1) * rows) for p in parts]
+
+    state, after = [], []
+    for h in heads:
         slot = lax.rem(step, steps_half) * PER_STEP + h
         ends = jnp.where(step < steps_half, got_ref[slot].astype(f32), own_ref[slot].astype(f32)).astype(bf16)
-        state, after = ends[:, :WIDTH], ends[:, WIDTH:]
-        keys = pick(k_ref, h)
-        query = q_ref[:, lanes]
-        grad = do_ref[h]
-        rate = column(rate_row(b_ref, h), diagonal)
-        norm = inverse_norms(keys)
-        yh, yl = split(y_ref[h])
-        errors = nn(yh, state) + nn(yl, state) - z_ref[h]
-        weighted = errors * rate
-        d_weighted = -u_ref[h] - norm * nn(keys, after)
-        high, low = split(d_weighted * rate)
-        back = d_weighted - tn(nh_ref[h], high) - tn(nl_ref[h], high) - tn(nh_ref[h], low)
-        scaled = back * rate
-        d_rate = jnp.sum(errors * back, axis=1, keepdims=True)
+        state.append(ends[:, :WIDTH])
+        after.append(ends[:, WIDTH:])
+    keys = {(h, p): pick(k_ref, h, p) for h, p in both}
+    rate = {(h, p): column(rate_row(b_ref, h, p), diagonal) for h, p in both}
+    norm = {c: inverse_norms(keys[c]) for c in both}
+    query = [q_ref[:, h * WIDTH : (h + 1) * WIDTH] for h in heads]
+
+    ahead = {(h, p): -u_ref[h, spans[p]] - norm[h, p] * nn(keys[h, p], after[h]) for h, p in both}
+    back = {}
+    for p in (1, 0):
+        if p == 0:
+            passed = {h: split(back[h, 1] * (rate[h, 1] * norm[h, 1])) for h in heads}
+            passed = {h: split(tn(keys[h, 1], passed[h][0]) + tn(keys[h, 1], passed[h][1])) for h in heads}
+            for h in heads:
+                ahead[h, 0] = ahead[h, 0] - norm[h, 0] * (nn(keys[h, 0], passed[h][0]) + nn(keys[h, 0], passed[h][1]))
+        pieces = {h: split(ahead[h, p] * rate[h, p]) for h in heads}
+        for h in heads:
+            high, low = pieces[h]
+            back[h, p] = ahead[h, p] - tn(nh_ref[h, p], high) - tn(nl_ref[h, p], high) - tn(nh_ref[h, p], low)
+    errors = {}
+    for h, p in both:
+        yh, yl = split(y_ref[h, spans[p]])
+        errors[h, p] = nn(yh, state[h]) + nn(yl, state[h]) - z_ref[h, spans[p]]
+    weighted = {c: errors[c] * rate[c] for c in both}
+    scaled = {c: back[c] * rate[c] for c in both}
+    for h, p in both:
+        d_rate = jnp.sum(errors[h, p] * back[h, p], axis=1, keepdims=True)
         d_rate = jnp.sum(jnp.where(diagonal, d_rate, 0.0), axis=0, keepdims=True)
-        db_ref[h, 0:1, :] = d_rate[:, :tokens]
-        db_ref[h, 1:2, :] = d_rate[:, tokens:]
-        dv_ref[0, :, lanes] = (-scaled[:tokens]).astype(bf16)
-        dv_ref[1, :, lanes] = (-scaled[tokens:]).astype(bf16)
-        wh, wl = split(weighted)
-        fh, fl = split(scaled)
-        wn = (weighted * norm).astype(bf16)
-        fn = (scaled * norm).astype(bf16)
-        d_scores = jnp.where(seen, -nt(grad, wn), 0.0).astype(bf16)
-        dq = nt(grad, state) + nn(d_scores, keys)
-        dq_ref[:, lanes] = (dq * SCALE).astype(bf16)
-        d_scores_t = jnp.where(seen_t, -nt(wh, grad), 0.0).astype(bf16)
-        lower = nt(jnp.concatenate([fh, fl], axis=1), jnp.concatenate([wn, wn], axis=1))
-        upper = nt(jnp.concatenate([wh, wl], axis=1), jnp.concatenate([fn, fn], axis=1))
-        pairs = jnp.where(before, lower, jnp.where(diagonal, 0.0, upper)).astype(bf16)
-        dk = nn(d_scores_t, query) * SCALE - nt(wh, after) + nt(fh, state) - nn(pairs, keys)
-        unit = keys.astype(f32) * norm
-        dk = norm * (dk - unit * jnp.sum(unit * dk, axis=1, keepdims=True))
-        dk_ref[0, :, lanes] = dk[:tokens].astype(bf16)
-        dk_ref[1, :, lanes] = dk[tokens:].astype(bf16)
+        db_ref[h, 0:1, p * half : (p + 1) * half] = d_rate[:, :half]
+        db_ref[h, 1:2, p * half : (p + 1) * half] = d_rate[:, half:]
+        put(dv_ref, h, p, (-scaled[h, p]).astype(bf16))
+    ws = {c: split(weighted[c]) for c in both}
+    fs = {c: split(scaled[c]) for c in both}
+    wn = [jnp.concatenate([(weighted[h, p] * norm[h, p]).astype(bf16) for p in parts], axis=0) for h in heads]
+    fn = [jnp.concatenate([(scaled[h, p] * norm[h, p]).astype(bf16) for p in parts], axis=0) for h in heads]
+    all_keys = [jnp.concatenate([keys[h, p] for p in parts], axis=0) for h in heads]
+
+    score = [nt(do_ref[h], wn[h]) for h in heads]
+    score_t = {(h, p): nt(ws[h, p][0], do_ref[h] if p == 0 else do_ref[h, half:]) for h, p in both}
+    lower, upper = {}, {}
+    for h, p in both:
+        first = jnp.concatenate(ws[h, p], axis=1)
+        second = jnp.concatenate(fs[h, p], axis=1)
+        wn2 = jnp.concatenate([wn[h], wn[h]], axis=1)
+        fn2 = jnp.concatenate([fn[h], fn[h]], axis=1)
+        upper[h, p] = nt(first, fn2 if p == 0 else fn2[rows:])
+        lower[h, p] = nt(second, wn2[:rows] if p == 0 else wn2)
+    pairs, reads = {}, {}
+    for h, p in both:
+        if p == 0:
+            own = jnp.where(before, lower[h, p], jnp.where(diagonal, 0.0, upper[h, p][:, :rows]))
+            pairs[h, p] = jnp.concatenate([own, upper[h, p][:, rows:]], axis=1).astype(bf16)
+            masked = jnp.concatenate(
+                [jnp.where(seen_t, score_t[h, p][:, :half], 0.0), score_t[h, p][:, half:]], axis=1
+            )
+            reads[h, p] = nn(masked.astype(bf16), query[h])
+        else:
+            own = jnp.where(before, lower[h, p][:, rows:], jnp.where(diagonal, 0.0, upper[h, p]))
+            pairs[h, p] = jnp.concatenate([lower[h, p][:, :rows], own], axis=1).astype(bf16)
+            reads[h, p] = nn(jnp.where(seen_t, score_t[h, p], 0.0).astype(bf16), query[h][half:])
+    for h in heads:
+        masked = jnp.concatenate([
+            jnp.concatenate([jnp.where(seen, score[h][:half, :rows], 0.0), jnp.zeros((half, rows), f32)], axis=1),
+            jnp.concatenate([score[h][half:, :rows], jnp.where(seen, score[h][half:, rows:], 0.0)], axis=1),
+        ], axis=0).astype(bf16)
+        dq = nt(do_ref[h], state[h]) - nn(masked, all_keys[h])
+        dq_ref[:, h * WIDTH : (h + 1) * WIDTH] = (dq * SCALE).astype(bf16)
+    for h, p in both:
+        dk = nt(fs[h, p][0], state[h]) - reads[h, p] * SCALE - nt(ws[h, p][0], after[h]) - nn(pairs[h, p], all_keys[h])
+        unit = keys[h, p].astype(f32) * norm[h, p]
+        dk = norm[h, p] * (dk - unit * jnp.sum(unit * dk, axis=1, keepdims=True))
+        put(dk_ref, h, p, dk.astype(bf16))
 
 
 def whole(shape):
     return pl.BlockSpec(shape, lambda *unused: (0,) * len(shape))
 
 
-def run(kernel, name, place, args, in_specs, outs, out_specs, grid=(1,), scratch=(), cost=None):
+def run(kernel, name, place, args, in_specs, outs, out_specs, grid=(1,), scratch=(), cost=None, vmem=56):
     return pl.pallas_call(
         kernel,
         name=name,
@@ -323,7 +412,7 @@
             scratch_shapes=list(scratch),
         ),
         out_shape=[jax.ShapeDtypeStruct(shape, dtype) for shape, dtype in outs],
-        compiler_params=pltpu.CompilerParams(vmem_limit_bytes=40 * 2**20),
+        compiler_params=pltpu.CompilerParams(vmem_limit_bytes=vmem * 2**20),
         cost_estimate=cost,
     )(place, *args)
 
@@ -335,6 +424,7 @@
         outs,
         [whole(shape) for shape, unused in outs],
         scratch=scratch,
+        vmem=16,
     )
 
 
@@ -343,8 +433,12 @@
     heads = queries.shape[1] // WIDTH
     rows = 2 * tokens
     model = out_weight.shape[1]
+    key_input, value_input, queries, out_weight, beta_rates = (
+        pltpu.with_memory_space_constraint(a, pltpu.HBM)
+        for a in (key_input, value_input, queries, out_weight, beta_rates)
+    )
     me = lax.axis_index("ctx")
-    place = jnp.stack([me % 2, (me // 2) % HALF, me // (2 * HALF)]).astype(jnp.int32)
+    place = jnp.stack([me % 2, (me // 2) % HALF, me // (2 * HALF), lax.axis_index("head")]).astype(jnp.int32)
 
     def move(value, target):
         return lax.ppermute(value, "ctx", [(i, target(i)) for i in range(32)])
@@ -369,31 +463,37 @@
     b_spec = pl.BlockSpec((PER_STEP, 2, tokens), lambda s, p: (block(s, p), 0, 0))
 
     def by_step(*shape):
-        return pl.BlockSpec((PER_STEP,) + shape, lambda s, p: (s, 0, 0))
-
-    gathered = lax.all_gather(out_grad, "head", axis=0, tiled=True)
+        return pl.BlockSpec((PER_STEP,) + shape, lambda s, p: (s,) + (0,) * len(shape))
+
+    gathered = [out_grad] + [
+        lax.ppermute(out_grad, "head", [(i, (i + by) % HALF) for i in range(HALF)]) for by in (1, 3, 2)
+    ]
+    gathered = [gathered[0], gathered[1], gathered[3], gathered[2]]
     send, keep, core_high, core_low, solved_k, solved_v = run(
         maps_kernel, "maps", place, (key_input, value_input, beta_rates),
         [kv_spec, kv_spec, b_spec],
-        [((HALF, WIDTH, 2 * WIDTH), bf16)] * 2 + [((heads, rows, rows), bf16)] * 2
+        [((HALF, WIDTH, 2 * WIDTH), bf16)] * 2 + [((heads, 2, tokens, tokens), bf16)] * 2
         + [((heads, rows, WIDTH), f32)] * 2,
-        [whole((HALF, WIDTH, 2 * WIDTH))] * 2 + [by_step(rows, rows)] * 2 + [by_step(rows, WIDTH)] * 2,
+        [whole((HALF, WIDTH, 2 * WIDTH))] * 2 + [by_step(2, tokens, tokens)] * 2 + [by_step(rows, WIDTH)] * 2,
         grid=(steps,),
-        scratch=[pltpu.VMEM((rows, rows), jnp.int32)],
+        scratch=[pltpu.VMEM((tokens, tokens), jnp.int32)],
+        vmem=24,
         cost=pl.CostEstimate(flops=14_000_000_000, transcendentals=0, bytes_accessed=8_000_000),
     )
     got = move(send, other_core)
     gsend, gkeep, grad, reached = run(
         local_grad_kernel, "local_grad", place,
-        (gathered, out_weight, key_input, queries, beta_rates, solved_k),
+        (*gathered, out_weight, key_input, queries, beta_rates, solved_k),
         [
-            whole((tokens, model)),
+            *[whole(out_grad.shape)] * HALF,
             pl.BlockSpec((PER_STEP * WIDTH, model), lambda s, p: (block(s, p), 0)),
             kv_spec, q_spec, b_spec, by_step(rows, WIDTH),
         ],
         [((HALF, WIDTH, WIDTH), bf16)] * 2 + [((heads, tokens, WIDTH), bf16), ((heads, rows, WIDTH), f32)],
         [whole((HALF, WIDTH, WIDTH))] * 2 + [by_step(tokens, WIDTH), by_step(rows, WIDTH)],
         grid=(steps,),
+        scratch=[pltpu.VMEM((tokens, model), bf16)],
+        vmem=32,
         cost=pl.CostEstimate(flops=4_000_000_000, transcendentals=0, bytes_accessed=14_000_000),
     )
     ggot = move(gsend, other_core)
@@ -416,7 +516,7 @@
         grads_kernel, "grads", place,
         (key_input, queries, beta_rates, grad, core_high, core_low, solved_k, solved_v, reached, own, taken),
         [
-            kv_spec, q_spec, b_spec, by_step(tokens, WIDTH), by_step(rows, rows), by_step(rows, rows),
+            kv_spec, q_spec, b_spec, by_step(tokens, WIDTH), by_step(2, tokens, tokens), by_step(2, tokens, tokens),
             by_step(rows, WIDTH), by_step(rows, WIDTH), by_step(rows, WIDTH),
             whole((HALF, WIDTH, 2 * WIDTH)), whole((HALF, WIDTH, 2 * WIDTH)),
         ],
@@ -425,6 +525,7 @@
         ],
         [q_spec, kv_spec, kv_spec, b_spec],
         grid=(steps,),
+        vmem=24,
         cost=pl.CostEstimate(flops=8_000_000_000, transcendentals=0, bytes_accessed=14_000_000),
     ))
 

time: 102 us -> 70.9 us (0.70)
  between operations: 14.1 us -> 0.7 us
  Pallas kernels: 41.4 us -> 30.6 us
  local copies, waits for them, and re-layouts: 10.3 us -> 0.01 us
  starting transfers between devices: 20.1 us -> 23.7 us
    pallas_call x7, Pallas kernels: 41.4 us -> 30.6 us  [run(): pl.pallas_call(kernel, name=name, grid_spec=pltpu.PrefetchScalarGridSpec(...]
    unnamed x28 -> x2, local copies, waits for them, and re-layouts: 10.3 us -> 0.01 us
    ppermute x0 -> x3, starting transfers between devices: none -> 7.18 us  [shards(): lax.ppermute(out_grad, 'head', [(i, (i + by) % HALF) for i in range(HALF)])]
    ppermute x12, starting transfers between devices: 20 us -> 16.6 us  [move(): return lax.ppermute(value, 'ctx', [(i, target(i)) for i in range(32)])]
    ppermute x12, waiting for transfers between devices: 13 us -> 15.6 us  [move(): return lax.ppermute(value, 'ctx', [(i, target(i)) for i in range(32)])]
    all_gather x1 -> x0, waiting for transfers between devices: 1.65 us -> none  [shards(): gathered = lax.all_gather(out_grad, 'head', axis=0, tiled=True)]
  transfers between devices with their start and end apart: 13 -> 15, of which waited for: 11 -> 9; matrix products, arithmetic and copies ran while one was open for 0% -> 0% of each run, Pallas kernels for 29% -> 26%
where the time goes in v2:
time: 70.9 us; the launch traced here: 70.8 us
  Pallas kernels  30.6 us (43%)
  starting transfers between devices  23.7 us (33%)
  waiting for transfers between devices  15.6 us (22%)
    pallas_call x7, Pallas kernels, run(): pl.pallas_call(kernel, name=name, grid_spec=pltpu.PrefetchScalarGridSpec(...  30.6 us
    ppermute x12, starting transfers between devices, move(): return lax.ppermute(value, 'ctx', [(i, target(i)) for i in range(32)])  16.6 us
    ppermute x12, waiting for transfers between devices, move(): return lax.ppermute(value, 'ctx', [(i, target(i)) for i in range(32)])  15.6 us
    ppermute x3, starting transfers between devices, shards(): lax.ppermute(out_grad, 'head', [(i, (i + by) % HALF) for i in range(HALF)])  7.18 us
  transfers between devices with their start and end apart: 15, of which 9 were waited for; matrix products, arithmetic and copies ran while one was open for 0% of the time, Pallas kernels for 26%

profile of v2, /device:TPU:1, one launch (start us, length us, event | category | flops | bytes accessed | tf_op | source)
XLA Modules:
  0.0 70.8 jit_solution(11097471537388339149)
XLA Ops:
  0.6 4.5 %collective-permute-start.1 = (bf16[32,4096]{1,0:T(8,128)(2,1)}, bf16[32,4096]{1,0:T(8,128)(2,1)S(1)}, u32[]{:S(2)}, u32[]{:S(2)}) collective-permute-start(bf16[32,4096]{1,0:T(8,128)(2,1)} %o0.1), channel_id=1, source_target_pairs={{0,2},{1,3},{2,0},{3,1},{4,6},{5,7},{6,4},{7,5},{8,10},{9,11},{10,... | collective-permute-start | bytes 786440 | tf_op jit(solution)/shard_map/ppermute | solution.py:469
  5.1 0.7 %collective-permute-start = (bf16[32,4096]{1,0:T(8,128)(2,1)}, bf16[32,4096]{1,0:T(8,128)(2,1)S(1)}, u32[]{:S(2)}, u32[]{:S(2)}) collective-permute-start(bf16[32,4096]{1,0:T(8,128)(2,1)} %o0.1), channel_id=1, source_target_pairs={{0,1},{1,2},{2,3},{3,0},{4,5},{5,6},{6,7},{7,4},{8,9},{9,10},{10,1... | collective-permute-start | bytes 786440 | tf_op jit(solution)/shard_map/ppermute | solution.py:469
  5.9 1.9 %collective-permute-start.2 = (bf16[32,4096]{1,0:T(8,128)(2,1)}, bf16[32,4096]{1,0:T(8,128)(2,1)S(1)}, u32[]{:S(2)}, u32[]{:S(2)}) collective-permute-start(bf16[32,4096]{1,0:T(8,128)(2,1)} %o0.1), channel_id=1, source_target_pairs={{0,3},{1,0},{2,1},{3,2},{4,7},{5,4},{6,5},{7,6},{8,11},{9,8},{10,9... | collective-permute-start | bytes 786440 | tf_op jit(solution)/shard_map/ppermute | solution.py:469
  7.8 0.1 pad_add_fusion.place
  7.9 0.0 copy-start
  7.9 10.8 %maps.1 = (bf16[4,128,256]{2,1,0:T(8,128)(2,1)S(1)}, bf16[4,128,256]{2,1,0:T(8,128)(2,1)S(1)}, bf16[8,2,128,128]{3,2,1,0:T(8,128)(2,1)S(1)}, bf16[8,2,128,128]{3...) custom-call(s32[4]{0:T(128)S(1)} %pad_add_fusion.place, bf16[2,128,1024]{2,1,0:T(8,128)(2,1)} %k_ref.5, ...), custom_call_target="tpu_custom_call" | custom-call | flops 14000000000 | bytes 8000000 | tf_op jit(solution)/shard_map/maps/pallas_call | solution.py:404
  18.7 1.6 %collective-permute-start.3 = (bf16[4,128,256]{2,1,0:T(8,128)(2,1)S(1)}, bf16[4,128,256]{2,1,0:T(8,128)(2,1)S(1)}, u32[]{:S(2)}, u32[]{:S(2)}) collective-permute-start(bf16[4,128,256]{2,1,0:T(8,128)(2,1)S(1)} %get-tuple-element.31), channel_id=1, source_target_pairs={{0,4},{4,0},{8,12},{12,8},{16,20},{20,16},{24,28},{28,24},{32,36},... | collective-permute-start | bytes 786440 | tf_op jit(solution)/shard_map/ppermute | solution.py:444
  20.2 0.0 collective-permute-done.1.o2
  20.3 0.0 collective-permute-done.o1
  20.3 0.0 collective-permute-done.2.o3
  20.3 0.0 copy-done
  20.3 7.9 %local_grad.1 = (bf16[4,128,128]{2,1,0:T(8,128)(2,1)S(1)}, bf16[4,128,128]{2,1,0:T(8,128)(2,1)S(1)}, bf16[8,128,128]{2,1,0:T(8,128)(2,1)S(1)}, f32[8,256,128]{2,1,0:T(8,128)S(1)}) custom-call(s32[4]{0:T(128)S(1)} %pad_add_fusion.place, bf16[32,4096]{1,0:T(8,128)(2,1)S(1)} %copy-done, bf16[32,4096]{1,0:T(8,128)(2,1)S(1)} %collective-permute-done.o1, ...), custom_call_target="tpu_custom_call" | custom-call | flops 4000000000 | bytes 14000000 | tf_op jit(solution)/shard_map/local_grad/pallas_call | solution.py:404
  28.1 0.1 collective-permute-start.4
  28.3 0.0 collective-permute-done.3.got_ref
  28.3 1.3 %collective-permute-done.4.ggot_ref = bf16[4,128,128]{2,1,0:T(8,128)(2,1)S(1)} collective-permute-done((bf16[4,128,128]{2,1,0:T(8,128)(2,1)S(1)}, bf16[4,128,128]{2,1,0:T(8,128)(2,1)S(1)}, u32[]{:S(2)}, u32[]{:S(2)}) %collective-permute-start.4) | collective-permute-done | bytes 131104 | tf_op jit(solution)/shard_map/ppermute | solution.py:444
  29.6 0.9 %pair.1 = (bf16[128,384]{1,0:T(8,128)(2,1)S(1)}, bf16[128,384]{1,0:T(8,128)(2,1)S(1)}, bf16[128,384]{1,0:T(8,128)(2,1)S(1)}, bf16[128,384]{1,0:T(8,128)(2,1)S(1)}) custom-call(s32[4]{0:T(128)S(1)} %pad_add_fusion.place, bf16[4,128,256]{2,1,0:T(8,128)(2,1)S(1)} %get-tuple-element.30.keep_ref, bf16[4,128,256]{2,1,0:T(8,128)(2,1)S(1)} %collective-permute-done.3.got_ref, ...), custom_call_target="tpu_custom_call" | custom-call | tf_op jit(solution)/shard_map/pair/pallas_call | solution.py:404
  30.4 1.3 %collective-permute-start.5 = (bf16[128,384]{1,0:T(8,128)(2,1)S(1)}, bf16[128,384]{1,0:T(8,128)(2,1)S(1)}, u32[]{:S(2)}, u32[]{:S(2)}) collective-permute-start(bf16[128,384]{1,0:T(8,128)(2,1)S(1)} %get-tuple-element.35), channel_id=1, source_target_pairs={{0,8},{4,12},{8,16},{12,20},{16,24},{20,28},{24,0},{28,4},{32,40},... | collective-permute-start | bytes 294920 | tf_op jit(solution)/shard_map/ppermute | solution.py:444
  31.7 2.5 %collective-permute-start.6 = (bf16[128,384]{1,0:T(8,128)(2,1)S(1)}, bf16[128,384]{1,0:T(8,128)(2,1)S(1)}, u32[]{:S(2)}, u32[]{:S(2)}) collective-permute-start(bf16[128,384]{1,0:T(8,128)(2,1)S(1)} %get-tuple-element.36), channel_id=1, source_target_pairs={{0,16},{4,20},{8,24},{12,28},{16,0},{20,4},{24,8},{28,12},{32,48},... | collective-permute-start | bytes 294920 | tf_op jit(solution)/shard_map/ppermute | solution.py:444
  34.2 1.1 %collective-permute-start.7 = (bf16[128,384]{1,0:T(8,128)(2,1)S(1)}, bf16[128,384]{1,0:T(8,128)(2,1)S(1)}, u32[]{:S(2)}, u32[]{:S(2)}) collective-permute-start(bf16[128,384]{1,0:T(8,128)(2,1)S(1)} %get-tuple-element.37), channel_id=1, source_target_pairs={{0,24},{4,28},{8,0},{12,4},{16,8},{20,12},{24,16},{28,20},{32,56},... | collective-permute-start | bytes 294920 | tf_op jit(solution)/shard_map/ppermute | solution.py:444
  35.3 0.6 collective-permute-done.5.b_ref
  36.0 3.1 %collective-permute-done.6.c_ref = bf16[128,384]{1,0:T(8,128)(2,1)S(1)} collective-permute-done((bf16[128,384]{1,0:T(8,128)(2,1)S(1)}, bf16[128,384]{1,0:T(8,128)(2,1)S(1)}, u32[]{:S(2)}, u32[]{:S(2)}) %collective-permute-start.6) | collective-permute-done | bytes 98336 | tf_op jit(solution)/shard_map/ppermute | solution.py:444
  39.0 0.0 collective-permute-done.7.d_ref
  39.1 0.9 %line.1.e_ref = bf16[128,384]{1,0:T(8,128)(2,1)S(1)} custom-call(s32[4]{0:T(128)S(1)} %pad_add_fusion.place, bf16[128,384]{1,0:T(8,128)(2,1)S(1)} %get-tuple-element.34.a_ref, bf16[128,384]{1,0:T(8,128)(2,1)S(1)} %collective-permute-done.5.b_ref, bf16[128,384]{1,0:T(8,128)(2,1)S(1)} %collective-permute-done.6.c_ref, ...), custom_call_target="tpu_custom_call" | custom-call | tf_op jit(solution)/shard_map/line/pallas_call | solution.py:404
  40.0 2.8 %collective-permute-start.10 = (bf16[128,384]{1,0:T(8,128)(2,1)S(1)}, bf16[128,384]{1,0:T(8,128)(2,1)S(1)}, u32[]{:S(2)}, u32[]{:S(2)}) collective-permute-start(bf16[128,384]{1,0:T(8,128)(2,1)S(1)} %line.1.e_ref), channel_id=1, source_target_pairs={{0,96},{4,100},{8,104},{12,108},{16,112},{20,116},{24,120},{28,124... | collective-permute-start | bytes 294920 | tf_op jit(solution)/shard_map/ppermute | solution.py:444
  42.8 0.4 collective-permute-start.9
  43.1 0.7 collective-permute-start.8
  43.8 0.6 collective-permute-done.10.h_ref
  44.4 3.4 %collective-permute-done.9.g_ref = bf16[128,384]{1,0:T(8,128)(2,1)S(1)} collective-permute-done((bf16[128,384]{1,0:T(8,128)(2,1)S(1)}, bf16[128,384]{1,0:T(8,128)(2,1)S(1)}, u32[]{:S(2)}, u32[]{:S(2)}) %collective-permute-start.9) | collective-permute-done | bytes 98336 | tf_op jit(solution)/shard_map/ppermute | solution.py:444
  47.9 2.4 %collective-permute-done.8.f_ref = bf16[128,384]{1,0:T(8,128)(2,1)S(1)} collective-permute-done((bf16[128,384]{1,0:T(8,128)(2,1)S(1)}, bf16[128,384]{1,0:T(8,128)(2,1)S(1)}, u32[]{:S(2)}, u32[]{:S(2)}) %collective-permute-start.8) | collective-permute-done | bytes 98336 | tf_op jit(solution)/shard_map/ppermute | solution.py:444
  50.3 1.6 %expand.1 = (bf16[128,256]{1,0:T(8,128)(2,1)S(1)}, bf16[128,256]{1,0:T(8,128)(2,1)S(1)}, bf16[128,256]{1,0:T(8,128)(2,1)S(1)}, bf16[128,256]{1,0:T(8,128)(2,1)S(1)}) custom-call(s32[4]{0:T(128)S(1)} %pad_add_fusion.place, bf16[128,384]{1,0:T(8,128)(2,1)S(1)} %get-tuple-element.34.a_ref, bf16[128,384]{1,0:T(8,128)(2,1)S(1)} %collective-permute-done.5.b_ref, ...), custom_call_target="tpu_custom_call" | custom-call | tf_op jit(solution)/shard_map/expand/pallas_call | solution.py:404
  51.9 0.1 collective-permute-start.11
  52.0 1.3 %collective-permute-start.12 = (bf16[128,256]{1,0:T(8,128)(2,1)S(1)}, bf16[128,256]{1,0:T(8,128)(2,1)S(1)}, u32[]{:S(2)}, u32[]{:S(2)}) collective-permute-start(bf16[128,256]{1,0:T(8,128)(2,1)S(1)} %get-tuple-element.40), channel_id=1, source_target_pairs={{0,16},{4,20},{8,24},{12,28},{16,0},{20,4},{24,8},{28,12},{32,48},... | collective-permute-start | bytes 196616 | tf_op jit(solution)/shard_map/ppermute | solution.py:444
  53.3 1.6 %collective-permute-start.13 = (bf16[128,256]{1,0:T(8,128)(2,1)S(1)}, bf16[128,256]{1,0:T(8,128)(2,1)S(1)}, u32[]{:S(2)}, u32[]{:S(2)}) collective-permute-start(bf16[128,256]{1,0:T(8,128)(2,1)S(1)} %get-tuple-element.41), channel_id=1, source_target_pairs={{0,24},{4,28},{8,0},{12,4},{16,8},{20,12},{24,16},{28,20},{32,56},... | collective-permute-start | bytes 196616 | tf_op jit(solution)/shard_map/ppermute | solution.py:444
  54.9 2.1 %collective-permute-done.11.b_ref = bf16[128,256]{1,0:T(8,128)(2,1)S(1)} collective-permute-done((bf16[128,256]{1,0:T(8,128)(2,1)S(1)}, bf16[128,256]{1,0:T(8,128)(2,1)S(1)}, u32[]{:S(2)}, u32[]{:S(2)}) %collective-permute-start.11) | collective-permute-done | bytes 65568 | tf_op jit(solution)/shard_map/ppermute | solution.py:444
  57.0 0.0 collective-permute-done.12.c_ref
  57.0 0.9 %collective-permute-done.13.d_ref = bf16[128,256]{1,0:T(8,128)(2,1)S(1)} collective-permute-done((bf16[128,256]{1,0:T(8,128)(2,1)S(1)}, bf16[128,256]{1,0:T(8,128)(2,1)S(1)}, u32[]{:S(2)}, u32[]{:S(2)}) %collective-permute-start.13) | collective-permute-done | bytes 65568 | tf_op jit(solution)/shard_map/ppermute | solution.py:444
  57.8 0.8 %down.1 = (bf16[4,128,256]{2,1,0:T(8,128)(2,1)S(1)}, bf16[4,128,256]{2,1,0:T(8,128)(2,1)S(1)}) custom-call(s32[4]{0:T(128)S(1)} %pad_add_fusion.place, bf16[128,256]{1,0:T(8,128)(2,1)S(1)} %get-tuple-element.38.a_ref, bf16[128,256]{1,0:T(8,128)(2,1)S(1)} %collective-permute-done.11.b_ref, bf16[128,256]{1,0:T(8,128)(2,1)S(1)} %collective-permute-done.12.c_ref, ...), custom_call_target="tpu_custom_call" | custom-call | tf_op jit(solution)/shard_map/down/pallas_call | solution.py:404
  58.7 3.1 %collective-permute-start.14 = (bf16[4,128,256]{2,1,0:T(8,128)(2,1)S(1)}, bf16[4,128,256]{2,1,0:T(8,128)(2,1)S(1)}, u32[]{:S(2)}, u32[]{:S(2)}) collective-permute-start(bf16[4,128,256]{2,1,0:T(8,128)(2,1)S(1)} %get-tuple-element.43), channel_id=1, source_target_pairs={{0,4},{4,0},{8,12},{12,8},{16,20},{20,16},{24,28},{28,24},{32,36},... | collective-permute-start | bytes 786440 | tf_op jit(solution)/shard_map/ppermute | solution.py:444
  61.8 1.2 %collective-permute-done.14.got_ref = bf16[4,128,256]{2,1,0:T(8,128)(2,1)S(1)} collective-permute-done((bf16[4,128,256]{2,1,0:T(8,128)(2,1)S(1)}, bf16[4,128,256]{2,1,0:T(8,128)(2,1)S(1)}, u32[]{:S(2)}, u32[]{:S(2)}) %collective-permute-start.14) | collective-permute-done | bytes 262176 | tf_op jit(solution)/shard_map/ppermute | solution.py:444
  63.0 7.8 %grads.1 = (bf16[128,1024]{1,0:T(8,128)(2,1)}, bf16[2,128,1024]{2,1,0:T(8,128)(2,1)}, bf16[2,128,1024]{2,1,0:T(8,128)(2,1)}, f32[8,2,128]{2,1,0:T(2,128)}) custom-call(s32[4]{0:T(128)S(1)} %pad_add_fusion.place, bf16[2,128,1024]{2,1,0:T(8,128)(2,1)} %k_ref.5, bf16[128,1024]{1,0:T(8,128)(2,1)} %q_ref.3, f32[8,2,128]{2,1,0:T(2,128)} %b_ref.5, ...), custom_call_target="tpu_custom_call" | custom-call | flops 8000000000 | bytes 14000000 | tf_op jit(solution)/shard_map/grads/pallas_call | solution.py:404
Async XLA Ops:
  0.6 19.6 %collective-permute-start.1 = (bf16[32,4096]{1,0:T(8,128)(2,1)}, bf16[32,4096]{1,0:T(8,128)(2,1)S(1)}, u32[]{:S(2)}, u32[]{:S(2)}) collective-permute-start(bf16[32,4096]{1,0:T(8,128)(2,1)} %o0.1), channel_id=1, source_target_pairs={{0,2},{1,3},{2,0},{3,1},{4,6},{5,7},{6,4},{7,5},{8,10},{9,11},{10,... | collective-permute-start | bytes 786440 | tf_op jit(solution)/shard_map/ppermute | solution.py:469
  5.1 15.1 %collective-permute-start = (bf16[32,4096]{1,0:T(8,128)(2,1)}, bf16[32,4096]{1,0:T(8,128)(2,1)S(1)}, u32[]{:S(2)}, u32[]{:S(2)}) collective-permute-start(bf16[32,4096]{1,0:T(8,128)(2,1)} %o0.1), channel_id=1, source_target_pairs={{0,1},{1,2},{2,3},{3,0},{4,5},{5,6},{6,7},{7,4},{8,9},{9,10},{10,1... | collective-permute-start | bytes 786440 | tf_op jit(solution)/shard_map/ppermute | solution.py:469
  5.9 14.4 %collective-permute-start.2 = (bf16[32,4096]{1,0:T(8,128)(2,1)}, bf16[32,4096]{1,0:T(8,128)(2,1)S(1)}, u32[]{:S(2)}, u32[]{:S(2)}) collective-permute-start(bf16[32,4096]{1,0:T(8,128)(2,1)} %o0.1), channel_id=1, source_target_pairs={{0,3},{1,0},{2,1},{3,2},{4,7},{5,4},{6,5},{7,6},{8,11},{9,8},{10,9... | collective-permute-start | bytes 786440 | tf_op jit(solution)/shard_map/ppermute | solution.py:469
  7.9 12.4 %copy-start = (bf16[32,4096]{1,0:T(8,128)(2,1)S(1)}, bf16[32,4096]{1,0:T(8,128)(2,1)}, u32[]{:S(2)}) copy-start(bf16[32,4096]{1,0:T(8,128)(2,1)} %o0.1) | copy-start | bytes 786436
  18.7 9.6 %collective-permute-start.3 = (bf16[4,128,256]{2,1,0:T(8,128)(2,1)S(1)}, bf16[4,128,256]{2,1,0:T(8,128)(2,1)S(1)}, u32[]{:S(2)}, u32[]{:S(2)}) collective-permute-start(bf16[4,128,256]{2,1,0:T(8,128)(2,1)S(1)} %get-tuple-element.31), channel_id=1, source_target_pairs={{0,4},{4,0},{8,12},{12,8},{16,20},{20,16},{24,28},{28,24},{32,36},... | collective-permute-start | bytes 786440 | tf_op jit(solution)/shard_map/ppermute | solution.py:444
  28.1 1.4 %collective-permute-start.4 = (bf16[4,128,128]{2,1,0:T(8,128)(2,1)S(1)}, bf16[4,128,128]{2,1,0:T(8,128)(2,1)S(1)}, u32[]{:S(2)}, u32[]{:S(2)}) collective-permute-start(bf16[4,128,128]{2,1,0:T(8,128)(2,1)S(1)} %get-tuple-element.33), channel_id=1, source_target_pairs={{0,4},{4,0},{8,12},{12,8},{16,20},{20,16},{24,28},{28,24},{32,36},... | collective-permute-start | bytes 393224 | tf_op jit(solution)/shard_map/ppermute | solution.py:444
  30.4 5.5 %collective-permute-start.5 = (bf16[128,384]{1,0:T(8,128)(2,1)S(1)}, bf16[128,384]{1,0:T(8,128)(2,1)S(1)}, u32[]{:S(2)}, u32[]{:S(2)}) collective-permute-start(bf16[128,384]{1,0:T(8,128)(2,1)S(1)} %get-tuple-element.35), channel_id=1, source_target_pairs={{0,8},{4,12},{8,16},{12,20},{16,24},{20,28},{24,0},{28,4},{32,40},... | collective-permute-start | bytes 294920 | tf_op jit(solution)/shard_map/ppermute | solution.py:444
  31.7 7.3 %collective-permute-start.6 = (bf16[128,384]{1,0:T(8,128)(2,1)S(1)}, bf16[128,384]{1,0:T(8,128)(2,1)S(1)}, u32[]{:S(2)}, u32[]{:S(2)}) collective-permute-start(bf16[128,384]{1,0:T(8,128)(2,1)S(1)} %get-tuple-element.36), channel_id=1, source_target_pairs={{0,16},{4,20},{8,24},{12,28},{16,0},{20,4},{24,8},{28,12},{32,48},... | collective-permute-start | bytes 294920 | tf_op jit(solution)/shard_map/ppermute | solution.py:444
  34.2 4.9 %collective-permute-start.7 = (bf16[128,384]{1,0:T(8,128)(2,1)S(1)}, bf16[128,384]{1,0:T(8,128)(2,1)S(1)}, u32[]{:S(2)}, u32[]{:S(2)}) collective-permute-start(bf16[128,384]{1,0:T(8,128)(2,1)S(1)} %get-tuple-element.37), channel_id=1, source_target_pairs={{0,24},{4,28},{8,0},{12,4},{16,8},{20,12},{24,16},{28,20},{32,56},... | collective-permute-start | bytes 294920 | tf_op jit(solution)/shard_map/ppermute | solution.py:444
  40.0 4.4 %collective-permute-start.10 = (bf16[128,384]{1,0:T(8,128)(2,1)S(1)}, bf16[128,384]{1,0:T(8,128)(2,1)S(1)}, u32[]{:S(2)}, u32[]{:S(2)}) collective-permute-start(bf16[128,384]{1,0:T(8,128)(2,1)S(1)} %line.1.e_ref), channel_id=1, source_target_pairs={{0,96},{4,100},{8,104},{12,108},{16,112},{20,116},{24,120},{28,124... | collective-permute-start | bytes 294920 | tf_op jit(solution)/shard_map/ppermute | solution.py:444
  42.8 5.1 %collective-permute-start.9 = (bf16[128,384]{1,0:T(8,128)(2,1)S(1)}, bf16[128,384]{1,0:T(8,128)(2,1)S(1)}, u32[]{:S(2)}, u32[]{:S(2)}) collective-permute-start(bf16[128,384]{1,0:T(8,128)(2,1)S(1)} %line.1.e_ref), channel_id=1, source_target_pairs={{0,64},{4,68},{8,72},{12,76},{16,80},{20,84},{24,88},{28,92},{32,9... | collective-permute-start | bytes 294920 | tf_op jit(solution)/shard_map/ppermute | solution.py:444
  43.1 7.1 %collective-permute-start.8 = (bf16[128,384]{1,0:T(8,128)(2,1)S(1)}, bf16[128,384]{1,0:T(8,128)(2,1)S(1)}, u32[]{:S(2)}, u32[]{:S(2)}) collective-permute-start(bf16[128,384]{1,0:T(8,128)(2,1)S(1)} %line.1.e_ref), channel_id=1, source_target_pairs={{0,32},{4,36},{8,40},{12,44},{16,48},{20,52},{24,56},{28,60},{32,6... | collective-permute-start | bytes 294920 | tf_op jit(solution)/shard_map/ppermute | solution.py:444
  51.9 5.1 %collective-permute-start.11 = (bf16[128,256]{1,0:T(8,128)(2,1)S(1)}, bf16[128,256]{1,0:T(8,128)(2,1)S(1)}, u32[]{:S(2)}, u32[]{:S(2)}) collective-permute-start(bf16[128,256]{1,0:T(8,128)(2,1)S(1)} %get-tuple-element.39), channel_id=1, source_target_pairs={{0,8},{4,12},{8,16},{12,20},{16,24},{20,28},{24,0},{28,4},{32,40},... | collective-permute-start | bytes 196616 | tf_op jit(solution)/shard_map/ppermute | solution.py:444
  52.0 5.0 %collective-permute-start.12 = (bf16[128,256]{1,0:T(8,128)(2,1)S(1)}, bf16[128,256]{1,0:T(8,128)(2,1)S(1)}, u32[]{:S(2)}, u32[]{:S(2)}) collective-permute-start(bf16[128,256]{1,0:T(8,128)(2,1)S(1)} %get-tuple-element.40), channel_id=1, source_target_pairs={{0,16},{4,20},{8,24},{12,28},{16,0},{20,4},{24,8},{28,12},{32,48},... | collective-permute-start | bytes 196616 | tf_op jit(solution)/shard_map/ppermute | solution.py:444
  53.3 4.6 %collective-permute-start.13 = (bf16[128,256]{1,0:T(8,128)(2,1)S(1)}, bf16[128,256]{1,0:T(8,128)(2,1)S(1)}, u32[]{:S(2)}, u32[]{:S(2)}) collective-permute-start(bf16[128,256]{1,0:T(8,128)(2,1)S(1)} %get-tuple-element.41), channel_id=1, source_target_pairs={{0,24},{4,28},{8,0},{12,4},{16,8},{20,12},{24,16},{28,20},{32,56},... | collective-permute-start | bytes 196616 | tf_op jit(solution)/shard_map/ppermute | solution.py:444
  58.7 4.3 %collective-permute-start.14 = (bf16[4,128,256]{2,1,0:T(8,128)(2,1)S(1)}, bf16[4,128,256]{2,1,0:T(8,128)(2,1)S(1)}, u32[]{:S(2)}, u32[]{:S(2)}) collective-permute-start(bf16[4,128,256]{2,1,0:T(8,128)(2,1)S(1)} %get-tuple-element.43), channel_id=1, source_target_pairs={{0,4},{4,0},{8,12},{12,8},{16,20},{20,16},{24,28},{28,24},{32,36},... | collective-permute-start | bytes 786440 | tf_op jit(solution)/shard_map/ppermute | solution.py:444

commit v3 on v2

v3 whole, which is shorter than its diff:
```python
import functools

import jax
import jax.numpy as jnp
from jax import lax
from jax.experimental import pallas as pl
from jax.experimental.pallas import tpu as pltpu
from jax.sharding import PartitionSpec as P

WIDTH = 128
HALF = 4
MAPS_HEADS = 8
LOCAL_HEADS = 8
PREP_HEADS = 8
GRADS_HEADS = 8
SCALE = WIDTH ** (-0.5)
bf16 = jnp.bfloat16
f32 = jnp.float32


def dims(left, right):
    return (((left,), (right,)), ((), ()))


def nn(a, b):
    return lax.dot_general(a, b, dims(1, 0), preferred_element_type=f32)


def nt(a, b):
    return lax.dot_general(a, b, dims(1, 1), preferred_element_type=f32)


def tn(a, b):
    return lax.dot_general(a, b, dims(0, 0), preferred_element_type=f32)


def split(x):
    high = x.astype(bf16)
    return high, (x - high.astype(f32)).astype(bf16)


def iota(shape, dim):
    return lax.broadcasted_iota(jnp.int32, shape, dim)


def order(shape, dim):
    index = iota(shape, dim)
    tokens = shape[dim] // 2
    return jnp.where(index < tokens, 2 * index, 2 * (index - tokens) + 1)


def level_table(rows):
    left = order((rows, rows), 0)
    right = order((rows, rows), 1)
    differ = left ^ right
    level = jnp.zeros((rows, rows), jnp.int32)
    for bit in range(1, (rows - 1).bit_length()):
        level = level + (differ >= (1 << bit)).astype(jnp.int32)
    return jnp.where(left > right, level, -1)


def eye_mask(rows):
    return iota((rows, rows), 0) == iota((rows, rows), 1)


def column(row, diagonal):
    return jnp.sum(jnp.where(diagonal, row, 0.0), axis=1, keepdims=True)


def inverse_norms(keys):
    wide = keys.astype(f32)
    return lax.rsqrt(jnp.sum(wide * wide, axis=1, keepdims=True) + 1e-06)


def pick(ref, head, part):
    lanes = slice(head * WIDTH, (head + 1) * WIDTH)
    half = ref.shape[1] // 2
    span = slice(part * half, (part + 1) * half)
    return jnp.concatenate([ref[0, span, lanes], ref[1, span, lanes]], axis=0)


def put(ref, head, part, value):
    lanes = slice(head * WIDTH, (head + 1) * WIDTH)
    half = ref.shape[1] // 2
    span = slice(part * half, (part + 1) * half)
    ref[0, span, lanes] = value[:half]
    ref[1, span, lanes] = value[half:]


def rate_row(ref, head, part):
    half = ref.shape[2] // 2
    span = slice(part * half, (part + 1) * half)
    return jnp.concatenate([ref[head, 0:1, span], ref[head, 1:2, span]], axis=1)


def here():
    me = lax.axis_index("ctx")
    return me % 2, lax.rem(me // 2, HALF), me // (2 * HALF)


def maps_kernel(
    k_ref, v_ref, q_ref, b_ref, w_ref, send_ref, keep_ref, nh_ref, nl_ref, yh_ref, yl_ref, z_ref, sh_ref, sl_ref,
    rh_ref, rl_ref, ph_ref, pl_ref, near_ref, near_sem,
):
    fetch = pltpu.make_async_copy(w_ref, near_ref, near_sem)
    fetch.start()
    rows = k_ref.shape[1]
    level_of = level_table(rows)
    diagonal = eye_mask(rows)
    heads = range(MAPS_HEADS)
    chains = [(h, part) for h in heads for part in range(2)]
    every = range(len(chains))
    keys = [pick(k_ref, h, part) for h, part in chains]
    rates = [rate_row(b_ref, h, part) for h, part in chains]
    rate_cols = [column(r, diagonal) for r in rates]
    norms = [inverse_norms(k) for k in keys]
    grams = []
    for i in every:
        raw = nt(keys[i], keys[i])
        norm_row = lax.rsqrt(jnp.sum(jnp.where(diagonal, raw, 0.0), axis=0, keepdims=True) + 1e-06)
        grams.append(jnp.where(level_of >= 0, raw * norms[i] * norm_row, 0.0))
    half = rows // 2
    seen = order((rows, half), 0) < 2 * (iota((rows, half), 1) + 1)
    scores = {}
    for i, (h, part) in enumerate(chains):
        query = q_ref[:, h * WIDTH : (h + 1) * WIDTH]
        score = nt(keys[i], query) * (norms[i] * SCALE)
        if part == 0:
            score = jnp.concatenate([jnp.where(seen, score[:, :half], 0.0), score[:, half:]], axis=1)
        else:
            score = jnp.concatenate([jnp.zeros((rows, half), f32), jnp.where(seen, score[:, half:], 0.0)], axis=1)
        scores[h, part] = split(score)
        sh_ref[h, part], sl_ref[h, part] = scores[h, part]
    core = list(grams)
    for level in range((rows - 1).bit_length()):
        joins = [jnp.where(level_of == level, core[i] * rates[i], 0.0).astype(bf16) for i in every]
        core = [core[i] - nn(joins[i], core[i].astype(bf16)) for i in every]
    core_high = [c.astype(bf16) for c in core]
    residual = []
    for i in every:
        high, low = split(grams[i] * rates[i])
        residual.append(grams[i] - core_high[i].astype(f32) - nn(high, core_high[i]) - nn(low, core_high[i]))
    core_low = [
        (residual[i] - nn(core_high[i], (rate_cols[i] * residual[i]).astype(bf16))).astype(bf16) for i in every
    ]
    for i, (h, part) in enumerate(chains):
        nh_ref[h, part] = core_high[i]
        nl_ref[h, part] = core_low[i]

    mapped = [None for h in heads]
    weighted, adjoint = {}, {}
    for part in range(2):
        now = [2 * h + part for h in heads]
        late = [2 * h + 1 - part for h in heads]
        both = [
            jnp.concatenate([keys[i].astype(f32) * norms[i], pick(v_ref, h, part).astype(f32)], axis=1)
            for h, i in enumerate(now)
        ]
        ahead = [keys[i].astype(f32) * norms[i] for i in late]
        if part:
            pieces = [split(m) for m in mapped]
            both = [
                both[h] - norms[i] * (nn(keys[i], pieces[h][0]) + nn(keys[i], pieces[h][1])) for h, i in enumerate(now)
            ]
            pieces = [split(adjoint[h] * (rate_cols[i + 1] * norms[i + 1])) for h, i in enumerate(late)]
            passed = [tn(keys[i + 1], pieces[h][0]) + tn(keys[i + 1], pieces[h][1]) for h, i in enumerate(late)]
            pieces = [split(p) for p in passed]
            ahead = [
                ahead[h] - norms[i] * (nn(keys[i], pieces[h][0]) + nn(keys[i], pieces[h][1]))
                for h, i in enumerate(late)
            ]
        pieces = [split(both[h] * rate_cols[i]) for h, i in enumerate(now)]
        solved = [
            both[h] - nn(core_high[i], pieces[h][0]) - nn(core_low[i], pieces[h][0]) - nn(core_high[i], pieces[h][1])
            for h, i in enumerate(now)
        ]
        pieces = [split(ahead[h] * rate_cols[i]) for h, i in enumerate(late)]
        adjoint = [
            ahead[h] - tn(core_high[i], pieces[h][0]) - tn(core_low[i], pieces[h][0]) - tn(core_high[i], pieces[h][1])
            for h, i in enumerate(late)
        ]
        for h, i in enumerate(now):
            yh_ref[h, part], yl_ref[h, part] = split(solved[h][:, :WIDTH])
            z_ref[h, part] = solved[h][:, WIDTH:]
            weighted[h, part] = split(solved[h][:, :WIDTH] * rate_cols[i])
        pieces = [split(solved[h] * (rate_cols[i] * norms[i])) for h, i in enumerate(now)]
        found = [tn(keys[i], pieces[h][0]) + tn(keys[i], pieces[h][1]) for h, i in enumerate(now)]
        mapped = [found[h] if part == 0 else mapped[h] + found[h] for h in heads]
        for h in heads:
            ph_ref[h, 1 - part], pl_ref[h, 1 - part] = split(adjoint[h])
    place_halves(send_ref, keep_ref, mapped)

    stacked = [
        [jnp.concatenate([pair[h, 0][k], pair[h, 1][k]], axis=0) for pair in (scores, weighted) for k in range(2)]
        for h in heads
    ]
    taken = [tn(sh, wh) + tn(sl, wh) + tn(sh, wl) for sh, sl, wh, wl in stacked]
    for h in heads:
        rh_ref[h], rl_ref[h] = split(q_ref[:, h * WIDTH : (h + 1) * WIDTH].astype(f32) * SCALE - taken[h])
    fetch.wait()


def place_halves(send_ref, keep_ref, values):
    first = here()[0] == 0
    for slot in range(HALF):
        low, high = values[slot], values[HALF + slot]
        keep_ref[slot] = jnp.where(first, low, high).astype(bf16)
        send_ref[slot] = jnp.where(first, high, low).astype(bf16)


def local_grad_kernel(o0, o1, o2, o3, w_ref, rh_ref, rl_ref, send_ref, keep_ref, do_ref, og_ref):
    part = o0.shape[0]
    for shift, ref in enumerate((o0, o1, o2, o3)):
        where = pl.multiple_of(lax.rem(lax.axis_index("head") + HALF - shift, HALF) * part, part)
        og_ref[pl.ds(where, part), :] = ref[...]
    grads = nt(og_ref[...], w_ref[...]).astype(bf16)
    found = []
    for h in range(LOCAL_HEADS):
        grad = grads[:, h * WIDTH : (h + 1) * WIDTH]
        do_ref[h] = grad
        found.append(tn(rh_ref[h], grad) + tn(rl_ref[h], grad))
    place_halves(send_ref, keep_ref, found)


def prep_kernel(k_ref, b_ref, do_ref, nh_ref, nl_ref, sh_ref, sl_ref, u_ref):
    heads = range(PREP_HEADS)
    rows = k_ref.shape[1]
    diagonal = eye_mask(rows)
    reached = {
        (h, part): nn(sh_ref[h, part], do_ref[h]) + nn(sl_ref[h, part], do_ref[h]) for part in (1, 0) for h in heads
    }
    keys = {(h, part): pick(k_ref, h, part) for part in (1, 0) for h in heads}
    norms = {c: inverse_norms(keys[c]) for c in keys}
    rates = {(h, part): column(rate_row(b_ref, h, part), diagonal) for part in (1, 0) for h in heads}
    solved = [None]*8
    for part in (1, 0):
        ahead = [reached[h, part] for h in heads]
        if part == 0:
            pieces = [split(solved[h] * (rates[h, 1] * norms[h, 1])) for h in heads]
            passed = [tn(keys[h, 1], pieces[h][0]) + tn(keys[h, 1], pieces[h][1]) for h in heads]
            pieces = [split(p) for p in passed]
            ahead = [
                ahead[h] - norms[h, 0] * (nn(keys[h, 0], pieces[h][0]) + nn(keys[h, 0], pieces[h][1])) for h in heads
            ]
        pieces = [split(ahead[h] * rates[h, part]) for h in heads]
        solved = [
            ahead[h] - tn(nh_ref[h, part], pieces[h][0]) - tn(nl_ref[h, part], pieces[h][0])
            - tn(nh_ref[h, part], pieces[h][1])
            for h in heads
        ]
        for h in heads:
            u_ref[h, part] = solved[h]


def pair_kernel(keep_ref, got_ref, gkeep_ref, ggot_ref, *outs):
    core, spot, unused = here()
    for shift in range(HALF):
        slot = lax.rem(spot + shift, HALF)
        mine, other = keep_ref[slot].astype(f32), got_ref[slot].astype(f32)
        first = jnp.where(core == 0, mine, other)
        second = jnp.where(core == 0, other, mine)
        mine, other = gkeep_ref[slot].astype(f32), ggot_ref[slot].astype(f32)
        gfirst = jnp.where(core == 0, mine, other)
        gsecond = jnp.where(core == 0, other, mine)
        joined = first + second - nn(second[:, :WIDTH].astype(bf16), first.astype(bf16))
        gjoined = gfirst + gsecond - tn(first[:, :WIDTH].astype(bf16), gsecond.astype(bf16))
        outs[shift][:, : 2 * WIDTH] = joined.astype(bf16)
        outs[shift][:, 2 * WIDTH :] = gjoined.astype(bf16)


def join(first, second):
    forward = first[:, : 2 * WIDTH] + second[:, : 2 * WIDTH]
    forward = forward - nn(second[:, :WIDTH].astype(bf16), first[:, : 2 * WIDTH].astype(bf16))
    backward = first[:, 2 * WIDTH :] + second[:, 2 * WIDTH :]
    backward = backward - tn(first[:, :WIDTH].astype(bf16), second[:, 2 * WIDTH :].astype(bf16))
    return jnp.concatenate([forward, backward], axis=1)


def gather_slots(slots, refs, spot):
    for shift in range(HALF):
        slots[lax.rem(spot + HALF - shift, HALF)] = refs[shift][...]


def row_kernel(a_ref, b_ref, c_ref, d_ref, out_ref, slots):
    gather_slots(slots, (a_ref, b_ref, c_ref, d_ref), here()[1])
    maps = [slots[i].astype(f32) for i in range(HALF)]
    out_ref[...] = join(join(maps[0], maps[1]), join(maps[2], maps[3])).astype(bf16)


def advance(block, state):
    high, low = split(state)
    moved = nn(block[:, :WIDTH], jnp.concatenate([high, low], axis=1))
    return state - moved[:, :WIDTH] - moved[:, WIDTH:] + block[:, WIDTH : 2 * WIDTH].astype(f32)


def retreat(block, grad):
    high, low = split(grad)
    moved = tn(block[:, :WIDTH], jnp.concatenate([high, low], axis=1))
    return grad - moved[:, :WIDTH] - moved[:, WIDTH:] + block[:, 2 * WIDTH :].astype(f32)


def expand_kernel(a_ref, b_ref, c_ref, d_ref, e_ref, f_ref, g_ref, h_ref, o0, o1, o2, o3, chips, lines, found):
    unused, spot, line = here()
    gather_slots(chips, (a_ref, b_ref, c_ref, d_ref), spot)
    gather_slots(lines, (e_ref, f_ref, g_ref, h_ref), line)
    state = jnp.zeros((WIDTH, WIDTH), f32)
    grad = jnp.zeros((WIDTH, WIDTH), f32)
    for i in range(HALF - 1):
        state = jnp.where(i < line, advance(lines[i], state), state)
        back = HALF - 1 - i
        grad = jnp.where(back > line, retreat(lines[back], grad), grad)
    for i in range(HALF):
        found[i, :, :WIDTH] = state.astype(bf16)
        back = HALF - 1 - i
        found[back, :, WIDTH:] = grad.astype(bf16)
        if i < HALF - 1:
            state = advance(chips[i], state)
            grad = retreat(chips[back], grad)
    for shift, out in enumerate((o0, o1, o2, o3)):
        out[...] = found[lax.rem(spot + shift, HALF)]


def down_kernel(a_ref, b_ref, c_ref, d_ref, keep_ref, got_ref, gkeep_ref, ggot_ref, own_ref, send_ref, slots):
    core, spot, unused = here()
    gather_slots(slots, (a_ref, b_ref, c_ref, d_ref), spot)
    for slot in range(HALF):
        state = slots[slot, :, :WIDTH]
        grad = slots[slot, :, WIDTH:]
        first = jnp.where(core == 0, keep_ref[slot].astype(f32), got_ref[slot].astype(f32))
        second = jnp.where(core == 0, got_ref[slot, :, :WIDTH].astype(f32), keep_ref[slot, :, :WIDTH].astype(f32))
        gsecond = jnp.where(core == 0, ggot_ref[slot].astype(f32), gkeep_ref[slot].astype(f32))
        middle = state.astype(f32) - nn(first[:, :WIDTH].astype(bf16), state) + first[:, WIDTH:]
        gmiddle = grad.astype(f32) - tn(second.astype(bf16), grad) + gsecond
        early = jnp.concatenate([state.astype(f32), gmiddle], axis=1)
        late = jnp.concatenate([middle, grad.astype(f32)], axis=1)
        own_ref[slot] = jnp.where(core == 0, early, late).astype(bf16)
        send_ref[slot] = jnp.where(core == 0, late, early).astype(bf16)


def grads_kernel(
    k_ref, q_ref, b_ref, do_ref, yh_ref, yl_ref, z_ref, ph_ref, pl_ref, u_ref, own_ref, got_ref,
    dq_ref, dk_ref, dv_ref, db_ref,
):
    step = pl.program_id(0)
    core = here()[0]
    heads = range(GRADS_HEADS)
    parts = range(2)
    both = [(h, p) for h in heads for p in parts]
    tokens = q_ref.shape[0]
    half = tokens // 2
    rows = 2 * half
    diagonal = eye_mask(rows)
    before = order((rows, rows), 1) < order((rows, rows), 0)
    seen = order((half, rows), 1) < 2 * (iota((half, rows), 0) + 1)
    seen_t = order((rows, half), 0) < 2 * (iota((rows, half), 1) + 1)
    state, after = [], []
    for h in heads:
        head = step * GRADS_HEADS + h
        slot = lax.rem(head, HALF)
        mine = head // HALF == core
        ends = jnp.where(mine, own_ref[slot].astype(f32), got_ref[slot].astype(f32)).astype(bf16)
        state.append(ends[:, :WIDTH])
        after.append(ends[:, WIDTH:])
    keys = {(h, p): pick(k_ref, h, p) for h, p in both}
    rate = {(h, p): column(rate_row(b_ref, h, p), diagonal) for h, p in both}
    norm = {c: inverse_norms(keys[c]) for c in both}
    query = [q_ref[:, h * WIDTH : (h + 1) * WIDTH] for h in heads]

    errors, back = {}, {}
    for h, p in both:
        errors[h, p] = nn(yh_ref[h, p], state[h]) + nn(yl_ref[h, p], state[h]) - z_ref[h, p]
        back[h, p] = -u_ref[h, p] - nn(ph_ref[h, p], after[h]) - nn(pl_ref[h, p], after[h])
    weighted = {c: errors[c] * rate[c] for c in both}
    scaled = {c: back[c] * rate[c] for c in both}
    d_rate = {c: jnp.sum(errors[c] * back[c], axis=1, keepdims=True) for c in both}
    d_rate = {c: jnp.sum(jnp.where(diagonal, d_rate[c], 0.0), axis=0, keepdims=True) for c in both}
    for h, p in both:
        db_ref[h, 0:1, p * half : (p + 1) * half] = d_rate[h, p][:, :half]
        db_ref[h, 1:2, p * half : (p + 1) * half] = d_rate[h, p][:, half:]
        put(dv_ref, h, p, (-scaled[h, p]).astype(bf16))
    ws = {c: split(weighted[c]) for c in both}
    fs = {c: split(scaled[c]) for c in both}
    wn = [jnp.concatenate([(weighted[h, p] * norm[h, p]).astype(bf16) for p in parts], axis=0) for h in heads]
    fn = [jnp.concatenate([(scaled[h, p] * norm[h, p]).astype(bf16) for p in parts], axis=0) for h in heads]
    all_keys = [jnp.concatenate([keys[h, p] for p in parts], axis=0) for h in heads]

    score = [nt(do_ref[h], wn[h]) for h in heads]
    score_t = {(h, p): nt(ws[h, p][0], do_ref[h] if p == 0 else do_ref[h, half:]) for h, p in both}
    lower, upper = {}, {}
    for h, p in both:
        first = jnp.concatenate(ws[h, p], axis=1)
        second = jnp.concatenate(fs[h, p], axis=1)
        wn2 = jnp.concatenate([wn[h], wn[h]], axis=1)
        fn2 = jnp.concatenate([fn[h], fn[h]], axis=1)
        upper[h, p] = nt(first, fn2 if p == 0 else fn2[rows:])
        lower[h, p] = nt(second, wn2[:rows] if p == 0 else wn2)
    pairs, reads = {}, {}
    for h, p in both:
        if p == 0:
            own = jnp.where(before, lower[h, p], jnp.where(diagonal, 0.0, upper[h, p][:, :rows]))
            pairs[h, p] = jnp.concatenate([own, upper[h, p][:, rows:]], axis=1).astype(bf16)
            masked = jnp.concatenate(
                [jnp.where(seen_t, score_t[h, p][:, :half], 0.0), score_t[h, p][:, half:]], axis=1
            )
            reads[h, p] = nn(masked.astype(bf16), query[h])
        else:
            own = jnp.where(before, lower[h, p][:, rows:], jnp.where(diagonal, 0.0, upper[h, p]))
            pairs[h, p] = jnp.concatenate([lower[h, p][:, :rows], own], axis=1).astype(bf16)
            reads[h, p] = nn(jnp.where(seen_t, score_t[h, p], 0.0).astype(bf16), query[h][half:])
    for h in heads:
        masked = jnp.concatenate([
            jnp.concatenate([jnp.where(seen, score[h][:half, :rows], 0.0), jnp.zeros((half, rows), f32)], axis=1),
            jnp.concatenate([score[h][half:, :rows], jnp.where(seen, score[h][half:, rows:], 0.0)], axis=1),
        ], axis=0).astype(bf16)
        dq = nt(do_ref[h], state[h]) - nn(masked, all_keys[h])
        dq_ref[:, h * WIDTH : (h + 1) * WIDTH] = (dq * SCALE).astype(bf16)
    dk = {
        (h, p): nt(fs[h, p][0], state[h]) - reads[h, p] * SCALE - nt(ws[h, p][0], after[h]) - nn(pairs[h, p], all_keys[h])
        for h, p in both
    }
    units = {c: keys[c].astype(f32) * norm[c] for c in both}
    along = {c: jnp.sum(units[c] * dk[c], axis=1, keepdims=True) for c in both}
    for h, p in both:
        put(dk_ref, h, p, (norm[h, p] * (dk[h, p] - units[h, p] * along[h, p])).astype(bf16))


def whole(shape):
    return pl.BlockSpec(shape, lambda *unused: (0,) * len(shape))


def run(kernel, name, args, in_specs, outs, out_specs, grid=(1,), scratch=(), cost=None, vmem=16):
    return pl.pallas_call(
        kernel,
        name=name,
        grid=grid,
        in_specs=in_specs,
        out_specs=out_specs,
        scratch_shapes=list(scratch),
        out_shape=[jax.ShapeDtypeStruct(shape, dtype) for shape, dtype in outs],
        compiler_params=pltpu.CompilerParams(vmem_limit_bytes=vmem * 2**20),
        cost_estimate=cost,
    )(*args)


def small(kernel, name, args, outs, scratch=()):
    return run(
        kernel, name, args,
        [whole(a.shape) for a in args],
        outs,
        [whole(shape) for shape, unused in outs],
        scratch=scratch,
    )


def shards(queries, key_input, value_input, beta_rates, out_grad, out_weight):
    tokens = queries.shape[0]
    heads = queries.shape[1] // WIDTH
    rows = 2 * tokens
    model = out_weight.shape[1]
    key_input, value_input, queries, out_weight, beta_rates = (
        pltpu.with_memory_space_constraint(a, pltpu.HBM)
        for a in (key_input, value_input, queries, out_weight, beta_rates)
    )

    def move(value, target):
        return lax.ppermute(value, "ctx", [(i, target(i)) for i in range(32)])

    def other_core(i):
        return i ^ 1

    def along_x(by):
        return lambda i: (i // 8) * 8 + ((i // 2 + by) % HALF) * 2 + i % 2

    def along_y(by):
        return lambda i: (i + 8 * by) % 32

    def kv_spec(count):
        return pl.BlockSpec((2, tokens, count * WIDTH), lambda s: (0, 0, s))

    def q_spec(count):
        return pl.BlockSpec((tokens, count * WIDTH), lambda s: (0, s))

    def b_spec(count):
        return pl.BlockSpec((count, 2, tokens), lambda s: (s, 0, 0))

    def by_step(count, *shape):
        return pl.BlockSpec((count,) + shape, lambda s: (s,) + (0,) * len(shape))

    gathered = [out_grad] + [
        lax.ppermute(out_grad, "head", [(i, (i + by) % HALF) for i in range(HALF)]) for by in (1, 3, 2)
    ]
    gathered = [gathered[0], gathered[1], gathered[3], gathered[2]]
    tile = (2, tokens, tokens)
    send, keep, nh, nl, yh, yl, z, sh, sl, rh, rl, ph, plow, near = run(
        maps_kernel, "maps", (key_input, value_input, queries, beta_rates, out_weight),
        [kv_spec(MAPS_HEADS), kv_spec(MAPS_HEADS), q_spec(MAPS_HEADS), b_spec(MAPS_HEADS), pl.BlockSpec(memory_space=pl.ANY)],
        [((HALF, WIDTH, 2 * WIDTH), bf16)] * 2 + [((heads,) + tile, bf16)] * 4 + [((heads,) + tile, f32)]
        + [((heads,) + tile, bf16)] * 2 + [((heads, tokens, WIDTH), bf16)] * 2 + [((heads,) + tile, bf16)] * 2 + [(out_weight.shape, bf16)],
        [whole((HALF, WIDTH, 2 * WIDTH))] * 2 + [by_step(MAPS_HEADS, *tile)] * 7
        + [by_step(MAPS_HEADS, tokens, WIDTH)] * 2 + [by_step(MAPS_HEADS, *tile)] * 2 + [pl.BlockSpec(memory_space=pltpu.VMEM)],
        grid=(heads // MAPS_HEADS,),
        scratch=[pltpu.SemaphoreType.DMA],
        vmem=30,
        cost=pl.CostEstimate(flops=14_000_000_000, transcendentals=0, bytes_accessed=8_000_000),
    )
    got = move(send, other_core)
    gsend, gkeep, grad = run(
        local_grad_kernel, "local_grad", (*gathered, near, rh, rl),
        [
            *[whole(out_grad.shape)] * HALF,
            pl.BlockSpec(memory_space=pltpu.VMEM),
            *[by_step(LOCAL_HEADS, tokens, WIDTH)] * 2,
        ],
        [((HALF, WIDTH, WIDTH), bf16)] * 2 + [((heads, tokens, WIDTH), bf16)],
        [whole((HALF, WIDTH, WIDTH))] * 2 + [by_step(LOCAL_HEADS, tokens, WIDTH)],
        grid=(heads // LOCAL_HEADS,),
        scratch=[pltpu.VMEM((tokens, model), bf16)],
        vmem=24,
        cost=pl.CostEstimate(flops=2_000_000_000, transcendentals=0, bytes_accessed=10_000_000),
    )
    ggot = move(gsend, other_core)
    map_shape = ((WIDTH, 3 * WIDTH), bf16)
    chip = small(pair_kernel, "pair", (keep, got, gkeep, ggot), [map_shape] * HALF)
    chip = list(chip)
    chip[0], grad = lax.optimization_barrier((chip[0], grad))
    (reached,) = run(
        prep_kernel, "prep", (key_input, beta_rates, grad, nh, nl, sh, sl),
        [
            kv_spec(PREP_HEADS), b_spec(PREP_HEADS), by_step(PREP_HEADS, tokens, WIDTH),
            *[by_step(PREP_HEADS, *tile)] * 4,
        ],
        [((heads,) + tile, f32)],
        [by_step(PREP_HEADS, *tile)],
        grid=(heads // PREP_HEADS,),
        vmem=24,
        cost=pl.CostEstimate(flops=4_000_000_000, transcendentals=0, bytes_accessed=6_000_000),
    )
    chip = [chip[0]] + [move(chip[by], along_x(by)) for by in range(1, HALF)]
    chip[0], reached = lax.optimization_barrier((chip[0], reached))
    slots = pltpu.VMEM((HALF, WIDTH, 3 * WIDTH), bf16)
    (line,) = small(row_kernel, "line", chip, [map_shape], [slots])
    lines = [line] + [move(line, along_y(by)) for by in range(1, HALF)]
    ends_shape = ((WIDTH, 2 * WIDTH), bf16)
    ends_slots = pltpu.VMEM((HALF, WIDTH, 2 * WIDTH), bf16)
    ends = small(expand_kernel, "expand", chip + lines, [ends_shape] * HALF, [slots, slots, ends_slots])
    ends = [ends[0]] + [move(ends[by], along_x(by)) for by in range(1, HALF)]
    own, passed = small(
        down_kernel, "down", ends + [keep, got, gkeep, ggot],
        [((HALF, WIDTH, 2 * WIDTH), bf16)] * 2, [ends_slots],
    )
    taken = move(passed, other_core)
    return tuple(run(
        grads_kernel, "grads",
        (key_input, queries, beta_rates, grad, yh, yl, z, ph, plow, reached, own, taken),
        [
            kv_spec(GRADS_HEADS), q_spec(GRADS_HEADS), b_spec(GRADS_HEADS), by_step(GRADS_HEADS, tokens, WIDTH),
            *[by_step(GRADS_HEADS, *tile)] * 6,
            whole((HALF, WIDTH, 2 * WIDTH)), whole((HALF, WIDTH, 2 * WIDTH)),
        ],
        [
            (queries.shape, bf16), (key_input.shape, bf16), (value_input.shape, bf16), (beta_rates.shape, f32),
        ],
        [q_spec(GRADS_HEADS), kv_spec(GRADS_HEADS), kv_spec(GRADS_HEADS), b_spec(GRADS_HEADS)],
        grid=(heads // GRADS_HEADS,),
        vmem=24,
        cost=pl.CostEstimate(flops=8_000_000_000, transcendentals=0, bytes_accessed=14_000_000),
    ))


def solution(mesh):
    placed = (
        P("ctx", "head"),
        P(None, "ctx", "head"),
        P(None, "ctx", "head"),
        P("head", None, "ctx"),
        P(("ctx", "head"), None),
        P("head", None),
    )
    return jax.shard_map(
        shards,
        mesh=mesh,
        in_specs=placed,
        out_specs=(
            P("ctx", "head"),
            P(None, "ctx", "head"),
            P(None, "ctx", "head"),
            P("head", None, "ctx"),
        ),
        check_vma=False,
    )
```

time: 70.9 us -> 61 us (0.86)
  Pallas kernels: 30.6 us -> 23.5 us
  waiting for transfers between devices: 15.6 us -> 12.9 us
    pallas_call x7 -> x8, Pallas kernels: 30.6 us -> 23.5 us  [run(): pl.pallas_call(kernel, name=name, grid=grid, in_specs=in_specs, out_specs...]
    ppermute x12, waiting for transfers between devices: 15.6 us -> 12.9 us  [move(): return lax.ppermute(value, 'ctx', [(i, target(i)) for i in range(32)])]
  transfers between devices with their start and end apart: 15 -> 15, of which waited for: 9 -> 8; matrix products, arithmetic and copies ran while one was open for 0% -> 0% of each run, Pallas kernels for 26% -> 26%
where the time goes in v3:
time: 61 us; the launch traced here: 60.8 us
  starting transfers between devices  23.7 us (39%)
  Pallas kernels  23.5 us (39%)
  waiting for transfers between devices  12.9 us (21%)
  between operations  0.72 us (1%)
    pallas_call x8, Pallas kernels, run(): pl.pallas_call(kernel, name=name, grid=grid, in_specs=in_specs, out_specs...  23.5 us
    ppermute x12, starting transfers between devices, move(): return lax.ppermute(value, 'ctx', [(i, target(i)) for i in range(32)])  16.5 us
    ppermute x12, waiting for transfers between devices, move(): return lax.ppermute(value, 'ctx', [(i, target(i)) for i in range(32)])  12.9 us
    ppermute x3, starting transfers between devices, shards(): lax.ppermute(out_grad, 'head', [(i, (i + by) % HALF) for i in range(HALF)])  7.18 us
  transfers between devices with their start and end apart: 15, of which 8 were waited for; matrix products, arithmetic and copies ran while one was open for 0% of the time, Pallas kernels for 26%

profile of v3, /device:TPU:1, one launch (start us, length us, event | category | flops | bytes accessed | tf_op | source)
XLA Modules:
  0.0 60.8 jit_solution(12183809046389493615)
XLA Ops:
  0.6 0.0 copy-start
  0.6 4.5 %collective-permute-start.2 = (bf16[32,4096]{1,0:T(8,128)(2,1)}, bf16[32,4096]{1,0:T(8,128)(2,1)S(1)}, u32[]{:S(2)}, u32[]{:S(2)}) collective-permute-start(bf16[32,4096]{1,0:T(8,128)(2,1)} %o0.1), channel_id=1, source_target_pairs={{0,2},{1,3},{2,0},{3,1},{4,6},{5,7},{6,4},{7,5},{8,10},{9,11},{10,... | collective-permute-start | bytes 786440 | tf_op jit(solution)/shard_map/ppermute | solution.py:490
  5.1 0.7 %collective-permute-start.1 = (bf16[32,4096]{1,0:T(8,128)(2,1)}, bf16[32,4096]{1,0:T(8,128)(2,1)S(1)}, u32[]{:S(2)}, u32[]{:S(2)}) collective-permute-start(bf16[32,4096]{1,0:T(8,128)(2,1)} %o0.1), channel_id=1, source_target_pairs={{0,1},{1,2},{2,3},{3,0},{4,5},{5,6},{6,7},{7,4},{8,9},{9,10},{10,1... | collective-permute-start | bytes 786440 | tf_op jit(solution)/shard_map/ppermute | solution.py:490
  5.9 1.9 %collective-permute-start.3 = (bf16[32,4096]{1,0:T(8,128)(2,1)}, bf16[32,4096]{1,0:T(8,128)(2,1)S(1)}, u32[]{:S(2)}, u32[]{:S(2)}) collective-permute-start(bf16[32,4096]{1,0:T(8,128)(2,1)} %o0.1), channel_id=1, source_target_pairs={{0,3},{1,0},{2,1},{3,2},{4,7},{5,4},{6,5},{7,6},{8,11},{9,8},{10,9... | collective-permute-start | bytes 786440 | tf_op jit(solution)/shard_map/ppermute | solution.py:490
  7.8 9.9 %maps.1 = (bf16[4,128,256]{2,1,0:T(8,128)(2,1)S(1)}, bf16[4,128,256]{2,1,0:T(8,128)(2,1)S(1)}, bf16[8,2,128,128]{3,2,1,0:T(8,128)(2,1)S(1)}, bf16[8,2,128,128]{3...) custom-call(bf16[2,128,1024]{2,1,0:T(8,128)(2,1)} %k_ref.5, ...), custom_call_target="tpu_custom_call" | custom-call | flops 14000000000 | bytes 8000000 | tf_op jit(solution)/shard_map/maps/pallas_call | solution.py:432
  17.7 1.6 %collective-permute-start = (bf16[4,128,256]{2,1,0:T(8,128)(2,1)S(1)}, bf16[4,128,256]{2,1,0:T(8,128)(2,1)S(1)}, u32[]{:S(2)}, u32[]{:S(2)}) collective-permute-start(bf16[4,128,256]{2,1,0:T(8,128)(2,1)S(1)} %get-tuple-element.36), channel_id=1, source_target_pairs={{0,4},{4,0},{8,12},{12,8},{16,20},{20,16},{24,28},{28,24},{32,36},... | collective-permute-start | bytes 786440 | tf_op jit(solution)/shard_map/ppermute | solution.py:466
  19.3 0.0 collective-permute-done.2.o2
  19.3 0.0 collective-permute-done.1.o1
  19.3 0.0 collective-permute-done.3.o3
  19.3 0.0 copy-done
  19.4 3.1 %local_grad.1 = (bf16[4,128,128]{2,1,0:T(8,128)(2,1)S(1)}, bf16[4,128,128]{2,1,0:T(8,128)(2,1)S(1)}, bf16[8,128,128]{2,1,0:T(8,128)(2,1)S(1)}) custom-call(bf16[32,4096]{1,0:T(8,128)(2,1)S(1)} %copy-done, bf16[32,4096]{1,0:T(8,128)(2,1)S(1)} %collective-permute-done.1.o1, bf16[32,4096]{1,0:T(8,128)(2,1)S(1)} %collective-permute-done.2.o2, ...), custom_call_target="tpu_custom_call" | custom-call | flops 2000000000 | bytes 10000000 | tf_op jit(solution)/shard_map/local_grad/pallas_call | solution.py:432
  22.5 0.1 collective-permute-start.4
  22.6 0.0 collective-permute-done.got_ref
  22.6 1.3 %collective-permute-done.4.ggot_ref = bf16[4,128,128]{2,1,0:T(8,128)(2,1)S(1)} collective-permute-done((bf16[4,128,128]{2,1,0:T(8,128)(2,1)S(1)}, bf16[4,128,128]{2,1,0:T(8,128)(2,1)S(1)}, u32[]{:S(2)}, u32[]{:S(2)}) %collective-permute-start.4) | collective-permute-done | bytes 131104 | tf_op jit(solution)/shard_map/ppermute | solution.py:466
  23.9 0.3 pair.1
  24.2 1.3 %collective-permute-start.5 = (bf16[128,384]{1,0:T(8,128)(2,1)S(1)}, bf16[128,384]{1,0:T(8,128)(2,1)S(1)}, u32[]{:S(2)}, u32[]{:S(2)}) collective-permute-start(bf16[128,384]{1,0:T(8,128)(2,1)S(1)} %get-tuple-element.57), channel_id=1, source_target_pairs={{0,8},{4,12},{8,16},{12,20},{16,24},{20,28},{24,0},{28,4},{32,40},... | collective-permute-start | bytes 294920 | tf_op jit(solution)/shard_map/ppermute | solution.py:466
  25.5 2.5 %collective-permute-start.6 = (bf16[128,384]{1,0:T(8,128)(2,1)S(1)}, bf16[128,384]{1,0:T(8,128)(2,1)S(1)}, u32[]{:S(2)}, u32[]{:S(2)}) collective-permute-start(bf16[128,384]{1,0:T(8,128)(2,1)S(1)} %get-tuple-element.58), channel_id=1, source_target_pairs={{0,16},{4,20},{8,24},{12,28},{16,0},{20,4},{24,8},{28,12},{32,48},... | collective-permute-start | bytes 294920 | tf_op jit(solution)/shard_map/ppermute | solution.py:466
  27.9 1.1 %collective-permute-start.7 = (bf16[128,384]{1,0:T(8,128)(2,1)S(1)}, bf16[128,384]{1,0:T(8,128)(2,1)S(1)}, u32[]{:S(2)}, u32[]{:S(2)}) collective-permute-start(bf16[128,384]{1,0:T(8,128)(2,1)S(1)} %get-tuple-element.59), channel_id=1, source_target_pairs={{0,24},{4,28},{8,0},{12,4},{16,8},{20,12},{24,16},{28,20},{32,56},... | collective-permute-start | bytes 294920 | tf_op jit(solution)/shard_map/ppermute | solution.py:466
  29.1 2.7 %prep.1.u_ref = f32[8,2,128,128]{3,2,1,0:T(8,128)S(1)} custom-call(bf16[2,128,1024]{2,1,0:T(8,128)(2,1)} %k_ref.5, f32[8,2,128]{2,1,0:T(2,128)} %b_ref.5, bf16[8,128,128]{2,1,0:T(8,128)(2,1)S(1)} %get-tuple-element.44.do_ref, bf16[8,2,128,128]{3,2,1,0:T(8,128)(2,1)S(1)} %get-tuple-element.51.nh_ref, bf16[8,2,128,128]{3,2,1,0:T(8,128)(2,1)S(1)} %get-tuple-element.52.nl_ref, ...), custom_call_target="tpu_custom_call" | custom-call | flops 4000000000 | bytes 6000000 | tf_op jit(solution)/shard_map/prep/pallas_call | solution.py:432
  31.8 0.0 collective-permute-done.5.b_ref
  31.8 1.0 %collective-permute-done.6.c_ref = bf16[128,384]{1,0:T(8,128)(2,1)S(1)} collective-permute-done((bf16[128,384]{1,0:T(8,128)(2,1)S(1)}, bf16[128,384]{1,0:T(8,128)(2,1)S(1)}, u32[]{:S(2)}, u32[]{:S(2)}) %collective-permute-start.6) | collective-permute-done | bytes 98336 | tf_op jit(solution)/shard_map/ppermute | solution.py:466
  32.8 0.0 collective-permute-done.7.d_ref
  32.8 0.4 line.1.e_ref
  33.2 2.8 %collective-permute-start.10 = (bf16[128,384]{1,0:T(8,128)(2,1)S(1)}, bf16[128,384]{1,0:T(8,128)(2,1)S(1)}, u32[]{:S(2)}, u32[]{:S(2)}) collective-permute-start(bf16[128,384]{1,0:T(8,128)(2,1)S(1)} %line.1.e_ref), channel_id=1, source_target_pairs={{0,96},{4,100},{8,104},{12,108},{16,112},{20,116},{24,120},{28,124... | collective-permute-start | bytes 294920 | tf_op jit(solution)/shard_map/ppermute | solution.py:466
  36.0 0.3 collective-permute-start.9
  36.4 0.7 %collective-permute-start.8 = (bf16[128,384]{1,0:T(8,128)(2,1)S(1)}, bf16[128,384]{1,0:T(8,128)(2,1)S(1)}, u32[]{:S(2)}, u32[]{:S(2)}) collective-permute-start(bf16[128,384]{1,0:T(8,128)(2,1)S(1)} %line.1.e_ref), channel_id=1, source_target_pairs={{0,32},{4,36},{8,40},{12,44},{16,48},{20,52},{24,56},{28,60},{32,6... | collective-permute-start | bytes 294920 | tf_op jit(solution)/shard_map/ppermute | solution.py:466
  37.1 0.6 collective-permute-done.10.h_ref
  37.7 3.4 %collective-permute-done.9.g_ref = bf16[128,384]{1,0:T(8,128)(2,1)S(1)} collective-permute-done((bf16[128,384]{1,0:T(8,128)(2,1)S(1)}, bf16[128,384]{1,0:T(8,128)(2,1)S(1)}, u32[]{:S(2)}, u32[]{:S(2)}) %collective-permute-start.9) | collective-permute-done | bytes 98336 | tf_op jit(solution)/shard_map/ppermute | solution.py:466
  41.1 2.4 %collective-permute-done.8.f_ref = bf16[128,384]{1,0:T(8,128)(2,1)S(1)} collective-permute-done((bf16[128,384]{1,0:T(8,128)(2,1)S(1)}, bf16[128,384]{1,0:T(8,128)(2,1)S(1)}, u32[]{:S(2)}, u32[]{:S(2)}) %collective-permute-start.8) | collective-permute-done | bytes 98336 | tf_op jit(solution)/shard_map/ppermute | solution.py:466
  43.5 1.0 %expand.1 = (bf16[128,256]{1,0:T(8,128)(2,1)S(1)}, bf16[128,256]{1,0:T(8,128)(2,1)S(1)}, bf16[128,256]{1,0:T(8,128)(2,1)S(1)}, bf16[128,256]{1,0:T(8,128)(2,1)S(1)}) custom-call(bf16[128,384]{1,0:T(8,128)(2,1)S(1)} %get-tuple-element.56.a_ref, bf16[128,384]{1,0:T(8,128)(2,1)S(1)} %collective-permute-done.5.b_ref, ...), custom_call_target="tpu_custom_call" | custom-call | tf_op jit(solution)/shard_map/expand/pallas_call | solution.py:432
  44.6 0.1 collective-permute-start.11
  44.7 1.3 %collective-permute-start.12 = (bf16[128,256]{1,0:T(8,128)(2,1)S(1)}, bf16[128,256]{1,0:T(8,128)(2,1)S(1)}, u32[]{:S(2)}, u32[]{:S(2)}) collective-permute-start(bf16[128,256]{1,0:T(8,128)(2,1)S(1)} %get-tuple-element.62), channel_id=1, source_target_pairs={{0,16},{4,20},{8,24},{12,28},{16,0},{20,4},{24,8},{28,12},{32,48},... | collective-permute-start | bytes 196616 | tf_op jit(solution)/shard_map/ppermute | solution.py:466
  45.9 1.7 %collective-permute-start.13 = (bf16[128,256]{1,0:T(8,128)(2,1)S(1)}, bf16[128,256]{1,0:T(8,128)(2,1)S(1)}, u32[]{:S(2)}, u32[]{:S(2)}) collective-permute-start(bf16[128,256]{1,0:T(8,128)(2,1)S(1)} %get-tuple-element.63), channel_id=1, source_target_pairs={{0,24},{4,28},{8,0},{12,4},{16,8},{20,12},{24,16},{28,20},{32,56},... | collective-permute-start | bytes 196616 | tf_op jit(solution)/shard_map/ppermute | solution.py:466
  47.6 2.1 %collective-permute-done.11.b_ref = bf16[128,256]{1,0:T(8,128)(2,1)S(1)} collective-permute-done((bf16[128,256]{1,0:T(8,128)(2,1)S(1)}, bf16[128,256]{1,0:T(8,128)(2,1)S(1)}, u32[]{:S(2)}, u32[]{:S(2)}) %collective-permute-start.11) | collective-permute-done | bytes 65568 | tf_op jit(solution)/shard_map/ppermute | solution.py:466
  49.7 0.0 collective-permute-done.12.c_ref
  49.7 0.9 %collective-permute-done.13.d_ref = bf16[128,256]{1,0:T(8,128)(2,1)S(1)} collective-permute-done((bf16[128,256]{1,0:T(8,128)(2,1)S(1)}, bf16[128,256]{1,0:T(8,128)(2,1)S(1)}, u32[]{:S(2)}, u32[]{:S(2)}) %collective-permute-start.13) | collective-permute-done | bytes 65568 | tf_op jit(solution)/shard_map/ppermute | solution.py:466
  50.5 0.3 down.1
  50.9 3.1 %collective-permute-start.14 = (bf16[4,128,256]{2,1,0:T(8,128)(2,1)S(1)}, bf16[4,128,256]{2,1,0:T(8,128)(2,1)S(1)}, u32[]{:S(2)}, u32[]{:S(2)}) collective-permute-start(bf16[4,128,256]{2,1,0:T(8,128)(2,1)S(1)} %get-tuple-element.65), channel_id=1, source_target_pairs={{0,4},{4,0},{8,12},{12,8},{16,20},{20,16},{24,28},{28,24},{32,36},... | collective-permute-start | bytes 786440 | tf_op jit(solution)/shard_map/ppermute | solution.py:466
  53.9 1.2 %collective-permute-done.14.got_ref = bf16[4,128,256]{2,1,0:T(8,128)(2,1)S(1)} collective-permute-done((bf16[4,128,256]{2,1,0:T(8,128)(2,1)S(1)}, bf16[4,128,256]{2,1,0:T(8,128)(2,1)S(1)}, u32[]{:S(2)}, u32[]{:S(2)}) %collective-permute-start.14) | collective-permute-done | bytes 262176 | tf_op jit(solution)/shard_map/ppermute | solution.py:466
  55.1 5.7 %grads.1 = (bf16[128,1024]{1,0:T(8,128)(2,1)}, bf16[2,128,1024]{2,1,0:T(8,128)(2,1)}, bf16[2,128,1024]{2,1,0:T(8,128)(2,1)}, f32[8,2,128]{2,1,0:T(2,128)}) custom-call(bf16[2,128,1024]{2,1,0:T(8,128)(2,1)} %k_ref.5, bf16[128,1024]{1,0:T(8,128)(2,1)} %q_ref.3, f32[8,2,128]{2,1,0:T(2,128)} %b_ref.5, bf16[8,128,128]{2,1,0:T(8,128)(2,1)S(1)} %get-tuple-element.44.do_ref, ...), custom_call_target="tpu_custom_call" | custom-call | flops 8000000000 | bytes 14000000 | tf_op jit(solution)/shard_map/grads/pallas_call | solution.py:432
Async XLA Ops:
  0.6 18.7 %copy-start = (bf16[32,4096]{1,0:T(8,128)(2,1)S(1)}, bf16[32,4096]{1,0:T(8,128)(2,1)}, u32[]{:S(2)}) copy-start(bf16[32,4096]{1,0:T(8,128)(2,1)} %o0.1) | copy-start | bytes 786436
  0.6 18.7 %collective-permute-start.2 = (bf16[32,4096]{1,0:T(8,128)(2,1)}, bf16[32,4096]{1,0:T(8,128)(2,1)S(1)}, u32[]{:S(2)}, u32[]{:S(2)}) collective-permute-start(bf16[32,4096]{1,0:T(8,128)(2,1)} %o0.1), channel_id=1, source_target_pairs={{0,2},{1,3},{2,0},{3,1},{4,6},{5,7},{6,4},{7,5},{8,10},{9,11},{10,... | collective-permute-start | bytes 786440 | tf_op jit(solution)/shard_map/ppermute | solution.py:490
  5.1 14.2 %collective-permute-start.1 = (bf16[32,4096]{1,0:T(8,128)(2,1)}, bf16[32,4096]{1,0:T(8,128)(2,1)S(1)}, u32[]{:S(2)}, u32[]{:S(2)}) collective-permute-start(bf16[32,4096]{1,0:T(8,128)(2,1)} %o0.1), channel_id=1, source_target_pairs={{0,1},{1,2},{2,3},{3,0},{4,5},{5,6},{6,7},{7,4},{8,9},{9,10},{10,1... | collective-permute-start | bytes 786440 | tf_op jit(solution)/shard_map/ppermute | solution.py:490
  5.9 13.5 %collective-permute-start.3 = (bf16[32,4096]{1,0:T(8,128)(2,1)}, bf16[32,4096]{1,0:T(8,128)(2,1)S(1)}, u32[]{:S(2)}, u32[]{:S(2)}) collective-permute-start(bf16[32,4096]{1,0:T(8,128)(2,1)} %o0.1), channel_id=1, source_target_pairs={{0,3},{1,0},{2,1},{3,2},{4,7},{5,4},{6,5},{7,6},{8,11},{9,8},{10,9... | collective-permute-start | bytes 786440 | tf_op jit(solution)/shard_map/ppermute | solution.py:490
  17.7 4.8 %collective-permute-start = (bf16[4,128,256]{2,1,0:T(8,128)(2,1)S(1)}, bf16[4,128,256]{2,1,0:T(8,128)(2,1)S(1)}, u32[]{:S(2)}, u32[]{:S(2)}) collective-permute-start(bf16[4,128,256]{2,1,0:T(8,128)(2,1)S(1)} %get-tuple-element.36), channel_id=1, source_target_pairs={{0,4},{4,0},{8,12},{12,8},{16,20},{20,16},{24,28},{28,24},{32,36},... | collective-permute-start | bytes 786440 | tf_op jit(solution)/shard_map/ppermute | solution.py:466
  22.5 1.4 %collective-permute-start.4 = (bf16[4,128,128]{2,1,0:T(8,128)(2,1)S(1)}, bf16[4,128,128]{2,1,0:T(8,128)(2,1)S(1)}, u32[]{:S(2)}, u32[]{:S(2)}) collective-permute-start(bf16[4,128,128]{2,1,0:T(8,128)(2,1)S(1)} %get-tuple-element.41), channel_id=1, source_target_pairs={{0,4},{4,0},{8,12},{12,8},{16,20},{20,16},{24,28},{28,24},{32,36},... | collective-permute-start | bytes 393224 | tf_op jit(solution)/shard_map/ppermute | solution.py:466
  24.2 7.6 %collective-permute-start.5 = (bf16[128,384]{1,0:T(8,128)(2,1)S(1)}, bf16[128,384]{1,0:T(8,128)(2,1)S(1)}, u32[]{:S(2)}, u32[]{:S(2)}) collective-permute-start(bf16[128,384]{1,0:T(8,128)(2,1)S(1)} %get-tuple-element.57), channel_id=1, source_target_pairs={{0,8},{4,12},{8,16},{12,20},{16,24},{20,28},{24,0},{28,4},{32,40},... | collective-permute-start | bytes 294920 | tf_op jit(solution)/shard_map/ppermute | solution.py:466
  25.5 7.3 %collective-permute-start.6 = (bf16[128,384]{1,0:T(8,128)(2,1)S(1)}, bf16[128,384]{1,0:T(8,128)(2,1)S(1)}, u32[]{:S(2)}, u32[]{:S(2)}) collective-permute-start(bf16[128,384]{1,0:T(8,128)(2,1)S(1)} %get-tuple-element.58), channel_id=1, source_target_pairs={{0,16},{4,20},{8,24},{12,28},{16,0},{20,4},{24,8},{28,12},{32,48},... | collective-permute-start | bytes 294920 | tf_op jit(solution)/shard_map/ppermute | solution.py:466
  27.9 4.9 %collective-permute-start.7 = (bf16[128,384]{1,0:T(8,128)(2,1)S(1)}, bf16[128,384]{1,0:T(8,128)(2,1)S(1)}, u32[]{:S(2)}, u32[]{:S(2)}) collective-permute-start(bf16[128,384]{1,0:T(8,128)(2,1)S(1)} %get-tuple-element.59), channel_id=1, source_target_pairs={{0,24},{4,28},{8,0},{12,4},{16,8},{20,12},{24,16},{28,20},{32,56},... | collective-permute-start | bytes 294920 | tf_op jit(solution)/shard_map/ppermute | solution.py:466
  33.2 4.4 %collective-permute-start.10 = (bf16[128,384]{1,0:T(8,128)(2,1)S(1)}, bf16[128,384]{1,0:T(8,128)(2,1)S(1)}, u32[]{:S(2)}, u32[]{:S(2)}) collective-permute-start(bf16[128,384]{1,0:T(8,128)(2,1)S(1)} %line.1.e_ref), channel_id=1, source_target_pairs={{0,96},{4,100},{8,104},{12,108},{16,112},{20,116},{24,120},{28,124... | collective-permute-start | bytes 294920 | tf_op jit(solution)/shard_map/ppermute | solution.py:466
  36.0 5.1 %collective-permute-start.9 = (bf16[128,384]{1,0:T(8,128)(2,1)S(1)}, bf16[128,384]{1,0:T(8,128)(2,1)S(1)}, u32[]{:S(2)}, u32[]{:S(2)}) collective-permute-start(bf16[128,384]{1,0:T(8,128)(2,1)S(1)} %line.1.e_ref), channel_id=1, source_target_pairs={{0,64},{4,68},{8,72},{12,76},{16,80},{20,84},{24,88},{28,92},{32,9... | collective-permute-start | bytes 294920 | tf_op jit(solution)/shard_map/ppermute | solution.py:466
  36.4 7.2 %collective-permute-start.8 = (bf16[128,384]{1,0:T(8,128)(2,1)S(1)}, bf16[128,384]{1,0:T(8,128)(2,1)S(1)}, u32[]{:S(2)}, u32[]{:S(2)}) collective-permute-start(bf16[128,384]{1,0:T(8,128)(2,1)S(1)} %line.1.e_ref), channel_id=1, source_target_pairs={{0,32},{4,36},{8,40},{12,44},{16,48},{20,52},{24,56},{28,60},{32,6... | collective-permute-start | bytes 294920 | tf_op jit(solution)/shard_map/ppermute | solution.py:466
  44.6 5.1 %collective-permute-start.11 = (bf16[128,256]{1,0:T(8,128)(2,1)S(1)}, bf16[128,256]{1,0:T(8,128)(2,1)S(1)}, u32[]{:S(2)}, u32[]{:S(2)}) collective-permute-start(bf16[128,256]{1,0:T(8,128)(2,1)S(1)} %get-tuple-element.61), channel_id=1, source_target_pairs={{0,8},{4,12},{8,16},{12,20},{16,24},{20,28},{24,0},{28,4},{32,40},... | collective-permute-start | bytes 196616 | tf_op jit(solution)/shard_map/ppermute | solution.py:466
  44.7 5.0 %collective-permute-start.12 = (bf16[128,256]{1,0:T(8,128)(2,1)S(1)}, bf16[128,256]{1,0:T(8,128)(2,1)S(1)}, u32[]{:S(2)}, u32[]{:S(2)}) collective-permute-start(bf16[128,256]{1,0:T(8,128)(2,1)S(1)} %get-tuple-element.62), channel_id=1, source_target_pairs={{0,16},{4,20},{8,24},{12,28},{16,0},{20,4},{24,8},{28,12},{32,48},... | collective-permute-start | bytes 196616 | tf_op jit(solution)/shard_map/ppermute | solution.py:466
  45.9 4.6 %collective-permute-start.13 = (bf16[128,256]{1,0:T(8,128)(2,1)S(1)}, bf16[128,256]{1,0:T(8,128)(2,1)S(1)}, u32[]{:S(2)}, u32[]{:S(2)}) collective-permute-start(bf16[128,256]{1,0:T(8,128)(2,1)S(1)} %get-tuple-element.63), channel_id=1, source_target_pairs={{0,24},{4,28},{8,0},{12,4},{16,8},{20,12},{24,16},{28,20},{32,56},... | collective-permute-start | bytes 196616 | tf_op jit(solution)/shard_map/ppermute | solution.py:466
  50.9 4.3 %collective-permute-start.14 = (bf16[4,128,256]{2,1,0:T(8,128)(2,1)S(1)}, bf16[4,128,256]{2,1,0:T(8,128)(2,1)S(1)}, u32[]{:S(2)}, u32[]{:S(2)}) collective-permute-start(bf16[4,128,256]{2,1,0:T(8,128)(2,1)S(1)} %get-tuple-element.65), channel_id=1, source_target_pairs={{0,4},{4,0},{8,12},{12,8},{16,20},{20,16},{24,28},{28,24},{32,36},... | collective-permute-start | bytes 786440 | tf_op jit(solution)/shard_map/ppermute | solution.py:466

commit v4 on v3

--- a/solution.py
+++ b/solution.py
@@ -303,9 +303,9 @@
     unused, spot, line = here()
     gather_slots(chips, (a_ref, b_ref, c_ref, d_ref), spot)
     gather_slots(lines, (e_ref, f_ref, g_ref, h_ref), line)
-    state = jnp.zeros((WIDTH, WIDTH), f32)
-    grad = jnp.zeros((WIDTH, WIDTH), f32)
-    for i in range(HALF - 1):
+    state = jnp.where(line > 0, lines[0, :, WIDTH : 2 * WIDTH].astype(f32), 0.0)
+    grad = jnp.where(line < HALF - 1, lines[HALF - 1, :, 2 * WIDTH :].astype(f32), 0.0)
+    for i in range(1, HALF - 1):
         state = jnp.where(i < line, advance(lines[i], state), state)
         back = HALF - 1 - i
         grad = jnp.where(back > line, retreat(lines[back], grad), grad)
@@ -457,6 +457,7 @@
     heads = queries.shape[1] // WIDTH
     rows = 2 * tokens
     model = out_weight.shape[1]
+    near_keys, near_queries, near_rates = key_input, queries, beta_rates
     key_input, value_input, queries, out_weight, beta_rates = (
         pltpu.with_memory_space_constraint(a, pltpu.HBM)
         for a in (key_input, value_input, queries, out_weight, beta_rates)
@@ -524,7 +525,7 @@
     chip = list(chip)
     chip[0], grad = lax.optimization_barrier((chip[0], grad))
     (reached,) = run(
-        prep_kernel, "prep", (key_input, beta_rates, grad, nh, nl, sh, sl),
+        prep_kernel, "prep", (near_keys, near_rates, grad, nh, nl, sh, sl),
         [
             kv_spec(PREP_HEADS), b_spec(PREP_HEADS), by_step(PREP_HEADS, tokens, WIDTH),
             *[by_step(PREP_HEADS, *tile)] * 4,
@@ -551,7 +552,7 @@
     taken = move(passed, other_core)
     return tuple(run(
         grads_kernel, "grads",
-        (key_input, queries, beta_rates, grad, yh, yl, z, ph, plow, reached, own, taken),
+        (near_keys, near_queries, near_rates, grad, yh, yl, z, ph, plow, reached, own, taken),
         [
             kv_spec(GRADS_HEADS), q_spec(GRADS_HEADS), b_spec(GRADS_HEADS), by_step(GRADS_HEADS, tokens, WIDTH),
             *[by_step(GRADS_HEADS, *tile)] * 6,

time: 61 us -> 59.8 us (0.980)
  Pallas kernels: 23.5 us -> 21.2 us
  waiting for transfers between devices: 12.9 us -> 13.9 us
    pallas_call x8, Pallas kernels: 23.5 us -> 21.2 us  [run(): pl.pallas_call(kernel, name=name, grid=grid, in_specs=in_specs, out_specs...]
    ppermute x12, waiting for transfers between devices: 12.9 us -> 13.9 us  [move(): return lax.ppermute(value, 'ctx', [(i, target(i)) for i in range(32)])]
  transfers between devices with their start and end apart: 15 -> 15, of which waited for: 8 -> 8; matrix products, arithmetic and copies ran while one was open for 0% -> 0% of each run, Pallas kernels for 26% -> 25%
where the time goes in v4:
time: 59.8 us; the launch traced here: 59.6 us
  starting transfers between devices  23.7 us (40%)
  Pallas kernels  21.2 us (35%)
  waiting for transfers between devices  13.9 us (23%)
  between operations  0.74 us (1%)
    pallas_call x8, Pallas kernels, run(): pl.pallas_call(kernel, name=name, grid=grid, in_specs=in_specs, out_specs...  21.2 us
    ppermute x12, starting transfers between devices, move(): return lax.ppermute(value, 'ctx', [(i, target(i)) for i in range(32)])  16.5 us
    ppermute x12, waiting for transfers between devices, move(): return lax.ppermute(value, 'ctx', [(i, target(i)) for i in range(32)])  13.9 us
    ppermute x3, starting transfers between devices, shards(): lax.ppermute(out_grad, 'head', [(i, (i + by) % HALF) for i in range(HALF)])  7.18 us
  transfers between devices with their start and end apart: 15, of which 8 were waited for; matrix products, arithmetic and copies ran while one was open for 0% of the time, Pallas kernels for 25%

profile of v4, /device:TPU:1, one launch (start us, length us, event | category | flops | bytes accessed | tf_op | source)
XLA Modules:
  0.0 59.6 jit_solution(12445481808900080205)
XLA Ops:
  0.6 0.0 copy-start
  0.6 4.5 %collective-permute-start.2 = (bf16[32,4096]{1,0:T(8,128)(2,1)}, bf16[32,4096]{1,0:T(8,128)(2,1)S(1)}, u32[]{:S(2)}, u32[]{:S(2)}) collective-permute-start(bf16[32,4096]{1,0:T(8,128)(2,1)} %o0.1), channel_id=1, source_target_pairs={{0,2},{1,3},{2,0},{3,1},{4,6},{5,7},{6,4},{7,5},{8,10},{9,11},{10,... | collective-permute-start | bytes 786440 | tf_op jit(solution)/shard_map/ppermute | solution.py:491
  5.1 0.7 %collective-permute-start.1 = (bf16[32,4096]{1,0:T(8,128)(2,1)}, bf16[32,4096]{1,0:T(8,128)(2,1)S(1)}, u32[]{:S(2)}, u32[]{:S(2)}) collective-permute-start(bf16[32,4096]{1,0:T(8,128)(2,1)} %o0.1), channel_id=1, source_target_pairs={{0,1},{1,2},{2,3},{3,0},{4,5},{5,6},{6,7},{7,4},{8,9},{9,10},{10,1... | collective-permute-start | bytes 786440 | tf_op jit(solution)/shard_map/ppermute | solution.py:491
  5.9 1.9 %collective-permute-start.3 = (bf16[32,4096]{1,0:T(8,128)(2,1)}, bf16[32,4096]{1,0:T(8,128)(2,1)S(1)}, u32[]{:S(2)}, u32[]{:S(2)}) collective-permute-start(bf16[32,4096]{1,0:T(8,128)(2,1)} %o0.1), channel_id=1, source_target_pairs={{0,3},{1,0},{2,1},{3,2},{4,7},{5,4},{6,5},{7,6},{8,11},{9,8},{10,9... | collective-permute-start | bytes 786440 | tf_op jit(solution)/shard_map/ppermute | solution.py:491
  7.8 9.9 %maps.1 = (bf16[4,128,256]{2,1,0:T(8,128)(2,1)S(1)}, bf16[4,128,256]{2,1,0:T(8,128)(2,1)S(1)}, bf16[8,2,128,128]{3,2,1,0:T(8,128)(2,1)S(1)}, bf16[8,2,128,128]{3...) custom-call(bf16[2,128,1024]{2,1,0:T(8,128)(2,1)} %k_ref.5, ...), custom_call_target="tpu_custom_call" | custom-call | flops 14000000000 | bytes 8000000 | tf_op jit(solution)/shard_map/maps/pallas_call | solution.py:432
  17.7 0.0 copy-start.1
  17.8 0.0 copy-start.3
  17.8 1.6 %collective-permute-start = (bf16[4,128,256]{2,1,0:T(8,128)(2,1)S(1)}, bf16[4,128,256]{2,1,0:T(8,128)(2,1)S(1)}, u32[]{:S(2)}, u32[]{:S(2)}) collective-permute-start(bf16[4,128,256]{2,1,0:T(8,128)(2,1)S(1)} %get-tuple-element.36), channel_id=1, source_target_pairs={{0,4},{4,0},{8,12},{12,8},{16,20},{20,16},{24,28},{28,24},{32,36},... | collective-permute-start | bytes 786440 | tf_op jit(solution)/shard_map/ppermute | solution.py:467
  19.4 0.0 collective-permute-done.2.o2
  19.4 0.0 collective-permute-done.1.o1
  19.4 0.0 collective-permute-done.3.o3
  19.4 0.0 copy-done
  19.4 3.1 %local_grad.1 = (bf16[4,128,128]{2,1,0:T(8,128)(2,1)S(1)}, bf16[4,128,128]{2,1,0:T(8,128)(2,1)S(1)}, bf16[8,128,128]{2,1,0:T(8,128)(2,1)S(1)}) custom-call(bf16[32,4096]{1,0:T(8,128)(2,1)S(1)} %copy-done, bf16[32,4096]{1,0:T(8,128)(2,1)S(1)} %collective-permute-done.1.o1, bf16[32,4096]{1,0:T(8,128)(2,1)S(1)} %collective-permute-done.2.o2, ...), custom_call_target="tpu_custom_call" | custom-call | flops 2000000000 | bytes 10000000 | tf_op jit(solution)/shard_map/local_grad/pallas_call | solution.py:432
  22.5 0.1 collective-permute-start.4
  22.6 0.0 collective-permute-done.got_ref
  22.6 1.3 %collective-permute-done.4.ggot_ref = bf16[4,128,128]{2,1,0:T(8,128)(2,1)S(1)} collective-permute-done((bf16[4,128,128]{2,1,0:T(8,128)(2,1)S(1)}, bf16[4,128,128]{2,1,0:T(8,128)(2,1)S(1)}, u32[]{:S(2)}, u32[]{:S(2)}) %collective-permute-start.4) | collective-permute-done | bytes 131104 | tf_op jit(solution)/shard_map/ppermute | solution.py:467
  23.9 0.3 pair.1
  24.2 1.3 %collective-permute-start.5 = (bf16[128,384]{1,0:T(8,128)(2,1)S(1)}, bf16[128,384]{1,0:T(8,128)(2,1)S(1)}, u32[]{:S(2)}, u32[]{:S(2)}) collective-permute-start(bf16[128,384]{1,0:T(8,128)(2,1)S(1)} %get-tuple-element.57), channel_id=1, source_target_pairs={{0,8},{4,12},{8,16},{12,20},{16,24},{20,28},{24,0},{28,4},{32,40},... | collective-permute-start | bytes 294920 | tf_op jit(solution)/shard_map/ppermute | solution.py:467
  25.5 2.5 %collective-permute-start.6 = (bf16[128,384]{1,0:T(8,128)(2,1)S(1)}, bf16[128,384]{1,0:T(8,128)(2,1)S(1)}, u32[]{:S(2)}, u32[]{:S(2)}) collective-permute-start(bf16[128,384]{1,0:T(8,128)(2,1)S(1)} %get-tuple-element.58), channel_id=1, source_target_pairs={{0,16},{4,20},{8,24},{12,28},{16,0},{20,4},{24,8},{28,12},{32,48},... | collective-permute-start | bytes 294920 | tf_op jit(solution)/shard_map/ppermute | solution.py:467
  28.0 1.1 %collective-permute-start.7 = (bf16[128,384]{1,0:T(8,128)(2,1)S(1)}, bf16[128,384]{1,0:T(8,128)(2,1)S(1)}, u32[]{:S(2)}, u32[]{:S(2)}) collective-permute-start(bf16[128,384]{1,0:T(8,128)(2,1)S(1)} %get-tuple-element.59), channel_id=1, source_target_pairs={{0,24},{4,28},{8,0},{12,4},{16,8},{20,12},{24,16},{28,20},{32,56},... | collective-permute-start | bytes 294920 | tf_op jit(solution)/shard_map/ppermute | solution.py:467
  29.1 0.0 copy-done.1
  29.1 0.0 copy-done.3
  29.1 0.0 copy-start.2
  29.1 1.7 %prep.1.u_ref = f32[8,2,128,128]{3,2,1,0:T(8,128)S(1)} custom-call(bf16[2,128,1024]{2,1,0:T(8,128)(2,1)S(1)} %copy-done.1, f32[8,2,128]{2,1,0:T(2,128)S(1)} %copy-done.3, bf16[8,128,128]{2,1,0:T(8,128)(2,1)S(1)} %get-tuple-element.44.do_ref, bf16[8,2,128,128]{3,2,1,0:T(8,128)(2,1)S(1)} %get-tuple-element.51.nh_ref, ...), custom_call_target="tpu_custom_call" | custom-call | flops 4000000000 | bytes 6000000 | tf_op jit(solution)/shard_map/prep/pallas_call | solution.py:432
  30.8 0.0 collective-permute-done.5.b_ref
  30.8 2.1 %collective-permute-done.6.c_ref = bf16[128,384]{1,0:T(8,128)(2,1)S(1)} collective-permute-done((bf16[128,384]{1,0:T(8,128)(2,1)S(1)}, bf16[128,384]{1,0:T(8,128)(2,1)S(1)}, u32[]{:S(2)}, u32[]{:S(2)}) %collective-permute-start.6) | collective-permute-done | bytes 98336 | tf_op jit(solution)/shard_map/ppermute | solution.py:467
  32.8 0.0 collective-permute-done.7.d_ref
  32.8 0.4 line.1.e_ref
  33.2 2.8 %collective-permute-start.10 = (bf16[128,384]{1,0:T(8,128)(2,1)S(1)}, bf16[128,384]{1,0:T(8,128)(2,1)S(1)}, u32[]{:S(2)}, u32[]{:S(2)}) collective-permute-start(bf16[128,384]{1,0:T(8,128)(2,1)S(1)} %line.1.e_ref), channel_id=1, source_target_pairs={{0,96},{4,100},{8,104},{12,108},{16,112},{20,116},{24,120},{28,124... | collective-permute-start | bytes 294920 | tf_op jit(solution)/shard_map/ppermute | solution.py:467
  36.0 0.3 collective-permute-start.9
  36.4 0.7 %collective-permute-start.8 = (bf16[128,384]{1,0:T(8,128)(2,1)S(1)}, bf16[128,384]{1,0:T(8,128)(2,1)S(1)}, u32[]{:S(2)}, u32[]{:S(2)}) collective-permute-start(bf16[128,384]{1,0:T(8,128)(2,1)S(1)} %line.1.e_ref), channel_id=1, source_target_pairs={{0,32},{4,36},{8,40},{12,44},{16,48},{20,52},{24,56},{28,60},{32,6... | collective-permute-start | bytes 294920 | tf_op jit(solution)/shard_map/ppermute | solution.py:467
  37.1 0.6 %collective-permute-done.10.h_ref = bf16[128,384]{1,0:T(8,128)(2,1)S(1)} collective-permute-done((bf16[128,384]{1,0:T(8,128)(2,1)S(1)}, bf16[128,384]{1,0:T(8,128)(2,1)S(1)}, u32[]{:S(2)}, u32[]{:S(2)}) %collective-permute-start.10) | collective-permute-done | bytes 98336 | tf_op jit(solution)/shard_map/ppermute | solution.py:467
  37.7 3.4 %collective-permute-done.9.g_ref = bf16[128,384]{1,0:T(8,128)(2,1)S(1)} collective-permute-done((bf16[128,384]{1,0:T(8,128)(2,1)S(1)}, bf16[128,384]{1,0:T(8,128)(2,1)S(1)}, u32[]{:S(2)}, u32[]{:S(2)}) %collective-permute-start.9) | collective-permute-done | bytes 98336 | tf_op jit(solution)/shard_map/ppermute | solution.py:467
  41.1 2.4 %collective-permute-done.8.f_ref = bf16[128,384]{1,0:T(8,128)(2,1)S(1)} collective-permute-done((bf16[128,384]{1,0:T(8,128)(2,1)S(1)}, bf16[128,384]{1,0:T(8,128)(2,1)S(1)}, u32[]{:S(2)}, u32[]{:S(2)}) %collective-permute-start.8) | collective-permute-done | bytes 98336 | tf_op jit(solution)/shard_map/ppermute | solution.py:467
  43.6 0.9 %expand.1 = (bf16[128,256]{1,0:T(8,128)(2,1)S(1)}, bf16[128,256]{1,0:T(8,128)(2,1)S(1)}, bf16[128,256]{1,0:T(8,128)(2,1)S(1)}, bf16[128,256]{1,0:T(8,128)(2,1)S(1)}) custom-call(bf16[128,384]{1,0:T(8,128)(2,1)S(1)} %get-tuple-element.56.a_ref, bf16[128,384]{1,0:T(8,128)(2,1)S(1)} %collective-permute-done.5.b_ref, ...), custom_call_target="tpu_custom_call" | custom-call | tf_op jit(solution)/shard_map/expand/pallas_call | solution.py:432
  44.5 0.1 collective-permute-start.11
  44.6 1.3 %collective-permute-start.12 = (bf16[128,256]{1,0:T(8,128)(2,1)S(1)}, bf16[128,256]{1,0:T(8,128)(2,1)S(1)}, u32[]{:S(2)}, u32[]{:S(2)}) collective-permute-start(bf16[128,256]{1,0:T(8,128)(2,1)S(1)} %get-tuple-element.62), channel_id=1, source_target_pairs={{0,16},{4,20},{8,24},{12,28},{16,0},{20,4},{24,8},{28,12},{32,48},... | collective-permute-start | bytes 196616 | tf_op jit(solution)/shard_map/ppermute | solution.py:467
  45.8 1.7 %collective-permute-start.13 = (bf16[128,256]{1,0:T(8,128)(2,1)S(1)}, bf16[128,256]{1,0:T(8,128)(2,1)S(1)}, u32[]{:S(2)}, u32[]{:S(2)}) collective-permute-start(bf16[128,256]{1,0:T(8,128)(2,1)S(1)} %get-tuple-element.63), channel_id=1, source_target_pairs={{0,24},{4,28},{8,0},{12,4},{16,8},{20,12},{24,16},{28,20},{32,56},... | collective-permute-start | bytes 196616 | tf_op jit(solution)/shard_map/ppermute | solution.py:467
  47.5 2.1 %collective-permute-done.11.b_ref = bf16[128,256]{1,0:T(8,128)(2,1)S(1)} collective-permute-done((bf16[128,256]{1,0:T(8,128)(2,1)S(1)}, bf16[128,256]{1,0:T(8,128)(2,1)S(1)}, u32[]{:S(2)}, u32[]{:S(2)}) %collective-permute-start.11) | collective-permute-done | bytes 65568 | tf_op jit(solution)/shard_map/ppermute | solution.py:467
  49.6 0.0 collective-permute-done.12.c_ref
  49.6 0.9 %collective-permute-done.13.d_ref = bf16[128,256]{1,0:T(8,128)(2,1)S(1)} collective-permute-done((bf16[128,256]{1,0:T(8,128)(2,1)S(1)}, bf16[128,256]{1,0:T(8,128)(2,1)S(1)}, u32[]{:S(2)}, u32[]{:S(2)}) %collective-permute-start.13) | collective-permute-done | bytes 65568 | tf_op jit(solution)/shard_map/ppermute | solution.py:467
  50.5 0.3 down.1
  50.8 3.1 %collective-permute-start.14 = (bf16[4,128,256]{2,1,0:T(8,128)(2,1)S(1)}, bf16[4,128,256]{2,1,0:T(8,128)(2,1)S(1)}, u32[]{:S(2)}, u32[]{:S(2)}) collective-permute-start(bf16[4,128,256]{2,1,0:T(8,128)(2,1)S(1)} %get-tuple-element.65), channel_id=1, source_target_pairs={{0,4},{4,0},{8,12},{12,8},{16,20},{20,16},{24,28},{28,24},{32,36},... | collective-permute-start | bytes 786440 | tf_op jit(solution)/shard_map/ppermute | solution.py:467
  53.9 1.2 %collective-permute-done.14.got_ref = bf16[4,128,256]{2,1,0:T(8,128)(2,1)S(1)} collective-permute-done((bf16[4,128,256]{2,1,0:T(8,128)(2,1)S(1)}, bf16[4,128,256]{2,1,0:T(8,128)(2,1)S(1)}, u32[]{:S(2)}, u32[]{:S(2)}) %collective-permute-start.14) | collective-permute-done | bytes 262176 | tf_op jit(solution)/shard_map/ppermute | solution.py:467
  55.0 0.0 copy-done.2
  55.0 4.6 %grads.1 = (bf16[128,1024]{1,0:T(8,128)(2,1)}, bf16[2,128,1024]{2,1,0:T(8,128)(2,1)}, bf16[2,128,1024]{2,1,0:T(8,128)(2,1)}, f32[8,2,128]{2,1,0:T(2,128)}) custom-call(bf16[2,128,1024]{2,1,0:T(8,128)(2,1)S(1)} %copy-done.1, bf16[128,1024]{1,0:T(8,128)(2,1)S(1)} %copy-done.2, f32[8,2,128]{2,1,0:T(2,128)S(1)} %copy-done.3, ...), custom_call_target="tpu_custom_call" | custom-call | flops 8000000000 | bytes 14000000 | tf_op jit(solution)/shard_map/grads/pallas_call | solution.py:432
Async XLA Ops:
  0.6 18.7 %copy-start = (bf16[32,4096]{1,0:T(8,128)(2,1)S(1)}, bf16[32,4096]{1,0:T(8,128)(2,1)}, u32[]{:S(2)}) copy-start(bf16[32,4096]{1,0:T(8,128)(2,1)} %o0.1) | copy-start | bytes 786436
  0.6 18.7 %collective-permute-start.2 = (bf16[32,4096]{1,0:T(8,128)(2,1)}, bf16[32,4096]{1,0:T(8,128)(2,1)S(1)}, u32[]{:S(2)}, u32[]{:S(2)}) collective-permute-start(bf16[32,4096]{1,0:T(8,128)(2,1)} %o0.1), channel_id=1, source_target_pairs={{0,2},{1,3},{2,0},{3,1},{4,6},{5,7},{6,4},{7,5},{8,10},{9,11},{10,... | collective-permute-start | bytes 786440 | tf_op jit(solution)/shard_map/ppermute | solution.py:491
  5.1 14.2 %collective-permute-start.1 = (bf16[32,4096]{1,0:T(8,128)(2,1)}, bf16[32,4096]{1,0:T(8,128)(2,1)S(1)}, u32[]{:S(2)}, u32[]{:S(2)}) collective-permute-start(bf16[32,4096]{1,0:T(8,128)(2,1)} %o0.1), channel_id=1, source_target_pairs={{0,1},{1,2},{2,3},{3,0},{4,5},{5,6},{6,7},{7,4},{8,9},{9,10},{10,1... | collective-permute-start | bytes 786440 | tf_op jit(solution)/shard_map/ppermute | solution.py:491
  5.9 13.5 %collective-permute-start.3 = (bf16[32,4096]{1,0:T(8,128)(2,1)}, bf16[32,4096]{1,0:T(8,128)(2,1)S(1)}, u32[]{:S(2)}, u32[]{:S(2)}) collective-permute-start(bf16[32,4096]{1,0:T(8,128)(2,1)} %o0.1), channel_id=1, source_target_pairs={{0,3},{1,0},{2,1},{3,2},{4,7},{5,4},{6,5},{7,6},{8,11},{9,8},{10,9... | collective-permute-start | bytes 786440 | tf_op jit(solution)/shard_map/ppermute | solution.py:491
  17.7 11.4 %copy-start.1 = (bf16[2,128,1024]{2,1,0:T(8,128)(2,1)S(1)}, bf16[2,128,1024]{2,1,0:T(8,128)(2,1)}, u32[]{:S(2)}) copy-start(bf16[2,128,1024]{2,1,0:T(8,128)(2,1)} %k_ref.5) | copy-start | bytes 1572868
  17.8 11.4 %copy-start.3 = (f32[8,2,128]{2,1,0:T(2,128)S(1)}, f32[8,2,128]{2,1,0:T(2,128)}, u32[]{:S(2)}) copy-start(f32[8,2,128]{2,1,0:T(2,128)} %b_ref.5) | copy-start | bytes 24580
  17.8 4.8 %collective-permute-start = (bf16[4,128,256]{2,1,0:T(8,128)(2,1)S(1)}, bf16[4,128,256]{2,1,0:T(8,128)(2,1)S(1)}, u32[]{:S(2)}, u32[]{:S(2)}) collective-permute-start(bf16[4,128,256]{2,1,0:T(8,128)(2,1)S(1)} %get-tuple-element.36), channel_id=1, source_target_pairs={{0,4},{4,0},{8,12},{12,8},{16,20},{20,16},{24,28},{28,24},{32,36},... | collective-permute-start | bytes 786440 | tf_op jit(solution)/shard_map/ppermute | solution.py:467
  22.5 1.4 %collective-permute-start.4 = (bf16[4,128,128]{2,1,0:T(8,128)(2,1)S(1)}, bf16[4,128,128]{2,1,0:T(8,128)(2,1)S(1)}, u32[]{:S(2)}, u32[]{:S(2)}) collective-permute-start(bf16[4,128,128]{2,1,0:T(8,128)(2,1)S(1)} %get-tuple-element.41), channel_id=1, source_target_pairs={{0,4},{4,0},{8,12},{12,8},{16,20},{20,16},{24,28},{28,24},{32,36},... | collective-permute-start | bytes 393224 | tf_op jit(solution)/shard_map/ppermute | solution.py:467
  24.2 6.6 %collective-permute-start.5 = (bf16[128,384]{1,0:T(8,128)(2,1)S(1)}, bf16[128,384]{1,0:T(8,128)(2,1)S(1)}, u32[]{:S(2)}, u32[]{:S(2)}) collective-permute-start(bf16[128,384]{1,0:T(8,128)(2,1)S(1)} %get-tuple-element.57), channel_id=1, source_target_pairs={{0,8},{4,12},{8,16},{12,20},{16,24},{20,28},{24,0},{28,4},{32,40},... | collective-permute-start | bytes 294920 | tf_op jit(solution)/shard_map/ppermute | solution.py:467
  25.5 7.3 %collective-permute-start.6 = (bf16[128,384]{1,0:T(8,128)(2,1)S(1)}, bf16[128,384]{1,0:T(8,128)(2,1)S(1)}, u32[]{:S(2)}, u32[]{:S(2)}) collective-permute-start(bf16[128,384]{1,0:T(8,128)(2,1)S(1)} %get-tuple-element.58), channel_id=1, source_target_pairs={{0,16},{4,20},{8,24},{12,28},{16,0},{20,4},{24,8},{28,12},{32,48},... | collective-permute-start | bytes 294920 | tf_op jit(solution)/shard_map/ppermute | solution.py:467
  28.0 4.9 %collective-permute-start.7 = (bf16[128,384]{1,0:T(8,128)(2,1)S(1)}, bf16[128,384]{1,0:T(8,128)(2,1)S(1)}, u32[]{:S(2)}, u32[]{:S(2)}) collective-permute-start(bf16[128,384]{1,0:T(8,128)(2,1)S(1)} %get-tuple-element.59), channel_id=1, source_target_pairs={{0,24},{4,28},{8,0},{12,4},{16,8},{20,12},{24,16},{28,20},{32,56},... | collective-permute-start | bytes 294920 | tf_op jit(solution)/shard_map/ppermute | solution.py:467
  29.1 25.9 %copy-start.2 = (bf16[128,1024]{1,0:T(8,128)(2,1)S(1)}, bf16[128,1024]{1,0:T(8,128)(2,1)}, u32[]{:S(2)}) copy-start(bf16[128,1024]{1,0:T(8,128)(2,1)} %q_ref.3) | copy-start | bytes 786436
  33.2 4.4 %collective-permute-start.10 = (bf16[128,384]{1,0:T(8,128)(2,1)S(1)}, bf16[128,384]{1,0:T(8,128)(2,1)S(1)}, u32[]{:S(2)}, u32[]{:S(2)}) collective-permute-start(bf16[128,384]{1,0:T(8,128)(2,1)S(1)} %line.1.e_ref), channel_id=1, source_target_pairs={{0,96},{4,100},{8,104},{12,108},{16,112},{20,116},{24,120},{28,124... | collective-permute-start | bytes 294920 | tf_op jit(solution)/shard_map/ppermute | solution.py:467
  36.0 5.1 %collective-permute-start.9 = (bf16[128,384]{1,0:T(8,128)(2,1)S(1)}, bf16[128,384]{1,0:T(8,128)(2,1)S(1)}, u32[]{:S(2)}, u32[]{:S(2)}) collective-permute-start(bf16[128,384]{1,0:T(8,128)(2,1)S(1)} %line.1.e_ref), channel_id=1, source_target_pairs={{0,64},{4,68},{8,72},{12,76},{16,80},{20,84},{24,88},{28,92},{32,9... | collective-permute-start | bytes 294920 | tf_op jit(solution)/shard_map/ppermute | solution.py:467
  36.4 7.2 %collective-permute-start.8 = (bf16[128,384]{1,0:T(8,128)(2,1)S(1)}, bf16[128,384]{1,0:T(8,128)(2,1)S(1)}, u32[]{:S(2)}, u32[]{:S(2)}) collective-permute-start(bf16[128,384]{1,0:T(8,128)(2,1)S(1)} %line.1.e_ref), channel_id=1, source_target_pairs={{0,32},{4,36},{8,40},{12,44},{16,48},{20,52},{24,56},{28,60},{32,6... | collective-permute-start | bytes 294920 | tf_op jit(solution)/shard_map/ppermute | solution.py:467
  44.5 5.1 %collective-permute-start.11 = (bf16[128,256]{1,0:T(8,128)(2,1)S(1)}, bf16[128,256]{1,0:T(8,128)(2,1)S(1)}, u32[]{:S(2)}, u32[]{:S(2)}) collective-permute-start(bf16[128,256]{1,0:T(8,128)(2,1)S(1)} %get-tuple-element.61), channel_id=1, source_target_pairs={{0,8},{4,12},{8,16},{12,20},{16,24},{20,28},{24,0},{28,4},{32,40},... | collective-permute-start | bytes 196616 | tf_op jit(solution)/shard_map/ppermute | solution.py:467
  44.6 5.0 %collective-permute-start.12 = (bf16[128,256]{1,0:T(8,128)(2,1)S(1)}, bf16[128,256]{1,0:T(8,128)(2,1)S(1)}, u32[]{:S(2)}, u32[]{:S(2)}) collective-permute-start(bf16[128,256]{1,0:T(8,128)(2,1)S(1)} %get-tuple-element.62), channel_id=1, source_target_pairs={{0,16},{4,20},{8,24},{12,28},{16,0},{20,4},{24,8},{28,12},{32,48},... | collective-permute-start | bytes 196616 | tf_op jit(solution)/shard_map/ppermute | solution.py:467
  45.8 4.6 %collective-permute-start.13 = (bf16[128,256]{1,0:T(8,128)(2,1)S(1)}, bf16[128,256]{1,0:T(8,128)(2,1)S(1)}, u32[]{:S(2)}, u32[]{:S(2)}) collective-permute-start(bf16[128,256]{1,0:T(8,128)(2,1)S(1)} %get-tuple-element.63), channel_id=1, source_target_pairs={{0,24},{4,28},{8,0},{12,4},{16,8},{20,12},{24,16},{28,20},{32,56},... | collective-permute-start | bytes 196616 | tf_op jit(solution)/shard_map/ppermute | solution.py:467
  50.8 4.3 %collective-permute-start.14 = (bf16[4,128,256]{2,1,0:T(8,128)(2,1)S(1)}, bf16[4,128,256]{2,1,0:T(8,128)(2,1)S(1)}, u32[]{:S(2)}, u32[]{:S(2)}) collective-permute-start(bf16[4,128,256]{2,1,0:T(8,128)(2,1)S(1)} %get-tuple-element.65), channel_id=1, source_target_pairs={{0,4},{4,0},{8,12},{12,8},{16,20},{20,16},{24,28},{28,24},{32,36},... | collective-permute-start | bytes 786440 | tf_op jit(solution)/shard_map/ppermute | solution.py:467

commit v5 on v4

--- a/solution.py
+++ b/solution.py
@@ -281,10 +281,14 @@
         slots[lax.rem(spot + HALF - shift, HALF)] = refs[shift][...]
 
 
-def row_kernel(a_ref, b_ref, c_ref, d_ref, out_ref, slots):
+def row_kernel(a_ref, b_ref, c_ref, d_ref, o1, o2, o3, slots):
     gather_slots(slots, (a_ref, b_ref, c_ref, d_ref), here()[1])
     maps = [slots[i].astype(f32) for i in range(HALF)]
-    out_ref[...] = join(join(maps[0], maps[1]), join(maps[2], maps[3])).astype(bf16)
+    joined = join(join(maps[0], maps[1]), join(maps[2], maps[3]))
+    for shift, out in enumerate((o1, o2, o3)):
+        later = here()[2] + shift + 1 < HALF
+        out[:, :WIDTH] = joined[:, :WIDTH].astype(bf16)
+        out[:, WIDTH:] = jnp.where(later, joined[:, WIDTH : 2 * WIDTH], joined[:, 2 * WIDTH :]).astype(bf16)
 
 
 def advance(block, state):
@@ -296,15 +300,17 @@
 def retreat(block, grad):
     high, low = split(grad)
     moved = tn(block[:, :WIDTH], jnp.concatenate([high, low], axis=1))
-    return grad - moved[:, :WIDTH] - moved[:, WIDTH:] + block[:, 2 * WIDTH :].astype(f32)
-
-
-def expand_kernel(a_ref, b_ref, c_ref, d_ref, e_ref, f_ref, g_ref, h_ref, o0, o1, o2, o3, chips, lines, found):
+    return grad - moved[:, :WIDTH] - moved[:, WIDTH:] + block[:, block.shape[1] - WIDTH :].astype(f32)
+
+
+def expand_kernel(a_ref, b_ref, c_ref, d_ref, f_ref, g_ref, h_ref, o0, o1, o2, o3, chips, lines, found):
     unused, spot, line = here()
     gather_slots(chips, (a_ref, b_ref, c_ref, d_ref), spot)
-    gather_slots(lines, (e_ref, f_ref, g_ref, h_ref), line)
+    for shift, ref in enumerate((f_ref, g_ref, h_ref)):
+        lines[lax.rem(line + HALF - 1 - shift, HALF)] = ref[...]
+    lines[line] = jnp.zeros((WIDTH, 2 * WIDTH), bf16)
     state = jnp.where(line > 0, lines[0, :, WIDTH : 2 * WIDTH].astype(f32), 0.0)
-    grad = jnp.where(line < HALF - 1, lines[HALF - 1, :, 2 * WIDTH :].astype(f32), 0.0)
+    grad = jnp.where(line < HALF - 1, lines[HALF - 1, :, WIDTH:].astype(f32), 0.0)
     for i in range(1, HALF - 1):
         state = jnp.where(i < line, advance(lines[i], state), state)
         back = HALF - 1 - i
@@ -539,11 +545,11 @@
     chip = [chip[0]] + [move(chip[by], along_x(by)) for by in range(1, HALF)]
     chip[0], reached = lax.optimization_barrier((chip[0], reached))
     slots = pltpu.VMEM((HALF, WIDTH, 3 * WIDTH), bf16)
-    (line,) = small(row_kernel, "line", chip, [map_shape], [slots])
-    lines = [line] + [move(line, along_y(by)) for by in range(1, HALF)]
     ends_shape = ((WIDTH, 2 * WIDTH), bf16)
+    line = small(row_kernel, "line", chip, [ends_shape] * (HALF - 1), [slots])
+    lines = [move(line[by - 1], along_y(by)) for by in range(1, HALF)]
     ends_slots = pltpu.VMEM((HALF, WIDTH, 2 * WIDTH), bf16)
-    ends = small(expand_kernel, "expand", chip + lines, [ends_shape] * HALF, [slots, slots, ends_slots])
+    ends = small(expand_kernel, "expand", chip + lines, [ends_shape] * HALF, [slots, ends_slots, ends_slots])
     ends = [ends[0]] + [move(ends[by], along_x(by)) for by in range(1, HALF)]
     own, passed = small(
         down_kernel, "down", ends + [keep, got, gkeep, ggot],

time: 59.8 us -> 58.3 us (0.975)
  waiting for transfers between devices: 13.9 us -> 9.29 us
  starting transfers between devices: 23.7 us -> 26.9 us
    ppermute x12, waiting for transfers between devices: 13.9 us -> 9.29 us  [move(): return lax.ppermute(value, 'ctx', [(i, target(i)) for i in range(32)])]
    ppermute x12, starting transfers between devices: 16.5 us -> 19.7 us  [move(): return lax.ppermute(value, 'ctx', [(i, target(i)) for i in range(32)])]
  transfers between devices with their start and end apart: 15 -> 15, of which waited for: 8 -> 7; matrix products, arithmetic and copies ran while one was open for 0% -> 0% of each run, Pallas kernels for 25% -> 25%
where the time goes in v5:
time: 58.3 us; the launch traced here: 58.1 us
  starting transfers between devices  26.9 us (46%)
  Pallas kernels  21.2 us (36%)
  waiting for transfers between devices  9.29 us (16%)
  between operations  0.74 us (1%)
    pallas_call x8, Pallas kernels, run(): pl.pallas_call(kernel, name=name, grid=grid, in_specs=in_specs, out_specs...  21.2 us
    ppermute x12, starting transfers between devices, move(): return lax.ppermute(value, 'ctx', [(i, target(i)) for i in range(32)])  19.7 us
    ppermute x12, waiting for transfers between devices, move(): return lax.ppermute(value, 'ctx', [(i, target(i)) for i in range(32)])  9.29 us
    ppermute x3, starting transfers between devices, shards(): lax.ppermute(out_grad, 'head', [(i, (i + by) % HALF) for i in range(HALF)])  7.18 us
  transfers between devices with their start and end apart: 15, of which 7 were waited for; matrix products, arithmetic and copies ran while one was open for 0% of the time, Pallas kernels for 25%

profile of v5, /device:TPU:1, one launch (start us, length us, event | category | flops | bytes accessed | tf_op | source)
XLA Modules:
  0.0 58.1 jit_solution(6099123564140889146)
XLA Ops:
  0.6 0.0 copy-start
  0.6 4.5 %collective-permute-start.2 = (bf16[32,4096]{1,0:T(8,128)(2,1)}, bf16[32,4096]{1,0:T(8,128)(2,1)S(1)}, u32[]{:S(2)}, u32[]{:S(2)}) collective-permute-start(bf16[32,4096]{1,0:T(8,128)(2,1)} %o0.1), channel_id=1, source_target_pairs={{0,2},{1,3},{2,0},{3,1},{4,6},{5,7},{6,4},{7,5},{8,10},{9,11},{10,... | collective-permute-start | bytes 786440 | tf_op jit(solution)/shard_map/ppermute | solution.py:497
  5.1 0.7 %collective-permute-start.1 = (bf16[32,4096]{1,0:T(8,128)(2,1)}, bf16[32,4096]{1,0:T(8,128)(2,1)S(1)}, u32[]{:S(2)}, u32[]{:S(2)}) collective-permute-start(bf16[32,4096]{1,0:T(8,128)(2,1)} %o0.1), channel_id=1, source_target_pairs={{0,1},{1,2},{2,3},{3,0},{4,5},{5,6},{6,7},{7,4},{8,9},{9,10},{10,1... | collective-permute-start | bytes 786440 | tf_op jit(solution)/shard_map/ppermute | solution.py:497
  5.9 1.9 %collective-permute-start.3 = (bf16[32,4096]{1,0:T(8,128)(2,1)}, bf16[32,4096]{1,0:T(8,128)(2,1)S(1)}, u32[]{:S(2)}, u32[]{:S(2)}) collective-permute-start(bf16[32,4096]{1,0:T(8,128)(2,1)} %o0.1), channel_id=1, source_target_pairs={{0,3},{1,0},{2,1},{3,2},{4,7},{5,4},{6,5},{7,6},{8,11},{9,8},{10,9... | collective-permute-start | bytes 786440 | tf_op jit(solution)/shard_map/ppermute | solution.py:497
  7.8 9.9 %maps.1 = (bf16[4,128,256]{2,1,0:T(8,128)(2,1)S(1)}, bf16[4,128,256]{2,1,0:T(8,128)(2,1)S(1)}, bf16[8,2,128,128]{3,2,1,0:T(8,128)(2,1)S(1)}, bf16[8,2,128,128]{3...) custom-call(bf16[2,128,1024]{2,1,0:T(8,128)(2,1)} %k_ref.5, ...), custom_call_target="tpu_custom_call" | custom-call | flops 14000000000 | bytes 8000000 | tf_op jit(solution)/shard_map/maps/pallas_call | solution.py:438
  17.7 0.0 copy-start.1
  17.8 0.0 copy-start.3
  17.8 1.6 %collective-permute-start = (bf16[4,128,256]{2,1,0:T(8,128)(2,1)S(1)}, bf16[4,128,256]{2,1,0:T(8,128)(2,1)S(1)}, u32[]{:S(2)}, u32[]{:S(2)}) collective-permute-start(bf16[4,128,256]{2,1,0:T(8,128)(2,1)S(1)} %get-tuple-element.39), channel_id=1, source_target_pairs={{0,4},{4,0},{8,12},{12,8},{16,20},{20,16},{24,28},{28,24},{32,36},... | collective-permute-start | bytes 786440 | tf_op jit(solution)/shard_map/ppermute | solution.py:473
  19.4 0.0 collective-permute-done.2.o2
  19.4 0.0 collective-permute-done.1.o1
  19.4 0.0 collective-permute-done.3.o3
  19.4 0.0 copy-done
  19.4 3.1 %local_grad.1 = (bf16[4,128,128]{2,1,0:T(8,128)(2,1)S(1)}, bf16[4,128,128]{2,1,0:T(8,128)(2,1)S(1)}, bf16[8,128,128]{2,1,0:T(8,128)(2,1)S(1)}) custom-call(bf16[32,4096]{1,0:T(8,128)(2,1)S(1)} %copy-done, bf16[32,4096]{1,0:T(8,128)(2,1)S(1)} %collective-permute-done.1.o1, bf16[32,4096]{1,0:T(8,128)(2,1)S(1)} %collective-permute-done.2.o2, ...), custom_call_target="tpu_custom_call" | custom-call | flops 2000000000 | bytes 10000000 | tf_op jit(solution)/shard_map/local_grad/pallas_call | solution.py:438
  22.5 0.1 collective-permute-start.4
  22.6 0.0 collective-permute-done.got_ref
  22.6 1.3 %collective-permute-done.4.ggot_ref = bf16[4,128,128]{2,1,0:T(8,128)(2,1)S(1)} collective-permute-done((bf16[4,128,128]{2,1,0:T(8,128)(2,1)S(1)}, bf16[4,128,128]{2,1,0:T(8,128)(2,1)S(1)}, u32[]{:S(2)}, u32[]{:S(2)}) %collective-permute-start.4) | collective-permute-done | bytes 131104 | tf_op jit(solution)/shard_map/ppermute | solution.py:473
  23.9 0.3 pair.1
  24.2 1.3 %collective-permute-start.5 = (bf16[128,384]{1,0:T(8,128)(2,1)S(1)}, bf16[128,384]{1,0:T(8,128)(2,1)S(1)}, u32[]{:S(2)}, u32[]{:S(2)}) collective-permute-start(bf16[128,384]{1,0:T(8,128)(2,1)S(1)} %get-tuple-element.60), channel_id=1, source_target_pairs={{0,8},{4,12},{8,16},{12,20},{16,24},{20,28},{24,0},{28,4},{32,40},... | collective-permute-start | bytes 294920 | tf_op jit(solution)/shard_map/ppermute | solution.py:473
  25.5 2.5 %collective-permute-start.6 = (bf16[128,384]{1,0:T(8,128)(2,1)S(1)}, bf16[128,384]{1,0:T(8,128)(2,1)S(1)}, u32[]{:S(2)}, u32[]{:S(2)}) collective-permute-start(bf16[128,384]{1,0:T(8,128)(2,1)S(1)} %get-tuple-element.61), channel_id=1, source_target_pairs={{0,16},{4,20},{8,24},{12,28},{16,0},{20,4},{24,8},{28,12},{32,48},... | collective-permute-start | bytes 294920 | tf_op jit(solution)/shard_map/ppermute | solution.py:473
  28.0 1.1 %collective-permute-start.7 = (bf16[128,384]{1,0:T(8,128)(2,1)S(1)}, bf16[128,384]{1,0:T(8,128)(2,1)S(1)}, u32[]{:S(2)}, u32[]{:S(2)}) collective-permute-start(bf16[128,384]{1,0:T(8,128)(2,1)S(1)} %get-tuple-element.62), channel_id=1, source_target_pairs={{0,24},{4,28},{8,0},{12,4},{16,8},{20,12},{24,16},{28,20},{32,56},... | collective-permute-start | bytes 294920 | tf_op jit(solution)/shard_map/ppermute | solution.py:473
  29.1 0.0 copy-done.1
  29.1 0.0 copy-done.3
  29.1 0.0 copy-start.2
  29.1 1.7 %prep.1.u_ref = f32[8,2,128,128]{3,2,1,0:T(8,128)S(1)} custom-call(bf16[2,128,1024]{2,1,0:T(8,128)(2,1)S(1)} %copy-done.1, f32[8,2,128]{2,1,0:T(2,128)S(1)} %copy-done.3, bf16[8,128,128]{2,1,0:T(8,128)(2,1)S(1)} %get-tuple-element.47.do_ref, bf16[8,2,128,128]{3,2,1,0:T(8,128)(2,1)S(1)} %get-tuple-element.54.nh_ref, ...), custom_call_target="tpu_custom_call" | custom-call | flops 4000000000 | bytes 6000000 | tf_op jit(solution)/shard_map/prep/pallas_call | solution.py:438
  30.8 0.0 collective-permute-done.5.b_ref
  30.8 2.1 %collective-permute-done.6.c_ref = bf16[128,384]{1,0:T(8,128)(2,1)S(1)} collective-permute-done((bf16[128,384]{1,0:T(8,128)(2,1)S(1)}, bf16[128,384]{1,0:T(8,128)(2,1)S(1)}, u32[]{:S(2)}, u32[]{:S(2)}) %collective-permute-start.6) | collective-permute-done | bytes 98336 | tf_op jit(solution)/shard_map/ppermute | solution.py:473
  32.8 0.0 collective-permute-done.7.d_ref
  32.8 0.4 line.1
  33.3 1.4 %collective-permute-start.8 = (bf16[128,256]{1,0:T(8,128)(2,1)S(1)}, bf16[128,256]{1,0:T(8,128)(2,1)S(1)}, u32[]{:S(2)}, u32[]{:S(2)}) collective-permute-start(bf16[128,256]{1,0:T(8,128)(2,1)S(1)} %get-tuple-element.63), channel_id=1, source_target_pairs={{0,32},{4,36},{8,40},{12,44},{16,48},{20,52},{24,56},{28,60},{32,6... | collective-permute-start | bytes 196616 | tf_op jit(solution)/shard_map/ppermute | solution.py:473
  34.6 2.6 %collective-permute-start.9 = (bf16[128,256]{1,0:T(8,128)(2,1)S(1)}, bf16[128,256]{1,0:T(8,128)(2,1)S(1)}, u32[]{:S(2)}, u32[]{:S(2)}) collective-permute-start(bf16[128,256]{1,0:T(8,128)(2,1)S(1)} %get-tuple-element.64), channel_id=1, source_target_pairs={{0,64},{4,68},{8,72},{12,76},{16,80},{20,84},{24,88},{28,92},{32,9... | collective-permute-start | bytes 196616 | tf_op jit(solution)/shard_map/ppermute | solution.py:473
  37.2 1.1 %collective-permute-start.10 = (bf16[128,256]{1,0:T(8,128)(2,1)S(1)}, bf16[128,256]{1,0:T(8,128)(2,1)S(1)}, u32[]{:S(2)}, u32[]{:S(2)}) collective-permute-start(bf16[128,256]{1,0:T(8,128)(2,1)S(1)} %get-tuple-element.65), channel_id=1, source_target_pairs={{0,96},{4,100},{8,104},{12,108},{16,112},{20,116},{24,120},{28,124... | collective-permute-start | bytes 196616 | tf_op jit(solution)/shard_map/ppermute | solution.py:473
  38.3 0.0 collective-permute-done.8.f_ref
  38.3 1.4 %collective-permute-done.9.g_ref = bf16[128,256]{1,0:T(8,128)(2,1)S(1)} collective-permute-done((bf16[128,256]{1,0:T(8,128)(2,1)S(1)}, bf16[128,256]{1,0:T(8,128)(2,1)S(1)}, u32[]{:S(2)}, u32[]{:S(2)}) %collective-permute-start.9) | collective-permute-done | bytes 65568 | tf_op jit(solution)/shard_map/ppermute | solution.py:473
  39.7 1.2 %collective-permute-done.10.h_ref = bf16[128,256]{1,0:T(8,128)(2,1)S(1)} collective-permute-done((bf16[128,256]{1,0:T(8,128)(2,1)S(1)}, bf16[128,256]{1,0:T(8,128)(2,1)S(1)}, u32[]{:S(2)}, u32[]{:S(2)}) %collective-permute-start.10) | collective-permute-done | bytes 65568 | tf_op jit(solution)/shard_map/ppermute | solution.py:473
  40.9 0.9 %expand.1 = (bf16[128,256]{1,0:T(8,128)(2,1)S(1)}, bf16[128,256]{1,0:T(8,128)(2,1)S(1)}, bf16[128,256]{1,0:T(8,128)(2,1)S(1)}, bf16[128,256]{1,0:T(8,128)(2,1)S(1)}) custom-call(bf16[128,384]{1,0:T(8,128)(2,1)S(1)} %get-tuple-element.59.a_ref, bf16[128,384]{1,0:T(8,128)(2,1)S(1)} %collective-permute-done.5.b_ref, ...), custom_call_target="tpu_custom_call" | custom-call | tf_op jit(solution)/shard_map/expand/pallas_call | solution.py:438
  41.8 0.9 %collective-permute-start.11 = (bf16[128,256]{1,0:T(8,128)(2,1)S(1)}, bf16[128,256]{1,0:T(8,128)(2,1)S(1)}, u32[]{:S(2)}, u32[]{:S(2)}) collective-permute-start(bf16[128,256]{1,0:T(8,128)(2,1)S(1)} %get-tuple-element.67), channel_id=1, source_target_pairs={{0,8},{4,12},{8,16},{12,20},{16,24},{20,28},{24,0},{28,4},{32,40},... | collective-permute-start | bytes 196616 | tf_op jit(solution)/shard_map/ppermute | solution.py:473
  42.7 2.4 %collective-permute-start.12 = (bf16[128,256]{1,0:T(8,128)(2,1)S(1)}, bf16[128,256]{1,0:T(8,128)(2,1)S(1)}, u32[]{:S(2)}, u32[]{:S(2)}) collective-permute-start(bf16[128,256]{1,0:T(8,128)(2,1)S(1)} %get-tuple-element.68), channel_id=1, source_target_pairs={{0,16},{4,20},{8,24},{12,28},{16,0},{20,4},{24,8},{28,12},{32,48},... | collective-permute-start | bytes 196616 | tf_op jit(solution)/shard_map/ppermute | solution.py:473
  45.1 1.3 %collective-permute-start.13 = (bf16[128,256]{1,0:T(8,128)(2,1)S(1)}, bf16[128,256]{1,0:T(8,128)(2,1)S(1)}, u32[]{:S(2)}, u32[]{:S(2)}) collective-permute-start(bf16[128,256]{1,0:T(8,128)(2,1)S(1)} %get-tuple-element.69), channel_id=1, source_target_pairs={{0,24},{4,28},{8,0},{12,4},{16,8},{20,12},{24,16},{28,20},{32,56},... | collective-permute-start | bytes 196616 | tf_op jit(solution)/shard_map/ppermute | solution.py:473
  46.4 0.0 collective-permute-done.11.b_ref
  46.4 1.1 %collective-permute-done.12.c_ref = bf16[128,256]{1,0:T(8,128)(2,1)S(1)} collective-permute-done((bf16[128,256]{1,0:T(8,128)(2,1)S(1)}, bf16[128,256]{1,0:T(8,128)(2,1)S(1)}, u32[]{:S(2)}, u32[]{:S(2)}) %collective-permute-start.12) | collective-permute-done | bytes 65568 | tf_op jit(solution)/shard_map/ppermute | solution.py:473
  47.4 1.1 %collective-permute-done.13.d_ref = bf16[128,256]{1,0:T(8,128)(2,1)S(1)} collective-permute-done((bf16[128,256]{1,0:T(8,128)(2,1)S(1)}, bf16[128,256]{1,0:T(8,128)(2,1)S(1)}, u32[]{:S(2)}, u32[]{:S(2)}) %collective-permute-start.13) | collective-permute-done | bytes 65568 | tf_op jit(solution)/shard_map/ppermute | solution.py:473
  48.5 0.3 down.1
  48.8 3.6 %collective-permute-start.14 = (bf16[4,128,256]{2,1,0:T(8,128)(2,1)S(1)}, bf16[4,128,256]{2,1,0:T(8,128)(2,1)S(1)}, u32[]{:S(2)}, u32[]{:S(2)}) collective-permute-start(bf16[4,128,256]{2,1,0:T(8,128)(2,1)S(1)} %get-tuple-element.71), channel_id=1, source_target_pairs={{0,4},{4,0},{8,12},{12,8},{16,20},{20,16},{24,28},{28,24},{32,36},... | collective-permute-start | bytes 786440 | tf_op jit(solution)/shard_map/ppermute | solution.py:473
  52.4 1.2 %collective-permute-done.14.got_ref = bf16[4,128,256]{2,1,0:T(8,128)(2,1)S(1)} collective-permute-done((bf16[4,128,256]{2,1,0:T(8,128)(2,1)S(1)}, bf16[4,128,256]{2,1,0:T(8,128)(2,1)S(1)}, u32[]{:S(2)}, u32[]{:S(2)}) %collective-permute-start.14) | collective-permute-done | bytes 262176 | tf_op jit(solution)/shard_map/ppermute | solution.py:473
  53.5 0.0 copy-done.2
  53.6 4.6 %grads.1 = (bf16[128,1024]{1,0:T(8,128)(2,1)}, bf16[2,128,1024]{2,1,0:T(8,128)(2,1)}, bf16[2,128,1024]{2,1,0:T(8,128)(2,1)}, f32[8,2,128]{2,1,0:T(2,128)}) custom-call(bf16[2,128,1024]{2,1,0:T(8,128)(2,1)S(1)} %copy-done.1, bf16[128,1024]{1,0:T(8,128)(2,1)S(1)} %copy-done.2, f32[8,2,128]{2,1,0:T(2,128)S(1)} %copy-done.3, ...), custom_call_target="tpu_custom_call" | custom-call | flops 8000000000 | bytes 14000000 | tf_op jit(solution)/shard_map/grads/pallas_call | solution.py:438
Async XLA Ops:
  0.6 18.7 %copy-start = (bf16[32,4096]{1,0:T(8,128)(2,1)S(1)}, bf16[32,4096]{1,0:T(8,128)(2,1)}, u32[]{:S(2)}) copy-start(bf16[32,4096]{1,0:T(8,128)(2,1)} %o0.1) | copy-start | bytes 786436
  0.6 18.7 %collective-permute-start.2 = (bf16[32,4096]{1,0:T(8,128)(2,1)}, bf16[32,4096]{1,0:T(8,128)(2,1)S(1)}, u32[]{:S(2)}, u32[]{:S(2)}) collective-permute-start(bf16[32,4096]{1,0:T(8,128)(2,1)} %o0.1), channel_id=1, source_target_pairs={{0,2},{1,3},{2,0},{3,1},{4,6},{5,7},{6,4},{7,5},{8,10},{9,11},{10,... | collective-permute-start | bytes 786440 | tf_op jit(solution)/shard_map/ppermute | solution.py:497
  5.1 14.2 %collective-permute-start.1 = (bf16[32,4096]{1,0:T(8,128)(2,1)}, bf16[32,4096]{1,0:T(8,128)(2,1)S(1)}, u32[]{:S(2)}, u32[]{:S(2)}) collective-permute-start(bf16[32,4096]{1,0:T(8,128)(2,1)} %o0.1), channel_id=1, source_target_pairs={{0,1},{1,2},{2,3},{3,0},{4,5},{5,6},{6,7},{7,4},{8,9},{9,10},{10,1... | collective-permute-start | bytes 786440 | tf_op jit(solution)/shard_map/ppermute | solution.py:497
  5.9 13.5 %collective-permute-start.3 = (bf16[32,4096]{1,0:T(8,128)(2,1)}, bf16[32,4096]{1,0:T(8,128)(2,1)S(1)}, u32[]{:S(2)}, u32[]{:S(2)}) collective-permute-start(bf16[32,4096]{1,0:T(8,128)(2,1)} %o0.1), channel_id=1, source_target_pairs={{0,3},{1,0},{2,1},{3,2},{4,7},{5,4},{6,5},{7,6},{8,11},{9,8},{10,9... | collective-permute-start | bytes 786440 | tf_op jit(solution)/shard_map/ppermute | solution.py:497
  17.7 11.4 %copy-start.1 = (bf16[2,128,1024]{2,1,0:T(8,128)(2,1)S(1)}, bf16[2,128,1024]{2,1,0:T(8,128)(2,1)}, u32[]{:S(2)}) copy-start(bf16[2,128,1024]{2,1,0:T(8,128)(2,1)} %k_ref.5) | copy-start | bytes 1572868
  17.8 11.4 %copy-start.3 = (f32[8,2,128]{2,1,0:T(2,128)S(1)}, f32[8,2,128]{2,1,0:T(2,128)}, u32[]{:S(2)}) copy-start(f32[8,2,128]{2,1,0:T(2,128)} %b_ref.5) | copy-start | bytes 24580
  17.8 4.8 %collective-permute-start = (bf16[4,128,256]{2,1,0:T(8,128)(2,1)S(1)}, bf16[4,128,256]{2,1,0:T(8,128)(2,1)S(1)}, u32[]{:S(2)}, u32[]{:S(2)}) collective-permute-start(bf16[4,128,256]{2,1,0:T(8,128)(2,1)S(1)} %get-tuple-element.39), channel_id=1, source_target_pairs={{0,4},{4,0},{8,12},{12,8},{16,20},{20,16},{24,28},{28,24},{32,36},... | collective-permute-start | bytes 786440 | tf_op jit(solution)/shard_map/ppermute | solution.py:473
  22.5 1.4 %collective-permute-start.4 = (bf16[4,128,128]{2,1,0:T(8,128)(2,1)S(1)}, bf16[4,128,128]{2,1,0:T(8,128)(2,1)S(1)}, u32[]{:S(2)}, u32[]{:S(2)}) collective-permute-start(bf16[4,128,128]{2,1,0:T(8,128)(2,1)S(1)} %get-tuple-element.44), channel_id=1, source_target_pairs={{0,4},{4,0},{8,12},{12,8},{16,20},{20,16},{24,28},{28,24},{32,36},... | collective-permute-start | bytes 393224 | tf_op jit(solution)/shard_map/ppermute | solution.py:473
  24.2 6.6 %collective-permute-start.5 = (bf16[128,384]{1,0:T(8,128)(2,1)S(1)}, bf16[128,384]{1,0:T(8,128)(2,1)S(1)}, u32[]{:S(2)}, u32[]{:S(2)}) collective-permute-start(bf16[128,384]{1,0:T(8,128)(2,1)S(1)} %get-tuple-element.60), channel_id=1, source_target_pairs={{0,8},{4,12},{8,16},{12,20},{16,24},{20,28},{24,0},{28,4},{32,40},... | collective-permute-start | bytes 294920 | tf_op jit(solution)/shard_map/ppermute | solution.py:473
  25.5 7.3 %collective-permute-start.6 = (bf16[128,384]{1,0:T(8,128)(2,1)S(1)}, bf16[128,384]{1,0:T(8,128)(2,1)S(1)}, u32[]{:S(2)}, u32[]{:S(2)}) collective-permute-start(bf16[128,384]{1,0:T(8,128)(2,1)S(1)} %get-tuple-element.61), channel_id=1, source_target_pairs={{0,16},{4,20},{8,24},{12,28},{16,0},{20,4},{24,8},{28,12},{32,48},... | collective-permute-start | bytes 294920 | tf_op jit(solution)/shard_map/ppermute | solution.py:473
  28.0 4.9 %collective-permute-start.7 = (bf16[128,384]{1,0:T(8,128)(2,1)S(1)}, bf16[128,384]{1,0:T(8,128)(2,1)S(1)}, u32[]{:S(2)}, u32[]{:S(2)}) collective-permute-start(bf16[128,384]{1,0:T(8,128)(2,1)S(1)} %get-tuple-element.62), channel_id=1, source_target_pairs={{0,24},{4,28},{8,0},{12,4},{16,8},{20,12},{24,16},{28,20},{32,56},... | collective-permute-start | bytes 294920 | tf_op jit(solution)/shard_map/ppermute | solution.py:473
  29.1 24.4 %copy-start.2 = (bf16[128,1024]{1,0:T(8,128)(2,1)S(1)}, bf16[128,1024]{1,0:T(8,128)(2,1)}, u32[]{:S(2)}) copy-start(bf16[128,1024]{1,0:T(8,128)(2,1)} %q_ref.3) | copy-start | bytes 786436
  33.3 5.1 %collective-permute-start.8 = (bf16[128,256]{1,0:T(8,128)(2,1)S(1)}, bf16[128,256]{1,0:T(8,128)(2,1)S(1)}, u32[]{:S(2)}, u32[]{:S(2)}) collective-permute-start(bf16[128,256]{1,0:T(8,128)(2,1)S(1)} %get-tuple-element.63), channel_id=1, source_target_pairs={{0,32},{4,36},{8,40},{12,44},{16,48},{20,52},{24,56},{28,60},{32,6... | collective-permute-start | bytes 196616 | tf_op jit(solution)/shard_map/ppermute | solution.py:473
  34.6 5.1 %collective-permute-start.9 = (bf16[128,256]{1,0:T(8,128)(2,1)S(1)}, bf16[128,256]{1,0:T(8,128)(2,1)S(1)}, u32[]{:S(2)}, u32[]{:S(2)}) collective-permute-start(bf16[128,256]{1,0:T(8,128)(2,1)S(1)} %get-tuple-element.64), channel_id=1, source_target_pairs={{0,64},{4,68},{8,72},{12,76},{16,80},{20,84},{24,88},{28,92},{32,9... | collective-permute-start | bytes 196616 | tf_op jit(solution)/shard_map/ppermute | solution.py:473
  37.2 3.7 %collective-permute-start.10 = (bf16[128,256]{1,0:T(8,128)(2,1)S(1)}, bf16[128,256]{1,0:T(8,128)(2,1)S(1)}, u32[]{:S(2)}, u32[]{:S(2)}) collective-permute-start(bf16[128,256]{1,0:T(8,128)(2,1)S(1)} %get-tuple-element.65), channel_id=1, source_target_pairs={{0,96},{4,100},{8,104},{12,108},{16,112},{20,116},{24,120},{28,124... | collective-permute-start | bytes 196616 | tf_op jit(solution)/shard_map/ppermute | solution.py:473
  41.8 4.5 %collective-permute-start.11 = (bf16[128,256]{1,0:T(8,128)(2,1)S(1)}, bf16[128,256]{1,0:T(8,128)(2,1)S(1)}, u32[]{:S(2)}, u32[]{:S(2)}) collective-permute-start(bf16[128,256]{1,0:T(8,128)(2,1)S(1)} %get-tuple-element.67), channel_id=1, source_target_pairs={{0,8},{4,12},{8,16},{12,20},{16,24},{20,28},{24,0},{28,4},{32,40},... | collective-permute-start | bytes 196616 | tf_op jit(solution)/shard_map/ppermute | solution.py:473
  42.7 4.7 %collective-permute-start.12 = (bf16[128,256]{1,0:T(8,128)(2,1)S(1)}, bf16[128,256]{1,0:T(8,128)(2,1)S(1)}, u32[]{:S(2)}, u32[]{:S(2)}) collective-permute-start(bf16[128,256]{1,0:T(8,128)(2,1)S(1)} %get-tuple-element.68), channel_id=1, source_target_pairs={{0,16},{4,20},{8,24},{12,28},{16,0},{20,4},{24,8},{28,12},{32,48},... | collective-permute-start | bytes 196616 | tf_op jit(solution)/shard_map/ppermute | solution.py:473
  45.1 3.4 %collective-permute-start.13 = (bf16[128,256]{1,0:T(8,128)(2,1)S(1)}, bf16[128,256]{1,0:T(8,128)(2,1)S(1)}, u32[]{:S(2)}, u32[]{:S(2)}) collective-permute-start(bf16[128,256]{1,0:T(8,128)(2,1)S(1)} %get-tuple-element.69), channel_id=1, source_target_pairs={{0,24},{4,28},{8,0},{12,4},{16,8},{20,12},{24,16},{28,20},{32,56},... | collective-permute-start | bytes 196616 | tf_op jit(solution)/shard_map/ppermute | solution.py:473
  48.8 4.8 %collective-permute-start.14 = (bf16[4,128,256]{2,1,0:T(8,128)(2,1)S(1)}, bf16[4,128,256]{2,1,0:T(8,128)(2,1)S(1)}, u32[]{:S(2)}, u32[]{:S(2)}) collective-permute-start(bf16[4,128,256]{2,1,0:T(8,128)(2,1)S(1)} %get-tuple-element.71), channel_id=1, source_target_pairs={{0,4},{4,0},{8,12},{12,8},{16,20},{20,16},{24,28},{28,24},{32,36},... | collective-permute-start | bytes 786440 | tf_op jit(solution)/shard_map/ppermute | solution.py:473
